TPU v7x, 32 devices: a whole 2x2x4 slice. The times are simulated.
32 devices in a mesh: grp: 1, fsdp: 32 (over z, y, x, core), rep: 1.
Axes of the slice: x: 2, y: 2, z: 4, core: 2. Of those that a mesh axis runs over, the one named last changes fastest.
Arguments:
- items: bfloat16 [1, 16384, 512], P('rep', ('grp', 'fsdp')), may hold values from -30 to 30, as said below
- w_in: bfloat16 [512, 2048], P('fsdp'), may hold values from -0.25 to 0.25
- w_out: bfloat16 [2048, 1024], P('fsdp'), may hold values from -0.125 to 0.125
- users: bfloat16 [1, 1024, 1024], P('rep', ('grp', 'fsdp')), may hold values from -0.19921875 to 0.19921875
- res_codes: int32 [1, 16384, 1024], P('rep', ('grp', 'fsdp')), may hold values from 0 to 15
- range_idx: int32 [1024], P('grp'), may hold values from 0 to 3
- range_lo: float32 [4], P('grp'), may hold values from -1 to 1
- range_step: float32 [4], P('grp'), may hold values from 0.05 to 0.2
Outputs:
- new_codes: bfloat16 [1, 16384, 1024], P('rep', ('grp', 'fsdp'))
- best: float32 [1, 1024], P('rep', ('grp', 'fsdp'))
Inputs may be any that keep to these rules, and one draw needn't show every extreme that they name: `items`: item features of order one.
All inputs are finite; a program needn't handle non-finite values.
Results may differ from a plain program's by a relative error of at most 0.0075.
Values may be sent and summed in bfloat16 or wider, within the bound.
No kernel may reach another device: no remote copies, remote signals or barrier semaphores. Data moves between devices by JAX's collectives and lax.ppermute only.
A program may use at most 64 MiB of HBM per device.

v0:
```python
import jax
import jax.numpy as jnp
from jax import lax
from jax.sharding import PartitionSpec as P


def row_adder(left, piece):
    return jnp.dot(left, piece, preferred_element_type=jnp.float32)


def on_device(items, w_in, w_out, users, res_codes, range_idx, range_lo, range_step):
    features = items[0]
    first = row_adder(features, lax.all_gather(w_in, "fsdp", axis=0, tiled=True))
    hidden = jax.nn.silu(first).astype(jnp.bfloat16)
    embed = row_adder(hidden, lax.all_gather(w_out, "fsdp", axis=0, tiled=True))
    local_upper = jnp.max(embed, axis=0)
    local_lower = jnp.min(embed, axis=0)
    upper = lax.pmax(local_upper, ("fsdp", "rep"))
    lower = lax.pmin(local_lower, ("fsdp", "rep"))
    mid = (upper + lower) * 0.5
    half = (upper - lower) * 0.5
    new_codes = (7.5 * (embed - mid) / (half + 1e-05)).astype(jnp.bfloat16)[None]
    levels = jnp.arange(range_lo.shape[0], dtype=jnp.int32)
    match = (range_idx[None, :] == levels[:, None]).astype(jnp.float32)
    step_d = jnp.sum(range_step[:, None] * match, axis=0)
    lo_d = jnp.sum(range_lo[:, None] * match, axis=0)
    resident = res_codes[0].astype(jnp.bfloat16)
    member = lax.all_gather(users, "fsdp", axis=1, tiled=True)[0]
    folded = (member.astype(jnp.float32) * step_d).astype(jnp.bfloat16)
    offset = jnp.dot(member.astype(jnp.float32), lo_d, precision=lax.Precision.HIGHEST)
    scores = lax.dot_general(
        resident, folded, (((1,), (1,)), ((), ())), preferred_element_type=jnp.float32
    )
    local_best = (jnp.max(scores, axis=0) + offset)[None]
    merged = lax.pmax(local_best, "fsdp")
    count = users.shape[1]
    best = lax.dynamic_slice_in_dim(merged, lax.axis_index("fsdp") * count, count, 1)
    return (new_codes, best)


def solution(mesh):
    return jax.shard_map(
        on_device,
        mesh=mesh,
        in_specs=(
            P("rep", ("grp", "fsdp"), None),
            P("fsdp", None),
            P("fsdp", None),
            P("rep", ("grp", "fsdp"), None),
            P("rep", ("grp", "fsdp"), None),
            P("grp"),
            P("grp"),
            P("grp"),
        ),
        out_specs=(P("rep", ("grp", "fsdp"), None), P("rep", ("grp", "fsdp"))),
        check_vma=False,
    )
```

profile of v0, /device:TPU:0, one launch (start us, length us, event | category | flops | bytes accessed | tf_op | source)
XLA Modules:
  0.0 286.0 jit_solution(5587563280381236445)
XLA Ops:
  7.2 0.0 copy-start
  7.2 0.0 all-gather.8.cloned.1.call-start
  7.2 0.7 all-gather.8.cloned.1.call-update
  7.9 0.0 all-gather.4.cloned.1.call-start
  8.0 0.7 all-gather.4.cloned.1.call-update
  8.7 0.0 all-gather.6.cloned.1.call-start
  8.7 0.7 all-gather.6.cloned.1.call-update
  9.4 0.8 select_reduce_fusion
  10.2 59.8 %all-gather.8.cloned.1.call-done = bf16[1,1024,1024]{2,1,0:T(8,128)(2,1)} async-done(((bf16[1,32,1024]{2,1,0:T(8,128)(2,1)}), bf16[1,1024,1024]{2,1,0:T(8,128)(2,1)}) %all-gather.8.cloned.1.call-update) | async-done | bytes 2097168 | tf_op jit(solution)/shard_map/all_gather | solution.py:28
  70.0 0.0 copy-start.1
  70.0 3.5 %fusion.3 = f32[1,1024]{1,0:T(1,128)S(1)} fusion(f32[1024,1]{0,1:T(1,128)S(1)} %bitcast.29, bf16[1,1024,1024]{2,1,0:T(8,128)(2,1)} %all-gather.8.cloned.1.call-done), kind=kOutput, calls=%fused_computation.4 | convolution fusion | flops 12582912 | bytes 2105344 | tf_op jit(solution)/shard_map/dot_general | solution.py:30
  73.4 0.0 copy-done.1
  73.4 2.9 %fusion.7 = f32[1024]{0:T(1024)S(1)} fusion(bf16[1,1024,1024]{2,1,0:T(8,128)(2,1)S(1)} %copy-done.1, f32[1024]{0:T(1024)S(1)} %get-tuple-element.5, s32[1,512,1024]{2,1,0:T(8,128)} %param.12), kind=kOutput, calls=%fused_computation.9 | convolution fusion | flops 1077935104 | bytes 4202496 | tf_op jit(solution)/shard_map/dot_general | solution.py:31
  76.4 51.7 %all-gather.4.cloned.1.call-done = bf16[512,2048]{1,0:T(8,128)(2,1)} async-done(((bf16[16,2048]{1,0:T(8,128)(2,1)}), bf16[512,2048]{1,0:T(8,128)(2,1)}) %all-gather.4.cloned.1.call-update) | async-done | bytes 2097168 | tf_op jit(solution)/shard_map/all_gather | solution.py:13
  128.1 63.8 %all-gather.6.cloned.1.call-done = bf16[2048,1024]{1,0:T(8,128)(2,1)} async-done(((bf16[64,1024]{1,0:T(8,128)(2,1)}), bf16[2048,1024]{1,0:T(8,128)(2,1)}) %all-gather.6.cloned.1.call-update) | async-done | bytes 4194320 | tf_op jit(solution)/shard_map/all_gather | solution.py:15
  191.9 0.0 copy-done
  191.9 6.4 %fusion.20 = (f32[1024]{0:T(1024)S(1)}, f32[1024]{0:T(1024)S(1)}, f32[512,1024]{1,0:T(8,128)S(1)}) fusion(bf16[2048,1024]{1,0:T(8,128)(2,1)} %all-gather.6.cloned.1.call-done, bf16[512,2048]{1,0:T(8,128)(2,1)} %all-gather.4.cloned.1.call-done, bf16[1,512,512]{2,1,0:T(8,128)(2,1)S(1)} %copy-done), kind=kOutput, calls=%fused_computation.22 | convolution fusion | flops 3227514880 | bytes 8921088 | tf_op jit(solution)/shard_map/dot_general | solution.py:8
  198.3 39.2 %pmin.7 = f32[1024]{0:T(1024)S(1)} all-reduce(f32[1024]{0:T(1024)S(1)} %get-tuple-element.2), channel_id=1, replica_groups=mesh['grp'=1,'fsdp'=32,'rep'=1] {'fsdp','rep'}, use_global_device_ids=true, to_apply=%region_3.4 | all-reduce | flops 1024 | bytes 8192 | tf_op jit(solution)/shard_map/pmin | solution.py:19
  237.5 40.1 %all-reduce = (f32[1024]{0:T(1024)S(1)}, f32[1,1024]{1,0:T(1,128)S(1)}) all-reduce(f32[1024]{0:T(1024)S(1)} %get-tuple-element.3, f32[1,1024]{1,0:T(1,128)S(1)} %bitcast.30), channel_id=1, replica_groups=mesh['grp'=1,'fsdp'=32,'rep'=1] {'fsdp','rep'}, use_global_device_ids=true, to_apply=%region_1.2 | all-reduce | flops 2048 | bytes 16384 | tf_op jit(solution)/shard_map/pmax | solution.py:18
  277.6 0.6 constant_dynamic-slice_fusion
  278.2 1.3 fusion.12
  (2 shorter events, 0.0 us)
Async XLA Ops:
  7.2 184.7 %copy-start = (bf16[1,512,512]{2,1,0:T(8,128)(2,1)S(1)}, bf16[1,512,512]{2,1,0:T(8,128)(2,1)}, u32[]{:S(2)}) copy-start(bf16[1,512,512]{2,1,0:T(8,128)(2,1)} %param.8) | copy-start | bytes 1572868
  7.2 62.8 %all-gather.8.cloned.1.call-start = ((), (), s32[]{:S(2)}) async-start(), calls=%async_computation.2 | async-start | bytes 2162688 | tf_op jit(solution)/shard_map/all_gather | solution.py:28
  7.9 120.2 %all-gather.4.cloned.1.call-start = ((), (), s32[]{:S(2)}) async-start(), calls=%async_computation | async-start | bytes 2162688 | tf_op jit(solution)/shard_map/all_gather | solution.py:13
  8.7 183.2 %all-gather.6.cloned.1.call-start = ((), (), s32[]{:S(2)}) async-start(), calls=%async_computation.1 | async-start | bytes 4325376 | tf_op jit(solution)/shard_map/all_gather | solution.py:15
  70.0 3.5 %copy-start.1 = (bf16[1,1024,1024]{2,1,0:T(8,128)(2,1)S(1)}, bf16[1,1024,1024]{2,1,0:T(8,128)(2,1)}, u32[]{:S(2)}) copy-start(bf16[1,1024,1024]{2,1,0:T(8,128)(2,1)} %all-gather.8.cloned.1.call-done) | copy-start | bytes 6291460
Sparse Core Ops, SparseCore 0:
  10.9 59.0 all-gather.7
  72.8 55.2 all-gather.3
  131.0 60.8 all-gather.5
where the time goes:
time: 286 us
  waiting for transfers between devices  177 us (62%)
  blocking collectives  79.3 us (28%)
  between operations  13.8 us (5%)
  matrix products  12.8 us (4%)
    all_gather x1, waiting for transfers between devices, on_device(): embed = row_adder(hidden, lax.all_gather(w_out, 'fsdp', axis=0, tiled=True))  63.8 us
    all_gather x1, waiting for transfers between devices, on_device(): member = lax.all_gather(users, 'fsdp', axis=1, tiled=True)[0]  59.8 us
    all_gather x1, waiting for transfers between devices, on_device(): lax.all_gather(w_in, 'fsdp', axis=0, tiled=True)  51.7 us
    pmax x1, blocking collectives, on_device(): upper = lax.pmax(local_upper, ('fsdp', 'rep'))  40.1 us
    pmin x1, blocking collectives, on_device(): lower = lax.pmin(local_lower, ('fsdp', 'rep'))  39.2 us
    dot_general x1, matrix products, row_adder(): return jnp.dot(left, piece, preferred_element_type=jnp.float32)  6.45 us
  transfers between devices with their start and end apart: 3, of which 3 were waited for; matrix products, arithmetic and copies ran while one was open for 3% of the time, Pallas kernels for 0%

commit v1 on v0

v1 whole, which is shorter than its diff:
```python
import functools

import jax
import jax.numpy as jnp
from jax import lax
from jax.experimental import pallas as pl
from jax.experimental.pallas import tpu as pltpu
from jax.sharding import PartitionSpec as P

ANY = pl.BlockSpec(memory_space=pl.ANY)
VMEM = pl.BlockSpec(memory_space=pltpu.VMEM)
SMEM = pl.BlockSpec(memory_space=pltpu.SMEM)
BF16 = jnp.bfloat16
F32 = jnp.float32
MIB = 1 << 20


def swap(x, axis, n, k):
    return lax.ppermute(x, axis, [(i, i ^ k) for i in range(n)])


def chip_and_core():
    me = lax.axis_index("fsdp")
    return me // 2, me % 2


def place(pieces, keys, rows, target, sems):
    chip, _ = chip_and_core()
    copies = []
    for piece, chips in zip(pieces, keys):
        for slot, key in enumerate(chips):
            copies.append(
                pltpu.make_async_copy(
                    piece.at[pl.ds(slot * rows, rows), :],
                    target.at[pl.ds(pl.multiple_of((chip ^ key) * rows, rows), rows), :],
                    sems.at[len(copies)],
                )
            )
    for copy in copies:
        copy.start()
    return copies


def score_kernel(
    keys, idx, lo, step, own, other, u0, u1, u2, u3, best, members, sems
):
    pieces = (u0, u1, u2, u3)
    rows = u0.shape[0] // 4
    copies = place(pieces, keys, rows, members, sems)
    index = idx[...]
    step_d = jnp.zeros(index.shape, F32)
    lo_d = jnp.zeros(index.shape, F32)
    for level in range(lo.shape[0]):
        step_d = jnp.where(index == level, step[level], step_d)
        lo_d = jnp.where(index == level, lo[level], lo_d)
    high = lo_d.astype(BF16)
    rest = lo_d - high.astype(F32)
    middle = rest.astype(BF16)
    low = (rest - middle.astype(F32)).astype(BF16)
    row = lax.broadcasted_iota(jnp.int32, (16, index.shape[1]), 0)
    parts = jnp.where(
        row == 0,
        high.astype(F32),
        jnp.where(row == 1, middle.astype(F32), jnp.where(row == 2, low.astype(F32), 0.0)),
    ).astype(BF16)
    for copy in copies:
        copy.wait()
    contract = (((1,), (1,)), ((), ()))
    block = 256
    for at in range(0, members.shape[0], block):
        member = members[at : at + block, :]
        folded = (member.astype(F32) * step_d).astype(BF16)
        offset = jnp.sum(
            lax.dot_general(parts, member, contract, preferred_element_type=F32),
            axis=0,
            keepdims=True,
        )
        top = jnp.max(
            lax.dot_general(own[...], folded, contract, preferred_element_type=F32),
            axis=0,
            keepdims=True,
        )
        top = jnp.maximum(
            top,
            jnp.max(
                lax.dot_general(other[...], folded, contract, preferred_element_type=F32),
                axis=0,
                keepdims=True,
            ),
        )
        best[:, at : at + block] = top + offset


def hidden_kernel(keys, own, other, w0, w1, w2, w3, hidden, weights, sems):
    chip, core = chip_and_core()
    rows = w0.shape[0] // 8
    copies = []
    for piece, chips in zip((w0, w1, w2, w3), keys):
        for slot, key in enumerate(chips):
            for half in range(2):
                device = (chip ^ key) * 2 + (core + half) % 2
                copies.append(
                    pltpu.make_async_copy(
                        piece.at[pl.ds((2 * slot + half) * rows, rows), :],
                        weights.at[pl.ds(pl.multiple_of(device * rows, rows), rows), :],
                        sems.at[len(copies)],
                    )
                )
    for copy in copies:
        copy.start()
    for copy in copies:
        copy.wait()
    count = own.shape[0]
    block = 256
    for at in range(0, 2 * count, block):
        features = own[at : at + block, :] if at < count else other[at - count : at - count + block, :]
        v = jnp.dot(features, weights[...], preferred_element_type=F32)
        v = 0.5 * v
        hidden[at : at + block, :] = (v * (1.0 + jnp.tanh(v))).astype(BF16)


def embed_kernel(keys, mine, theirs, w0, w1, w2, w3, own, other, bounds, weights, sems):
    chip, core = chip_and_core()
    rows = w0.shape[0] // 8
    copies = []
    for piece, chips in zip((w0, w1, w2, w3), keys):
        for slot, key in enumerate(chips):
            for half in range(2):
                device = (chip ^ key) * 2 + (core + half) % 2
                copies.append(
                    pltpu.make_async_copy(
                        piece.at[pl.ds((2 * slot + half) * rows, rows), :],
                        weights.at[pl.ds(pl.multiple_of(device * rows, rows), rows), :],
                        sems.at[len(copies)],
                    )
                )
    for copy in copies:
        copy.start()
    for copy in copies:
        copy.wait()
    count = own.shape[0]
    depth = mine.shape[1]
    here = pl.ds(pl.multiple_of(core * depth, depth), depth)
    there = pl.ds(pl.multiple_of((1 - core) * depth, depth), depth)
    block = 256
    upper = lower = None
    for at in range(0, 2 * count, block):
        flip = at + count if at < count else at - count
        e = jnp.dot(
            mine[at : at + block, :], weights[here, :], preferred_element_type=F32
        ) + jnp.dot(
            theirs[flip : flip + block, :], weights[there, :], preferred_element_type=F32
        )
        if at < count:
            own[at : at + block, :] = e
        else:
            other[at - count : at - count + block, :] = e
        top = jnp.max(e, axis=0, keepdims=True)
        bottom = jnp.min(e, axis=0, keepdims=True)
        upper = top if upper is None else jnp.maximum(upper, top)
        lower = bottom if lower is None else jnp.minimum(lower, bottom)
    bounds[0:1, :] = upper
    bounds[1:2, :] = -lower


def code_kernel(own, other, here, there, codes):
    _, core = chip_and_core()
    width = own.shape[1]
    for values, bounds, part in ((own, here, core), (other, there, 1 - core)):
        upper = bounds[0:1, :]
        lower = -bounds[1:2, :]
        mid = (upper + lower) * 0.5
        scale = 7.5 / ((upper - lower) * 0.5 + 1e-05)
        at = pl.ds(pl.multiple_of(part * width, width), width)
        codes[:, at] = ((values[...] - mid) * scale).astype(BF16)


def call(kernel, out, specs, scratch=(), limit=24):
    return pl.pallas_call(
        kernel,
        out_shape=out,
        in_specs=specs,
        out_specs=jax.tree.map(lambda _: VMEM, out),
        scratch_shapes=scratch,
        compiler_params=pltpu.CompilerParams(vmem_limit_bytes=limit * MIB),
    )


def shape(dims, dtype):
    return jax.ShapeDtypeStruct(dims, dtype)


def half_columns(x, core):
    width = x.shape[1] // 2
    return lax.dynamic_slice_in_dim(x, core * width, width, 1)


def by_permutes(n, n_rep, items, w_in, w_out, users, res_codes, range_idx, range_lo, range_step):
    move = lambda x, k: swap(x, "fsdp", n, k)
    _, core = chip_and_core()
    z_first = tuple(tuple(b + 4 * j for j in range(4)) for b in range(4))
    xy_first = tuple(tuple(4 * b + j for j in range(4)) for b in range(4))

    user_plane = jnp.concatenate(
        [users[0]] + [move(users[0], k) for k in (2, 4, 6)], axis=0
    )

    in_rows = jnp.concatenate(
        [half_columns(w_in, core), move(half_columns(w_in, 1 - core), 1)], axis=0
    )
    out_rows = jnp.concatenate(
        [half_columns(w_out, core), move(half_columns(w_out, 1 - core), 1)], axis=0
    )
    in_column = jnp.concatenate([in_rows] + [move(in_rows, k) for k in (8, 16, 24)], axis=0)
    in_pieces = [in_column] + [move(in_column, k) for k in (2, 4, 6)]
    out_column = jnp.concatenate([out_rows] + [move(out_rows, k) for k in (8, 16, 24)], axis=0)
    out_pieces = [out_column] + [move(out_column, k) for k in (2, 4, 6)]
    user_pieces = [user_plane] + [move(user_plane, k) for k in (8, 16, 24)]

    features = items[0]
    count, d_in = features.shape
    features_other = move(features, 1)
    codes = res_codes[0].astype(BF16)
    codes_other = move(codes, 1)

    members = n // 2 * users.shape[1]
    depth = users.shape[2]
    best = call(
        functools.partial(score_kernel, xy_first),
        shape((1, members), F32),
        [VMEM, SMEM, SMEM, VMEM, VMEM] + [ANY] * 4,
        [pltpu.VMEM((members, depth), BF16), pltpu.SemaphoreType.DMA((16,))],
    )(range_idx[None, :], range_lo, range_step, codes, codes_other, *user_pieces)

    wide = w_in.shape[1] // 2
    hidden = call(
        functools.partial(hidden_kernel, z_first),
        shape((2 * count, wide), BF16),
        [VMEM, VMEM] + [ANY] * 4,
        [pltpu.VMEM((d_in, wide), BF16), pltpu.SemaphoreType.DMA((32,))],
    )(features, features_other, *in_pieces)
    hidden_other = move(hidden, 1)

    width = w_out.shape[1] // 2
    own, other, bounds = call(
        functools.partial(embed_kernel, z_first),
        (
            shape((count, width), F32),
            shape((count, width), F32),
            shape((2, width), F32),
        ),
        [VMEM, VMEM] + [ANY] * 4,
        [pltpu.VMEM((2 * wide, width), BF16), pltpu.SemaphoreType.DMA((32,))],
    )(hidden, hidden_other, *out_pieces)
    received = move(other, 1)

    merged = jnp.concatenate([bounds, best], axis=0)
    for k in (2, 4, 8, 16):
        merged = jnp.maximum(merged, move(merged, k))
    bounds = merged[:2]
    if n_rep > 1:
        bounds = lax.pmax(bounds, "rep")
    new_codes = call(
        code_kernel,
        shape((count, 2 * width), BF16),
        [VMEM] * 4,
    )(own, received, bounds, move(bounds, 1))
    chip, _ = chip_and_core()
    each = users.shape[1]
    mine = lax.dynamic_slice_in_dim(merged[2:], chip * each, each, 1)
    return new_codes[None], mine


def on_any(items, w_in, w_out, users, res_codes, range_idx, range_lo, range_step):
    features = items[0]
    dot = functools.partial(jnp.dot, preferred_element_type=F32)
    first = dot(features, lax.all_gather(w_in, "fsdp", axis=0, tiled=True))
    hidden = jax.nn.silu(first).astype(BF16)
    embed = dot(hidden, lax.all_gather(w_out, "fsdp", axis=0, tiled=True))
    upper = lax.pmax(jnp.max(embed, axis=0), ("fsdp", "rep"))
    lower = lax.pmin(jnp.min(embed, axis=0), ("fsdp", "rep"))
    mid = (upper + lower) * 0.5
    half = (upper - lower) * 0.5
    new_codes = (7.5 * (embed - mid) / (half + 1e-05)).astype(BF16)[None]
    levels = jnp.arange(range_lo.shape[0], dtype=jnp.int32)
    match = (range_idx[None, :] == levels[:, None]).astype(F32)
    step_d = jnp.sum(range_step[:, None] * match, axis=0)
    lo_d = jnp.sum(range_lo[:, None] * match, axis=0)
    member = lax.all_gather(users, "fsdp", axis=1, tiled=True)[0]
    folded = (member.astype(F32) * step_d).astype(BF16)
    offset = jnp.dot(member.astype(F32), lo_d, precision=lax.Precision.HIGHEST)
    scores = dot(res_codes[0].astype(BF16), folded.T)
    merged = lax.pmax((jnp.max(scores, axis=0) + offset)[None], "fsdp")
    count = users.shape[1]
    best = lax.dynamic_slice_in_dim(merged, lax.axis_index("fsdp") * count, count, 1)
    return new_codes, best


def solution(mesh):
    n = mesh.shape["fsdp"]
    body = on_any
    if n == 32:
        body = functools.partial(by_permutes, n, mesh.shape["rep"])
    return jax.shard_map(
        body,
        mesh=mesh,
        in_specs=(
            P("rep", ("grp", "fsdp"), None),
            P("fsdp", None),
            P("fsdp", None),
            P("rep", ("grp", "fsdp"), None),
            P("rep", ("grp", "fsdp"), None),
            P("grp"),
            P("grp"),
            P("grp"),
        ),
        out_specs=(P("rep", ("grp", "fsdp"), None), P("rep", ("grp", "fsdp"))),
        check_vma=False,
    )
```

time: 286 us -> 140 us (0.49)
  waiting for transfers between devices: 177 us -> 81.9 us
  blocking collectives: 79.3 us -> 0 us
  starting transfers between devices: 0.11 us -> 35.6 us
  Pallas kernels: 0 us -> 16.6 us
  between operations: 13.8 us -> 0.9 us
  matrix products: 12.8 us -> 0 us
    all_gather x3 -> x0, waiting for transfers between devices: 175 us -> none  [the longest x1 63.8 us: on_device(): embed = row_adder(hidden, lax.all_gather(w_out, 'fsdp', axis=0, tiled=True))]
    ppermute x0 -> x29, waiting for transfers between devices: none -> 81.9 us  [swap(): return lax.ppermute(x, axis, [(i, i ^ k) for i in range(n)])]
    pmax x1 -> x0, blocking collectives: 40.1 us -> none  [on_device(): upper = lax.pmax(local_upper, ('fsdp', 'rep'))]
    pmin x1 -> x0, blocking collectives: 39.2 us -> none  [on_device(): lower = lax.pmin(local_lower, ('fsdp', 'rep'))]
    ppermute x0 -> x29, starting transfers between devices: none -> 35.6 us  [swap(): return lax.ppermute(x, axis, [(i, i ^ k) for i in range(n)])]
    pallas_call x0 -> x4, Pallas kernels: none -> 16.6 us  [the longest x1 8.39 us: by_permutes(): call(functools.partial(embed_kernel, z_first), (shape((count, width), F32...]
    dot_general x3 -> x0, matrix products: 12.8 us -> none  [the longest x1 6.45 us: row_adder(): return jnp.dot(left, piece, preferred_element_type=jnp.float32)]
  transfers between devices with their start and end apart: 3 -> 29, of which waited for: 3 -> 21; matrix products, arithmetic and copies ran while one was open for 3% -> 2% of each run, Pallas kernels for 0% -> 9%
where the time goes in v1:
time: 140 us; the launch traced here: 139 us
  waiting for transfers between devices  81.9 us (59%)
  starting transfers between devices  35.6 us (25%)
  Pallas kernels  16.6 us (12%)
  local copies, waits for them, and re-layouts  2.53 us (2%)
  other arithmetic  1.89 us (1%)
    ppermute x29, waiting for transfers between devices, swap(): return lax.ppermute(x, axis, [(i, i ^ k) for i in range(n)])  81.9 us
    ppermute x29, starting transfers between devices, swap(): return lax.ppermute(x, axis, [(i, i ^ k) for i in range(n)])  35.6 us
    pallas_call x1, Pallas kernels, by_permutes(): call(functools.partial(embed_kernel, z_first), (shape((count, width), F32...  8.39 us
    pallas_call x1, Pallas kernels, by_permutes(): call(functools.partial(score_kernel, xy_first), shape((1, members), F32),...  3.8 us
    pallas_call x1, Pallas kernels, by_permutes(): call(functools.partial(hidden_kernel, z_first), shape((2 * count, wide),...  3.24 us
  transfers between devices with their start and end apart: 29, of which 21 were waited for; matrix products, arithmetic and copies ran while one was open for 2% of the time, Pallas kernels for 9%

profile of v1, /device:TPU:0, one launch (start us, length us, event | category | flops | bytes accessed | tf_op | source)
XLA Modules:
  0.0 139.4 jit_solution(7558716471058770530)
XLA Ops:
  2.8 2.9 %collective-permute-start.2 = (bf16[32,1024]{1,0:T(8,128)(2,1)S(1)}, bf16[32,1024]{1,0:T(8,128)(2,1)S(1)}, u32[]{:S(2)}, u32[]{:S(2)}) collective-permute-start(bf16[32,1024]{1,0:T(8,128)(2,1)S(1)} %pad_maximum_fusion.2), channel_id=1, source_target_pairs={{0,8},{1,9},{2,10},{3,11},{4,12},{5,13},{6,14},{7,15},{8,0},{9,1},... | collective-permute-start | bytes 196616 | tf_op jit(solution)/shard_map/ppermute | solution.py:19
  5.7 2.6 %collective-permute-start.3 = (bf16[32,1024]{1,0:T(8,128)(2,1)S(1)}, bf16[32,1024]{1,0:T(8,128)(2,1)S(1)}, u32[]{:S(2)}, u32[]{:S(2)}) collective-permute-start(bf16[32,1024]{1,0:T(8,128)(2,1)S(1)} %pad_maximum_fusion.2), channel_id=1, source_target_pairs={{0,16},{1,17},{2,18},{3,19},{4,20},{5,21},{6,22},{7,23},{8,24},{9,... | collective-permute-start | bytes 196616 | tf_op jit(solution)/shard_map/ppermute | solution.py:19
  8.3 4.9 %collective-permute-done.3 = bf16[32,1024]{1,0:T(8,128)(2,1)S(1)} collective-permute-done((bf16[32,1024]{1,0:T(8,128)(2,1)S(1)}, bf16[32,1024]{1,0:T(8,128)(2,1)S(1)}, u32[]{:S(2)}, u32[]{:S(2)}) %collective-permute-start.3) | collective-permute-done | bytes 65568 | tf_op jit(solution)/shard_map/ppermute | solution.py:19
  18.1 5.8 %collective-permute-done.5.w1 = bf16[128,1024]{1,0:T(8,128)(2,1)S(1)} collective-permute-done((bf16[128,1024]{1,0:T(8,128)(2,1)S(1)}, bf16[128,1024]{1,0:T(8,128)(2,1)S(1)}, u32[]{:S(2)}, u32[]{:S(2)}) %collective-permute-start.5) | collective-permute-done | bytes 262176 | tf_op jit(solution)/shard_map/ppermute | solution.py:19
  23.8 4.2 %collective-permute-done.6.w2 = bf16[128,1024]{1,0:T(8,128)(2,1)S(1)} collective-permute-done((bf16[128,1024]{1,0:T(8,128)(2,1)S(1)}, bf16[128,1024]{1,0:T(8,128)(2,1)S(1)}, u32[]{:S(2)}, u32[]{:S(2)}) %collective-permute-start.6) | collective-permute-done | bytes 262176 | tf_op jit(solution)/shard_map/ppermute | solution.py:19
  29.1 3.2 %shard_map.95.mine = bf16[1024,1024]{1,0:T(8,128)(2,1)S(1)} custom-call(bf16[512,512]{1,0:T(8,128)(2,1)S(1)} %bitcast.7, bf16[512,512]{1,0:T(8,128)(2,1)S(1)} %collective-permute-done.other, bf16[128,1024]{1,0:T(8,128)(2,1)S(1)} %constant_dynamic-update-slice_fusion.w0, bf16[128,1024]{1,0:T(8,128)(2,1)S(1)} %collective-permute-done.5.w1, ...), custom_call_target="tpu_custom_call" | custom-call | tf_op jit(solution)/shard_map/pallas_call | solution.py:236
  33.0 3.3 %collective-permute-done.9 = bf16[64,512]{1,0:T(8,128)(2,1)S(1)} collective-permute-done((bf16[64,512]{1,0:T(8,128)(2,1)S(1)}, bf16[64,512]{1,0:T(8,128)(2,1)S(1)}, u32[]{:S(2)}, u32[]{:S(2)}) %collective-permute-start.9) | collective-permute-done | bytes 65568 | tf_op jit(solution)/shard_map/ppermute | solution.py:19
  38.6 2.2 %collective-permute-start.12 = (bf16[128,512]{1,0:T(8,128)(2,1)S(1)}, bf16[128,512]{1,0:T(8,128)(2,1)S(1)}, u32[]{:S(2)}, u32[]{:S(2)}) collective-permute-start(bf16[128,512]{1,0:T(8,128)(2,1)S(1)} %pad_maximum_fusion.1), channel_id=1, source_target_pairs={{0,24},{1,25},{2,26},{3,27},{4,28},{5,29},{6,30},{7,31},{8,16},{9,... | collective-permute-start | bytes 393224 | tf_op jit(solution)/shard_map/ppermute | solution.py:19
  40.8 3.6 %collective-permute-done.10 = bf16[128,512]{1,0:T(8,128)(2,1)S(1)} collective-permute-done((bf16[128,512]{1,0:T(8,128)(2,1)S(1)}, bf16[128,512]{1,0:T(8,128)(2,1)S(1)}, u32[]{:S(2)}, u32[]{:S(2)}) %collective-permute-start.10) | collective-permute-done | bytes 131104 | tf_op jit(solution)/shard_map/ppermute | solution.py:19
  44.4 6.1 %collective-permute-done.11 = bf16[128,512]{1,0:T(8,128)(2,1)S(1)} collective-permute-done((bf16[128,512]{1,0:T(8,128)(2,1)S(1)}, bf16[128,512]{1,0:T(8,128)(2,1)S(1)}, u32[]{:S(2)}, u32[]{:S(2)}) %collective-permute-start.11) | collective-permute-done | bytes 131104 | tf_op jit(solution)/shard_map/ppermute | solution.py:19
  54.2 1.8 %convert_bitcast_fusion.own = bf16[512,1024]{1,0:T(8,128)(2,1)S(1)} fusion(s32[1,512,1024]{2,1,0:T(8,128)} %param.12), kind=kLoop, calls=%fused_computation | loop fusion | flops 524288 | bytes 3145728 | tf_op jit(solution)/shard_map/convert_element_type | solution.py:223
  56.1 9.4 %collective-permute-done.13.w1 = bf16[512,512]{1,0:T(8,128)(2,1)S(1)} collective-permute-done((bf16[512,512]{1,0:T(8,128)(2,1)S(1)}, bf16[512,512]{1,0:T(8,128)(2,1)S(1)}, u32[]{:S(2)}, u32[]{:S(2)}) %collective-permute-start.13) | collective-permute-done | bytes 524320 | tf_op jit(solution)/shard_map/ppermute | solution.py:19
  65.5 7.9 %collective-permute-done.14.w2 = bf16[512,512]{1,0:T(8,128)(2,1)S(1)} collective-permute-done((bf16[512,512]{1,0:T(8,128)(2,1)S(1)}, bf16[512,512]{1,0:T(8,128)(2,1)S(1)}, u32[]{:S(2)}, u32[]{:S(2)}) %collective-permute-start.14) | collective-permute-done | bytes 524320 | tf_op jit(solution)/shard_map/ppermute | solution.py:19
  75.0 8.4 %shard_map.96 = (f32[512,512]{1,0:T(8,128)S(1)}, f32[512,512]{1,0:T(8,128)}, f32[2,512]{1,0:T(2,128)S(1)}) custom-call(bf16[1024,1024]{1,0:T(8,128)(2,1)S(1)} %shard_map.95.mine, bf16[1024,1024]{1,0:T(8,128)(2,1)} %collective-permute-done.8.theirs, bf16[512,512]{1,0:T(8,128)(2,1)S(1)} %constant_dynamic-update-slice_fusion.5.w0, ...), custom_call_target="tpu_custom_call" | custom-call | tf_op jit(solution)/shard_map/pallas_call | solution.py:245
  88.6 2.4 %collective-permute-done.20 = bf16[32,1024]{1,0:T(8,128)(2,1)S(1)} collective-permute-done((bf16[32,1024]{1,0:T(8,128)(2,1)S(1)}, bf16[32,1024]{1,0:T(8,128)(2,1)S(1)}, u32[]{:S(2)}, u32[]{:S(2)}) %collective-permute-start.20) | collective-permute-done | bytes 65568 | tf_op jit(solution)/shard_map/ppermute | solution.py:19
  91.1 3.4 %collective-permute-start.21 = (bf16[128,1024]{1,0:T(8,128)(2,1)S(1)}, bf16[128,1024]{1,0:T(8,128)(2,1)S(1)}, u32[]{:S(2)}, u32[]{:S(2)}) collective-permute-start(bf16[128,1024]{1,0:T(8,128)(2,1)S(1)} %pad_maximum_fusion.u0), channel_id=1, source_target_pairs={{0,8},{1,9},{2,10},{3,11},{4,12},{5,13},{6,14},{7,15},{8,0},{9,1},... | collective-permute-start | bytes 786440 | tf_op jit(solution)/shard_map/ppermute | solution.py:19
  97.0 6.9 %collective-permute-done.21.u1 = bf16[128,1024]{1,0:T(8,128)(2,1)S(1)} collective-permute-done((bf16[128,1024]{1,0:T(8,128)(2,1)S(1)}, bf16[128,1024]{1,0:T(8,128)(2,1)S(1)}, u32[]{:S(2)}, u32[]{:S(2)}) %collective-permute-start.21) | collective-permute-done | bytes 262176 | tf_op jit(solution)/shard_map/ppermute | solution.py:19
  103.8 12.1 %collective-permute-done.22.u2 = bf16[128,1024]{1,0:T(8,128)(2,1)S(1)} collective-permute-done((bf16[128,1024]{1,0:T(8,128)(2,1)S(1)}, bf16[128,1024]{1,0:T(8,128)(2,1)S(1)}, u32[]{:S(2)}, u32[]{:S(2)}) %collective-permute-start.22) | collective-permute-done | bytes 262176 | tf_op jit(solution)/shard_map/ppermute | solution.py:19
  115.9 3.8 %shard_map.97 = f32[1,512]{1,0:T(1,128)S(1)} custom-call(s32[1,1024]{1,0:T(1,128)S(1)} %bitcast.8, f32[4]{0:T(128)S(1)} %copy-done.2, f32[4]{0:T(128)S(1)} %copy-done.3, bf16[512,1024]{1,0:T(8,128)(2,1)S(1)} %convert_bitcast_fusion.own, bf16[512,1024]{1,0:T(8,128)(2,1)S(1)} %collective-permute-done.17.other, bf16[128,1024]{1,0:T(8,128)(2,1)S(1)} %pad_maximum_fusion.u0, ...), custom_call_target="tpu_custom_call" | custom-call | tf_op jit(solution)/shard_map/pallas_call | solution.py:228
  120.3 3.1 %collective-permute-done.24 = f32[3,512]{1,0:T(4,128)S(1)} collective-permute-done((f32[3,512]{1,0:T(4,128)S(1)}, f32[3,512]{1,0:T(4,128)S(1)}, u32[]{:S(2)}, u32[]{:S(2)}) %collective-permute-start.24) | collective-permute-done | bytes 6176 | tf_op jit(solution)/shard_map/ppermute | solution.py:19
  124.1 3.1 %collective-permute-done.25 = f32[3,512]{1,0:T(4,128)S(1)} collective-permute-done((f32[3,512]{1,0:T(4,128)S(1)}, f32[3,512]{1,0:T(4,128)S(1)}, u32[]{:S(2)}, u32[]{:S(2)}) %collective-permute-start.25) | collective-permute-done | bytes 6176 | tf_op jit(solution)/shard_map/ppermute | solution.py:19
  127.2 3.6 %collective-permute-start.26 = (f32[3,512]{1,0:T(4,128)S(1)}, f32[3,512]{1,0:T(4,128)S(1)}, u32[]{:S(2)}, u32[]{:S(2)}) collective-permute-start(f32[3,512]{1,0:T(4,128)S(1)} %max.13), channel_id=1, source_target_pairs={{0,8},{1,9},{2,10},{3,11},{4,12},{5,13},{6,14},{7,15},{8,0},{9,1},... | collective-permute-start | bytes 18440 | tf_op jit(solution)/shard_map/ppermute | solution.py:19
  132.5 2.9 %collective-permute-start.27 = (f32[3,512]{1,0:T(4,128)S(1)}, f32[3,512]{1,0:T(4,128)S(1)}, u32[]{:S(2)}, u32[]{:S(2)}) collective-permute-start(f32[3,512]{1,0:T(4,128)S(1)} %max.14), channel_id=1, source_target_pairs={{0,16},{1,17},{2,18},{3,19},{4,20},{5,21},{6,22},{7,23},{8,24},{9,... | collective-permute-start | bytes 18440 | tf_op jit(solution)/shard_map/ppermute | solution.py:19
  135.3 1.7 %collective-permute-done.27 = f32[3,512]{1,0:T(4,128)S(1)} collective-permute-done((f32[3,512]{1,0:T(4,128)S(1)}, f32[3,512]{1,0:T(4,128)S(1)}, u32[]{:S(2)}, u32[]{:S(2)}) %collective-permute-start.27) | collective-permute-done | bytes 6176 | tf_op jit(solution)/shard_map/ppermute | solution.py:19
  (72 shorter events, 29.1 us)
Async XLA Ops:
  1.9 26.1 %collective-permute-start = (bf16[512,512]{1,0:T(8,128)(2,1)}, bf16[512,512]{1,0:T(8,128)(2,1)S(1)}, u32[]{:S(2)}, u32[]{:S(2)}) collective-permute-start(bf16[512,512]{1,0:T(8,128)(2,1)} %bitcast.6), channel_id=1, source_target_pairs={{0,1},{1,0},{2,3},{3,2},{4,5},{5,4},{6,7},{7,6},{8,9},{9,8},{10,11... | collective-permute-start | bytes 1572872 | tf_op jit(solution)/shard_map/ppermute | solution.py:19
  2.8 5.5 %collective-permute-start.2 = (bf16[32,1024]{1,0:T(8,128)(2,1)S(1)}, bf16[32,1024]{1,0:T(8,128)(2,1)S(1)}, u32[]{:S(2)}, u32[]{:S(2)}) collective-permute-start(bf16[32,1024]{1,0:T(8,128)(2,1)S(1)} %pad_maximum_fusion.2), channel_id=1, source_target_pairs={{0,8},{1,9},{2,10},{3,11},{4,12},{5,13},{6,14},{7,15},{8,0},{9,1},... | collective-permute-start | bytes 196616 | tf_op jit(solution)/shard_map/ppermute | solution.py:19
  5.7 7.5 %collective-permute-start.3 = (bf16[32,1024]{1,0:T(8,128)(2,1)S(1)}, bf16[32,1024]{1,0:T(8,128)(2,1)S(1)}, u32[]{:S(2)}, u32[]{:S(2)}) collective-permute-start(bf16[32,1024]{1,0:T(8,128)(2,1)S(1)} %pad_maximum_fusion.2), channel_id=1, source_target_pairs={{0,16},{1,17},{2,18},{3,19},{4,20},{5,21},{6,22},{7,23},{8,24},{9,... | collective-permute-start | bytes 196616 | tf_op jit(solution)/shard_map/ppermute | solution.py:19
  8.3 6.2 %collective-permute-start.4 = (bf16[32,1024]{1,0:T(8,128)(2,1)S(1)}, bf16[32,1024]{1,0:T(8,128)(2,1)S(1)}, u32[]{:S(2)}, u32[]{:S(2)}) collective-permute-start(bf16[32,1024]{1,0:T(8,128)(2,1)S(1)} %pad_maximum_fusion.2), channel_id=1, source_target_pairs={{0,24},{1,25},{2,26},{3,27},{4,28},{5,29},{6,30},{7,31},{8,16},{9,... | collective-permute-start | bytes 196616 | tf_op jit(solution)/shard_map/ppermute | solution.py:19
  14.5 9.3 %collective-permute-start.5 = (bf16[128,1024]{1,0:T(8,128)(2,1)S(1)}, bf16[128,1024]{1,0:T(8,128)(2,1)S(1)}, u32[]{:S(2)}, u32[]{:S(2)}) collective-permute-start(bf16[128,1024]{1,0:T(8,128)(2,1)S(1)} %constant_dynamic-update-slice_fusion.w0), channel_id=1, source_target_pairs={{0,2},{1,3},{2,0},{3,1},{4,6},{5,7},{6,4},{7,5},{8,10},{9,11},{10,... | collective-permute-start | bytes 786440 | tf_op jit(solution)/shard_map/ppermute | solution.py:19
  16.1 12.0 %collective-permute-start.6 = (bf16[128,1024]{1,0:T(8,128)(2,1)S(1)}, bf16[128,1024]{1,0:T(8,128)(2,1)S(1)}, u32[]{:S(2)}, u32[]{:S(2)}) collective-permute-start(bf16[128,1024]{1,0:T(8,128)(2,1)S(1)} %constant_dynamic-update-slice_fusion.w0), channel_id=1, source_target_pairs={{0,4},{1,5},{2,6},{3,7},{4,0},{5,1},{6,2},{7,3},{8,12},{9,13},{10,... | collective-permute-start | bytes 786440 | tf_op jit(solution)/shard_map/ppermute | solution.py:19
  17.6 10.5 %collective-permute-start.7 = (bf16[128,1024]{1,0:T(8,128)(2,1)S(1)}, bf16[128,1024]{1,0:T(8,128)(2,1)S(1)}, u32[]{:S(2)}, u32[]{:S(2)}) collective-permute-start(bf16[128,1024]{1,0:T(8,128)(2,1)S(1)} %constant_dynamic-update-slice_fusion.w0), channel_id=1, source_target_pairs={{0,6},{1,7},{2,4},{3,5},{4,2},{5,3},{6,0},{7,1},{8,14},{9,15},{10,... | collective-permute-start | bytes 786440 | tf_op jit(solution)/shard_map/ppermute | solution.py:19
  32.4 42.7 %collective-permute-start.8 = (bf16[1024,1024]{1,0:T(8,128)(2,1)S(1)}, bf16[1024,1024]{1,0:T(8,128)(2,1)}, u32[]{:S(2)}, u32[]{:S(2)}) collective-permute-start(bf16[1024,1024]{1,0:T(8,128)(2,1)S(1)} %shard_map.95.mine), channel_id=1, source_target_pairs={{0,1},{1,0},{2,3},{3,2},{4,5},{5,4},{6,7},{7,6},{8,9},{9,8},{10,11... | collective-permute-start | bytes 6291464 | tf_op jit(solution)/shard_map/ppermute | solution.py:19
  36.3 8.1 %collective-permute-start.10 = (bf16[128,512]{1,0:T(8,128)(2,1)S(1)}, bf16[128,512]{1,0:T(8,128)(2,1)S(1)}, u32[]{:S(2)}, u32[]{:S(2)}) collective-permute-start(bf16[128,512]{1,0:T(8,128)(2,1)S(1)} %pad_maximum_fusion.1), channel_id=1, source_target_pairs={{0,8},{1,9},{2,10},{3,11},{4,12},{5,13},{6,14},{7,15},{8,0},{9,1},... | collective-permute-start | bytes 393224 | tf_op jit(solution)/shard_map/ppermute | solution.py:19
  37.6 12.9 %collective-permute-start.11 = (bf16[128,512]{1,0:T(8,128)(2,1)S(1)}, bf16[128,512]{1,0:T(8,128)(2,1)S(1)}, u32[]{:S(2)}, u32[]{:S(2)}) collective-permute-start(bf16[128,512]{1,0:T(8,128)(2,1)S(1)} %pad_maximum_fusion.1), channel_id=1, source_target_pairs={{0,16},{1,17},{2,18},{3,19},{4,20},{5,21},{6,22},{7,23},{8,24},{9,... | collective-permute-start | bytes 393224 | tf_op jit(solution)/shard_map/ppermute | solution.py:19
  38.6 12.0 %collective-permute-start.12 = (bf16[128,512]{1,0:T(8,128)(2,1)S(1)}, bf16[128,512]{1,0:T(8,128)(2,1)S(1)}, u32[]{:S(2)}, u32[]{:S(2)}) collective-permute-start(bf16[128,512]{1,0:T(8,128)(2,1)S(1)} %pad_maximum_fusion.1), channel_id=1, source_target_pairs={{0,24},{1,25},{2,26},{3,27},{4,28},{5,29},{6,30},{7,31},{8,16},{9,... | collective-permute-start | bytes 393224 | tf_op jit(solution)/shard_map/ppermute | solution.py:19
  50.6 14.9 %collective-permute-start.13 = (bf16[512,512]{1,0:T(8,128)(2,1)S(1)}, bf16[512,512]{1,0:T(8,128)(2,1)S(1)}, u32[]{:S(2)}, u32[]{:S(2)}) collective-permute-start(bf16[512,512]{1,0:T(8,128)(2,1)S(1)} %constant_dynamic-update-slice_fusion.5.w0), channel_id=1, source_target_pairs={{0,2},{1,3},{2,0},{3,1},{4,6},{5,7},{6,4},{7,5},{8,10},{9,11},{10,... | collective-permute-start | bytes 1572872 | tf_op jit(solution)/shard_map/ppermute | solution.py:19
  51.9 21.5 %collective-permute-start.14 = (bf16[512,512]{1,0:T(8,128)(2,1)S(1)}, bf16[512,512]{1,0:T(8,128)(2,1)S(1)}, u32[]{:S(2)}, u32[]{:S(2)}) collective-permute-start(bf16[512,512]{1,0:T(8,128)(2,1)S(1)} %constant_dynamic-update-slice_fusion.5.w0), channel_id=1, source_target_pairs={{0,4},{1,5},{2,6},{3,7},{4,0},{5,1},{6,2},{7,3},{8,12},{9,13},{10,... | collective-permute-start | bytes 1572872 | tf_op jit(solution)/shard_map/ppermute | solution.py:19
  52.7 22.3 %collective-permute-start.15 = (bf16[512,512]{1,0:T(8,128)(2,1)S(1)}, bf16[512,512]{1,0:T(8,128)(2,1)S(1)}, u32[]{:S(2)}, u32[]{:S(2)}) collective-permute-start(bf16[512,512]{1,0:T(8,128)(2,1)S(1)} %constant_dynamic-update-slice_fusion.5.w0), channel_id=1, source_target_pairs={{0,6},{1,7},{2,4},{3,5},{4,2},{5,3},{6,0},{7,1},{8,14},{9,15},{10,... | collective-permute-start | bytes 1572872 | tf_op jit(solution)/shard_map/ppermute | solution.py:19
  56.0 59.9 %collective-permute-start.17 = (bf16[512,1024]{1,0:T(8,128)(2,1)S(1)}, bf16[512,1024]{1,0:T(8,128)(2,1)S(1)}, u32[]{:S(2)}, u32[]{:S(2)}) collective-permute-start(bf16[512,1024]{1,0:T(8,128)(2,1)S(1)} %convert_bitcast_fusion.own), channel_id=1, source_target_pairs={{0,1},{1,0},{2,3},{3,2},{4,5},{5,4},{6,7},{7,6},{8,9},{9,8},{10,11... | collective-permute-start | bytes 3145736 | tf_op jit(solution)/shard_map/ppermute | solution.py:19
  83.4 54.9 %collective-permute-start.16 = (f32[512,512]{1,0:T(8,128)}, f32[512,512]{1,0:T(8,128)S(1)}, u32[]{:S(2)}, u32[]{:S(2)}) collective-permute-start(f32[512,512]{1,0:T(8,128)} %get-tuple-element.6), channel_id=1, source_target_pairs={{0,1},{1,0},{2,3},{3,2},{4,5},{5,4},{6,7},{7,6},{8,9},{9,8},{10,11... | collective-permute-start | bytes 3145736 | tf_op jit(solution)/shard_map/ppermute | solution.py:19
  83.5 4.5 %collective-permute-start.18 = (bf16[32,1024]{1,0:T(8,128)(2,1)S(1)}, bf16[32,1024]{1,0:T(8,128)(2,1)S(1)}, u32[]{:S(2)}, u32[]{:S(2)}) collective-permute-start(bf16[32,1024]{1,0:T(8,128)(2,1)S(1)} %bitcast.10), channel_id=1, source_target_pairs={{0,2},{1,3},{2,0},{3,1},{4,6},{5,7},{6,4},{7,5},{8,10},{9,11},{10,... | collective-permute-start | bytes 196616 | tf_op jit(solution)/shard_map/ppermute | solution.py:19
  84.4 4.3 %collective-permute-start.19 = (bf16[32,1024]{1,0:T(8,128)(2,1)S(1)}, bf16[32,1024]{1,0:T(8,128)(2,1)S(1)}, u32[]{:S(2)}, u32[]{:S(2)}) collective-permute-start(bf16[32,1024]{1,0:T(8,128)(2,1)S(1)} %bitcast.11), channel_id=1, source_target_pairs={{0,4},{1,5},{2,6},{3,7},{4,0},{5,1},{6,2},{7,3},{8,12},{9,13},{10,... | collective-permute-start | bytes 196616 | tf_op jit(solution)/shard_map/ppermute | solution.py:19
  85.9 5.2 %collective-permute-start.20 = (bf16[32,1024]{1,0:T(8,128)(2,1)S(1)}, bf16[32,1024]{1,0:T(8,128)(2,1)S(1)}, u32[]{:S(2)}, u32[]{:S(2)}) collective-permute-start(bf16[32,1024]{1,0:T(8,128)(2,1)S(1)} %bitcast.12), channel_id=1, source_target_pairs={{0,6},{1,7},{2,4},{3,5},{4,2},{5,3},{6,0},{7,1},{8,14},{9,15},{10,... | collective-permute-start | bytes 196616 | tf_op jit(solution)/shard_map/ppermute | solution.py:19
  91.1 12.7 %collective-permute-start.21 = (bf16[128,1024]{1,0:T(8,128)(2,1)S(1)}, bf16[128,1024]{1,0:T(8,128)(2,1)S(1)}, u32[]{:S(2)}, u32[]{:S(2)}) collective-permute-start(bf16[128,1024]{1,0:T(8,128)(2,1)S(1)} %pad_maximum_fusion.u0), channel_id=1, source_target_pairs={{0,8},{1,9},{2,10},{3,11},{4,12},{5,13},{6,14},{7,15},{8,0},{9,1},... | collective-permute-start | bytes 786440 | tf_op jit(solution)/shard_map/ppermute | solution.py:19
  94.5 21.4 %collective-permute-start.22 = (bf16[128,1024]{1,0:T(8,128)(2,1)S(1)}, bf16[128,1024]{1,0:T(8,128)(2,1)S(1)}, u32[]{:S(2)}, u32[]{:S(2)}) collective-permute-start(bf16[128,1024]{1,0:T(8,128)(2,1)S(1)} %pad_maximum_fusion.u0), channel_id=1, source_target_pairs={{0,16},{1,17},{2,18},{3,19},{4,20},{5,21},{6,22},{7,23},{8,24},{9,... | collective-permute-start | bytes 786440 | tf_op jit(solution)/shard_map/ppermute | solution.py:19
  95.5 20.4 %collective-permute-start.23 = (bf16[128,1024]{1,0:T(8,128)(2,1)S(1)}, bf16[128,1024]{1,0:T(8,128)(2,1)S(1)}, u32[]{:S(2)}, u32[]{:S(2)}) collective-permute-start(bf16[128,1024]{1,0:T(8,128)(2,1)S(1)} %pad_maximum_fusion.u0), channel_id=1, source_target_pairs={{0,24},{1,25},{2,26},{3,27},{4,28},{5,29},{6,30},{7,31},{8,16},{9,... | collective-permute-start | bytes 786440 | tf_op jit(solution)/shard_map/ppermute | solution.py:19
  127.2 5.3 %collective-permute-start.26 = (f32[3,512]{1,0:T(4,128)S(1)}, f32[3,512]{1,0:T(4,128)S(1)}, u32[]{:S(2)}, u32[]{:S(2)}) collective-permute-start(f32[3,512]{1,0:T(4,128)S(1)} %max.13), channel_id=1, source_target_pairs={{0,8},{1,9},{2,10},{3,11},{4,12},{5,13},{6,14},{7,15},{8,0},{9,1},... | collective-permute-start | bytes 18440 | tf_op jit(solution)/shard_map/ppermute | solution.py:19
  132.5 4.5 %collective-permute-start.27 = (f32[3,512]{1,0:T(4,128)S(1)}, f32[3,512]{1,0:T(4,128)S(1)}, u32[]{:S(2)}, u32[]{:S(2)}) collective-permute-start(f32[3,512]{1,0:T(4,128)S(1)} %max.14), channel_id=1, source_target_pairs={{0,16},{1,17},{2,18},{3,19},{4,20},{5,21},{6,22},{7,23},{8,24},{9,... | collective-permute-start | bytes 18440 | tf_op jit(solution)/shard_map/ppermute | solution.py:19
  (11 other events, 240.0 us)

commit v2 on v0

v2 whole, which is shorter than its diff:
```python
import functools

import jax
import jax.numpy as jnp
from jax import lax
from jax.experimental import pallas as pl
from jax.experimental.pallas import tpu as pltpu
from jax.sharding import PartitionSpec as P

VMEM = pl.BlockSpec(memory_space=pltpu.VMEM)
SMEM = pl.BlockSpec(memory_space=pltpu.SMEM)
BF16 = jnp.bfloat16
F32 = jnp.float32
MIB = 1 << 20


def swap(x, axis, n, k):
    return lax.ppermute(x, axis, [(i, i ^ k) for i in range(n)])


def chip_and_core():
    me = lax.axis_index("fsdp")
    return me // 2, me % 2


def score_parts(idx, lo, step):
    index = idx[...]
    step_d = jnp.zeros(index.shape, F32)
    lo_d = jnp.zeros(index.shape, F32)
    for level in range(lo.shape[0]):
        step_d = jnp.where(index == level, step[level], step_d)
        lo_d = jnp.where(index == level, lo[level], lo_d)
    high = lo_d.astype(BF16)
    rest = lo_d - high.astype(F32)
    middle = rest.astype(BF16)
    low = rest - middle.astype(F32)
    row = lax.broadcasted_iota(jnp.int32, (16, index.shape[1]), 0)
    parts = jnp.where(
        row == 0,
        high.astype(F32),
        jnp.where(row == 1, middle.astype(F32), jnp.where(row == 2, low, 0.0)),
    ).astype(BF16)
    return step_d, parts


def score(step_d, parts, own, other, member):
    contract = (((1,), (1,)), ((), ()))
    product = lambda left, right: lax.dot_general(
        left, right, contract, preferred_element_type=F32
    )
    folded = (member.astype(F32) * step_d).astype(BF16)
    most = jnp.maximum(
        jnp.max(product(own[...], folded), axis=0, keepdims=True),
        jnp.max(product(other[...], folded), axis=0, keepdims=True),
    )
    return most + jnp.sum(product(parts, member), axis=0, keepdims=True)


def near_score_kernel(idx, lo, step, own, other, members, best):
    step_d, parts = score_parts(idx, lo, step)
    best[...] = score(step_d, parts, own, other, members[...])


def far_score_kernel(idx, lo, step, own, other, members, near, best):
    chip, _ = chip_and_core()
    step_d, parts = score_parts(idx, lo, step)
    found = jnp.concatenate(
        [near[...], score(step_d, parts, own, other, members[...])], axis=1
    )
    total = found.shape[1]
    each = total // 16
    lane = lax.broadcasted_iota(jnp.int32, found.shape, 1)
    for bit in (1, 2, 4, 8):
        far = bit * each
        crossed = jnp.where(
            (lane // far) % 2 == 1,
            pltpu.roll(found, far, 1),
            pltpu.roll(found, total - far, 1),
        )
        found = jnp.where((chip // bit) % 2 == 1, crossed, found)
    best[...] = found


def order_kernel(own, other, ordered):
    chip, core = chip_and_core()
    count, depth = own.shape
    each = depth // 32
    row = lax.broadcasted_iota(jnp.int32, (depth, depth), 0)
    col = lax.broadcasted_iota(jnp.int32, (depth, depth), 1)
    slot = col // each
    key = slot // 8 + 4 * ((slot // 2) % 4)
    source = ((chip ^ key) * 2 + (core + slot) % 2) * each + col % each
    pick = jnp.where(row == source, 1.0, 0.0).astype(BF16)
    for at, features in ((0, own), (count, other)):
        ordered[at : at + count, :] = jnp.dot(
            features[...], pick, preferred_element_type=F32
        ).astype(BF16)


def hidden_kernel(features, w0, w1, w2, w3, hidden):
    weights = jnp.concatenate([w[...] for w in (w0, w1, w2, w3)], axis=0)
    block = 256
    for at in range(0, features.shape[0], block):
        v = 0.5 * jnp.dot(
            features[at : at + block, :], weights, preferred_element_type=F32
        )
        hidden[at : at + block, :] = (v * (1.0 + jnp.tanh(v))).astype(BF16)


def add_up(keys, mine, theirs, pieces, finish):
    chip, core = chip_and_core()
    depth = mine.shape[1]
    rows = pieces[0].shape[0] // 4
    count = mine.shape[0]
    block = 256
    near = chip // 8 == core

    def work(first, second, first_is_mine):
        for at in range(0, count, block):
            flip = (at + count // 2) % count
            total = None
            for piece, chips in zip(pieces, keys):
                left = []
                for slot, key in enumerate(chips):
                    source = first if slot < 2 else second
                    start = at if (slot < 2) == first_is_mine else flip
                    column = pl.multiple_of((((chip ^ key) * rows) % depth), rows)
                    left.append(source[start : start + block, pl.ds(column, rows)])
                product = jnp.dot(
                    jnp.concatenate(left, axis=1), piece[...], preferred_element_type=F32
                )
                total = product if total is None else total + product
            finish(at, total)

    @pl.when(near)
    def _():
        work(mine, theirs, True)

    @pl.when(jnp.logical_not(near))
    def _():
        work(theirs, mine, False)


def first_embed_kernel(keys, mine, theirs, w0, w1, partial):
    def finish(at, total):
        partial[at : at + total.shape[0], :] = total

    add_up(keys, mine, theirs, (w0, w1), finish)


def last_embed_kernel(keys, mine, theirs, w0, w1, partial, own, other, bounds):
    count = own.shape[0]
    bounds[...] = jnp.full(bounds.shape, -jnp.inf, F32)

    def finish(at, total):
        total = total + partial[at : at + total.shape[0], :]
        if at < count:
            own[at : at + total.shape[0], :] = total
        else:
            other[at - count : at - count + total.shape[0], :] = total
        top = jnp.max(total, axis=0, keepdims=True)
        bottom = jnp.max(-total, axis=0, keepdims=True)
        bounds[0:1, :] = jnp.maximum(bounds[0:1, :], top)
        bounds[1:2, :] = jnp.maximum(bounds[1:2, :], bottom)

    add_up(keys, mine, theirs, (w0, w1), finish)


def code_kernel(own, other, here, there, codes):
    _, core = chip_and_core()
    width = own.shape[1]
    for values, bounds, part in ((own, here, core), (other, there, 1 - core)):
        upper = bounds[0:1, :]
        lower = -bounds[1:2, :]
        mid = (upper + lower) * 0.5
        scale = 7.5 / ((upper - lower) * 0.5 + 1e-05)
        at = pl.ds(pl.multiple_of(part * width, width), width)
        codes[:, at] = ((values[...] - mid) * scale).astype(BF16)


def call(kernel, out, specs, flops, limit=24):
    outs = jax.tree.leaves(out)
    return pl.pallas_call(
        kernel,
        out_shape=out,
        in_specs=specs,
        out_specs=jax.tree.map(lambda _: VMEM, out),
        compiler_params=pltpu.CompilerParams(vmem_limit_bytes=limit * MIB),
        cost_estimate=pl.CostEstimate(
            flops=flops,
            transcendentals=0,
            bytes_accessed=sum(o.size * o.dtype.itemsize for o in outs),
        ),
    )


def shape(dims, dtype):
    return jax.ShapeDtypeStruct(dims, dtype)


def half_columns(x, core):
    width = x.shape[1] // 2
    return lax.dynamic_slice_in_dim(x, core * width, width, 1)


def by_permutes(n, n_rep, items, w_in, w_out, users, res_codes, range_idx, range_lo, range_step):
    move = lambda x, k: swap(x, "fsdp", n, k)
    cat = lambda *parts: jnp.concatenate(parts, axis=0)
    chip, core = chip_and_core()
    keys = tuple(tuple(b + 4 * j for j in range(4)) for b in range(4))
    count, d_in = items.shape[1:]
    wide = w_in.shape[1] // 2
    width = w_out.shape[1] // 2

    in_rows = cat(half_columns(w_in, core), move(half_columns(w_in, 1 - core), 1))
    in_column = cat(in_rows, *(move(in_rows, k) for k in (8, 16, 24)))
    here, there = half_columns(w_out, core), move(half_columns(w_out, 1 - core), 1)
    out_rows = jnp.where(core == 0, cat(here, there), cat(there, here))
    out_pair = cat(out_rows, move(out_rows, 8))
    user_pair = cat(users[0], move(users[0], 2))
    user_plane = cat(user_pair, move(user_pair, 4))

    features = items[0]
    ordered = call(
        order_kernel, shape((2 * count, d_in), BF16), [VMEM, VMEM], 4 * count * d_in * d_in
    )(features, move(features, 1))
    in_column, out_pair, user_plane, ordered, resident = lax.optimization_barrier(
        (in_column, out_pair, user_plane, ordered, res_codes[0])
    )
    in_pieces = [in_column] + [move(in_column, k) for k in (2, 4, 6)]
    out_column = cat(out_pair, move(out_pair, 16))
    near_users = cat(user_plane, move(user_plane, 8))
    codes = resident.astype(BF16)
    codes_other = move(codes, 1)

    *in_pieces, out_column, near_users = lax.optimization_barrier(
        (*in_pieces, out_column, near_users)
    )
    out_pieces = [out_column] + [move(out_column, k) for k in (2, 4, 6)]
    far_users = move(near_users, 16)
    last_pieces, far_users = lax.optimization_barrier((out_pieces[2:], far_users))
    ranges = (range_idx[None, :], range_lo, range_step)
    members = near_users.shape[0]
    score_flops = 4 * members * count * users.shape[2]
    near_best = call(
        near_score_kernel,
        shape((1, members), F32),
        [VMEM, SMEM, SMEM] + [VMEM] * 3,
        score_flops,
    )(*ranges, codes, codes_other, near_users)

    hidden = call(
        hidden_kernel,
        shape((2 * count, wide), BF16),
        [VMEM] * 5,
        4 * count * d_in * wide,
    )(ordered, *in_pieces)
    hidden_other = move(hidden, 1)

    best = call(
        far_score_kernel,
        shape((1, 2 * members), F32),
        [VMEM, SMEM, SMEM] + [VMEM] * 4,
        score_flops,
    )(*ranges, codes, codes_other, far_users, near_best)

    partial = call(
        functools.partial(first_embed_kernel, keys[:2]),
        shape((2 * count, width), F32),
        [VMEM] * 4,
        4 * count * wide * width,
    )(hidden, hidden_other, *out_pieces[:2])
    own, other, bounds = call(
        functools.partial(last_embed_kernel, keys[2:]),
        (
            shape((count, width), F32),
            shape((count, width), F32),
            shape((2, width), F32),
        ),
        [VMEM] * 5,
        4 * count * wide * width,
    )(hidden, hidden_other, *last_pieces, partial)
    received = move(other, 1)

    merged = cat(bounds, best)
    for k in (2, 4, 8, 16):
        merged = jnp.maximum(merged, move(merged, k))
    bounds = merged[:2]
    if n_rep > 1:
        bounds = lax.pmax(bounds, "rep")
    new_codes = call(
        code_kernel, shape((count, 2 * width), BF16), [VMEM] * 4, 4 * count * width
    )(own, received, bounds, move(bounds, 1))
    each = users.shape[1]
    mine = lax.dynamic_slice_in_dim(merged[2:], chip * each, each, 1)
    return new_codes[None], mine


def on_any(items, w_in, w_out, users, res_codes, range_idx, range_lo, range_step):
    features = items[0]
    dot = functools.partial(jnp.dot, preferred_element_type=F32)
    first = dot(features, lax.all_gather(w_in, "fsdp", axis=0, tiled=True))
    hidden = jax.nn.silu(first).astype(BF16)
    embed = dot(hidden, lax.all_gather(w_out, "fsdp", axis=0, tiled=True))
    upper = lax.pmax(jnp.max(embed, axis=0), ("fsdp", "rep"))
    lower = lax.pmin(jnp.min(embed, axis=0), ("fsdp", "rep"))
    mid = (upper + lower) * 0.5
    half = (upper - lower) * 0.5
    new_codes = (7.5 * (embed - mid) / (half + 1e-05)).astype(BF16)[None]
    levels = jnp.arange(range_lo.shape[0], dtype=jnp.int32)
    match = (range_idx[None, :] == levels[:, None]).astype(F32)
    step_d = jnp.sum(range_step[:, None] * match, axis=0)
    lo_d = jnp.sum(range_lo[:, None] * match, axis=0)
    member = lax.all_gather(users, "fsdp", axis=1, tiled=True)[0]
    folded = (member.astype(F32) * step_d).astype(BF16)
    offset = jnp.dot(member.astype(F32), lo_d, precision=lax.Precision.HIGHEST)
    scores = dot(res_codes[0].astype(BF16), folded.T)
    merged = lax.pmax((jnp.max(scores, axis=0) + offset)[None], "fsdp")
    count = users.shape[1]
    best = lax.dynamic_slice_in_dim(merged, lax.axis_index("fsdp") * count, count, 1)
    return new_codes, best


def solution(mesh):
    n = mesh.shape["fsdp"]
    body = on_any
    if n == 32:
        body = functools.partial(by_permutes, n, mesh.shape["rep"])
    return jax.shard_map(
        body,
        mesh=mesh,
        in_specs=(
            P("rep", ("grp", "fsdp"), None),
            P("fsdp", None),
            P("fsdp", None),
            P("rep", ("grp", "fsdp"), None),
            P("rep", ("grp", "fsdp"), None),
            P("grp"),
            P("grp"),
            P("grp"),
        ),
        out_specs=(P("rep", ("grp", "fsdp"), None), P("rep", ("grp", "fsdp"))),
        check_vma=False,
    )
```

time: 286 us -> 90.8 us (0.32)
  waiting for transfers between devices: 177 us -> 48.2 us
  blocking collectives: 79.3 us -> 0 us
  starting transfers between devices: 0.11 us -> 28 us
  between operations: 13.8 us -> 0.92 us
  matrix products: 12.8 us -> 0 us
  Pallas kernels: 0 us -> 8.94 us
    all_gather x3 -> x0, waiting for transfers between devices: 175 us -> none  [the longest x1 63.8 us: on_device(): embed = row_adder(hidden, lax.all_gather(w_out, 'fsdp', axis=0, tiled=True))]
    ppermute x0 -> x26, waiting for transfers between devices: none -> 48.2 us  [swap(): return lax.ppermute(x, axis, [(i, i ^ k) for i in range(n)])]
    pmax x1 -> x0, blocking collectives: 40.1 us -> none  [on_device(): upper = lax.pmax(local_upper, ('fsdp', 'rep'))]
    pmin x1 -> x0, blocking collectives: 39.2 us -> none  [on_device(): lower = lax.pmin(local_lower, ('fsdp', 'rep'))]
    ppermute x0 -> x26, starting transfers between devices: none -> 28 us  [swap(): return lax.ppermute(x, axis, [(i, i ^ k) for i in range(n)])]
    dot_general x3 -> x0, matrix products: 12.8 us -> none  [the longest x1 6.45 us: row_adder(): return jnp.dot(left, piece, preferred_element_type=jnp.float32)]
    pallas_call x0 -> x7, Pallas kernels: none -> 8.94 us  [the longest x1 1.6 us: by_permutes(): call(far_score_kernel, shape((1, 2 * members), F32), [VMEM, SMEM, SMEM] +...]
  transfers between devices with their start and end apart: 3 -> 26, of which waited for: 3 -> 12; matrix products, arithmetic and copies ran while one was open for 3% -> 5% of each run, Pallas kernels for 0% -> 6%
where the time goes in v2:
time: 90.8 us; the launch traced here: 90.5 us
  waiting for transfers between devices  48.2 us (53%)
  starting transfers between devices  28 us (31%)
  Pallas kernels  8.94 us (10%)
  local copies, waits for them, and re-layouts  2.32 us (3%)
  other arithmetic  2.11 us (2%)
  between operations  0.92 us (1%)
    ppermute x26, waiting for transfers between devices, swap(): return lax.ppermute(x, axis, [(i, i ^ k) for i in range(n)])  48.2 us
    ppermute x26, starting transfers between devices, swap(): return lax.ppermute(x, axis, [(i, i ^ k) for i in range(n)])  28 us
  transfers between devices with their start and end apart: 26, of which 12 were waited for; matrix products, arithmetic and copies ran while one was open for 5% of the time, Pallas kernels for 6%

profile of v2, /device:TPU:0, one launch (start us, length us, event | category | flops | bytes accessed | tf_op | source)
XLA Modules:
  0.0 90.5 jit_solution(3284942938577757409)
XLA Ops:
  0.6 3.0 %collective-permute-start.6 = (bf16[32,1024]{1,0:T(8,128)(2,1)}, bf16[32,1024]{1,0:T(8,128)(2,1)S(1)}, u32[]{:S(2)}, u32[]{:S(2)}) collective-permute-start(bf16[32,1024]{1,0:T(8,128)(2,1)} %bitcast.11), channel_id=1, source_target_pairs={{0,2},{1,3},{2,0},{3,1},{4,6},{5,7},{6,4},{7,5},{8,10},{9,11},{10,... | collective-permute-start | bytes 196616 | tf_op jit(solution)/shard_map/ppermute | solution.py:18
  6.0 3.7 %collective-permute-start.3 = (bf16[32,1024]{1,0:T(8,128)(2,1)S(1)}, bf16[32,1024]{1,0:T(8,128)(2,1)S(1)}, u32[]{:S(2)}, u32[]{:S(2)}) collective-permute-start(bf16[32,1024]{1,0:T(8,128)(2,1)S(1)} %pad_maximum_fusion.5), channel_id=1, source_target_pairs={{0,24},{1,25},{2,26},{3,27},{4,28},{5,29},{6,30},{7,31},{8,16},{9,... | collective-permute-start | bytes 196616 | tf_op jit(solution)/shard_map/ppermute | solution.py:18
  11.4 1.6 %collective-permute-start.7 = (bf16[64,1024]{1,0:T(8,128)(2,1)S(1)}, bf16[64,1024]{1,0:T(8,128)(2,1)S(1)}, u32[]{:S(2)}, u32[]{:S(2)}) collective-permute-start(bf16[64,1024]{1,0:T(8,128)(2,1)S(1)} %pad_maximum_fusion.4), channel_id=1, source_target_pairs={{0,4},{1,5},{2,6},{3,7},{4,0},{5,1},{6,2},{7,3},{8,12},{9,13},{10,... | collective-permute-start | bytes 393224 | tf_op jit(solution)/shard_map/ppermute | solution.py:18
  13.0 1.5 %collective-permute-done.1 = bf16[32,1024]{1,0:T(8,128)(2,1)S(1)} collective-permute-done((bf16[32,1024]{1,0:T(8,128)(2,1)S(1)}, bf16[32,1024]{1,0:T(8,128)(2,1)S(1)}, u32[]{:S(2)}, u32[]{:S(2)}) %collective-permute-start.1) | collective-permute-done | bytes 65568 | tf_op jit(solution)/shard_map/ppermute | solution.py:18
  14.5 2.5 %collective-permute-start.5 = (bf16[128,512]{1,0:T(8,128)(2,1)S(1)}, bf16[128,512]{1,0:T(8,128)(2,1)S(1)}, u32[]{:S(2)}, u32[]{:S(2)}) collective-permute-start(bf16[128,512]{1,0:T(8,128)(2,1)S(1)} %maximum_select_fusion), channel_id=1, source_target_pairs={{0,8},{1,9},{2,10},{3,11},{4,12},{5,13},{6,14},{7,15},{8,0},{9,1},... | collective-permute-start | bytes 393224 | tf_op jit(solution)/shard_map/ppermute | solution.py:18
  17.9 2.4 %collective-permute-done.5 = bf16[128,512]{1,0:T(8,128)(2,1)S(1)} collective-permute-done((bf16[128,512]{1,0:T(8,128)(2,1)S(1)}, bf16[128,512]{1,0:T(8,128)(2,1)S(1)}, u32[]{:S(2)}, u32[]{:S(2)}) %collective-permute-start.5) | collective-permute-done | bytes 131104 | tf_op jit(solution)/shard_map/ppermute | solution.py:18
  21.1 1.8 %collective-permute-start.12 = (bf16[256,512]{1,0:T(8,128)(2,1)S(1)}, bf16[256,512]{1,0:T(8,128)(2,1)S(1)}, u32[]{:S(2)}, u32[]{:S(2)}) collective-permute-start(bf16[256,512]{1,0:T(8,128)(2,1)S(1)} %pad_maximum_fusion.2), channel_id=1, source_target_pairs={{0,16},{1,17},{2,18},{3,19},{4,20},{5,21},{6,22},{7,23},{8,24},{9,... | collective-permute-start | bytes 786440 | tf_op jit(solution)/shard_map/ppermute | solution.py:18
  22.9 1.7 %collective-permute-start.13 = (bf16[128,1024]{1,0:T(8,128)(2,1)S(1)}, bf16[128,1024]{1,0:T(8,128)(2,1)S(1)}, u32[]{:S(2)}, u32[]{:S(2)}) collective-permute-start(bf16[128,1024]{1,0:T(8,128)(2,1)S(1)} %pad_maximum_fusion.3), channel_id=1, source_target_pairs={{0,8},{1,9},{2,10},{3,11},{4,12},{5,13},{6,14},{7,15},{8,0},{9,1},... | collective-permute-start | bytes 786440 | tf_op jit(solution)/shard_map/ppermute | solution.py:18
  24.6 1.5 %collective-permute-start.11 = (bf16[128,1024]{1,0:T(8,128)(2,1)S(1)}, bf16[128,1024]{1,0:T(8,128)(2,1)S(1)}, u32[]{:S(2)}, u32[]{:S(2)}) collective-permute-start(bf16[128,1024]{1,0:T(8,128)(2,1)S(1)} %constant_dynamic-update-slice_fusion.w0), channel_id=1, source_target_pairs={{0,6},{1,7},{2,4},{3,5},{4,2},{5,3},{6,0},{7,1},{8,14},{9,15},{10,... | collective-permute-start | bytes 786440 | tf_op jit(solution)/shard_map/ppermute | solution.py:18
  26.6 1.5 %collective-permute-start.9 = (bf16[128,1024]{1,0:T(8,128)(2,1)S(1)}, bf16[128,1024]{1,0:T(8,128)(2,1)S(1)}, u32[]{:S(2)}, u32[]{:S(2)}) collective-permute-start(bf16[128,1024]{1,0:T(8,128)(2,1)S(1)} %constant_dynamic-update-slice_fusion.w0), channel_id=1, source_target_pairs={{0,2},{1,3},{2,0},{3,1},{4,6},{5,7},{6,4},{7,5},{8,10},{9,11},{10,... | collective-permute-start | bytes 786440 | tf_op jit(solution)/shard_map/ppermute | solution.py:18
  28.1 6.9 %collective-permute-done.12 = bf16[256,512]{1,0:T(8,128)(2,1)S(1)} collective-permute-done((bf16[256,512]{1,0:T(8,128)(2,1)S(1)}, bf16[256,512]{1,0:T(8,128)(2,1)S(1)}, u32[]{:S(2)}, u32[]{:S(2)}) %collective-permute-start.12) | collective-permute-done | bytes 262176 | tf_op jit(solution)/shard_map/ppermute | solution.py:18
  35.1 2.8 %collective-permute-done.10.w2 = bf16[128,1024]{1,0:T(8,128)(2,1)S(1)} collective-permute-done((bf16[128,1024]{1,0:T(8,128)(2,1)S(1)}, bf16[128,1024]{1,0:T(8,128)(2,1)S(1)}, u32[]{:S(2)}, u32[]{:S(2)}) %collective-permute-start.10) | collective-permute-done | bytes 262176 | tf_op jit(solution)/shard_map/ppermute | solution.py:18
  38.0 1.3 %shard_map.96.mine = bf16[1024,1024]{1,0:T(8,128)(2,1)S(1)} custom-call(bf16[1024,512]{1,0:T(8,128)(2,1)S(1)} %shard_map.95.features, bf16[128,1024]{1,0:T(8,128)(2,1)S(1)} %constant_dynamic-update-slice_fusion.w0, bf16[128,1024]{1,0:T(8,128)(2,1)S(1)} %collective-permute-done.9.w1, bf16[128,1024]{1,0:T(8,128)(2,1)S(1)} %collective-permute-done.10.w2, ...), custom_call_target="tpu_custom_call" | custom-call | flops 1073741824 | bytes 2097152 | tf_op jit(solution)/shard_map/pallas_call | solution.py:252
  40.4 1.4 %collective-permute-start.16 = (bf16[512,512]{1,0:T(8,128)(2,1)S(1)}, bf16[512,512]{1,0:T(8,128)(2,1)S(1)}, u32[]{:S(2)}, u32[]{:S(2)}) collective-permute-start(bf16[512,512]{1,0:T(8,128)(2,1)S(1)} %pad_maximum_fusion.w0), channel_id=1, source_target_pairs={{0,6},{1,7},{2,4},{3,5},{4,2},{5,3},{6,0},{7,1},{8,14},{9,15},{10,... | collective-permute-start | bytes 1572872 | tf_op jit(solution)/shard_map/ppermute | solution.py:18
  42.4 1.5 %collective-permute-start.18 = (bf16[512,512]{1,0:T(8,128)(2,1)S(1)}, bf16[512,512]{1,0:T(8,128)(2,1)S(1)}, u32[]{:S(2)}, u32[]{:S(2)}) collective-permute-start(bf16[512,512]{1,0:T(8,128)(2,1)S(1)} %pad_maximum_fusion.w0), channel_id=1, source_target_pairs={{0,2},{1,3},{2,0},{3,1},{4,6},{5,7},{6,4},{7,5},{8,10},{9,11},{10,... | collective-permute-start | bytes 1572872 | tf_op jit(solution)/shard_map/ppermute | solution.py:18
  44.1 21.5 %collective-permute-done.17.members = bf16[256,1024]{1,0:T(8,128)(2,1)S(1)} collective-permute-done((bf16[256,1024]{1,0:T(8,128)(2,1)S(1)}, bf16[256,1024]{1,0:T(8,128)(2,1)S(1)}, u32[]{:S(2)}, u32[]{:S(2)}) %collective-permute-start.17) | collective-permute-done | bytes 524320 | tf_op jit(solution)/shard_map/ppermute | solution.py:18
  67.9 1.3 %shard_map.98 = (f32[512,512]{1,0:T(8,128)S(1)}, f32[512,512]{1,0:T(8,128)S(1)}, f32[2,512]{1,0:T(2,128)S(1)}) custom-call(bf16[1024,1024]{1,0:T(8,128)(2,1)S(1)} %shard_map.96.mine, bf16[1024,1024]{1,0:T(8,128)(2,1)S(1)} %collective-permute-done.14.theirs, bf16[512,512]{1,0:T(8,128)(2,1)S(1)} %collective-permute-done.15.w0, ...), custom_call_target="tpu_custom_call" | custom-call | flops 1073741824 | bytes 2101248 | tf_op jit(solution)/shard_map/pallas_call | solution.py:273
  69.3 1.5 %shard_map.99.near = f32[1,256]{1,0:T(1,128)S(1)} custom-call(s32[1,1024]{1,0:T(1,128)S(1)} %bitcast.7, f32[4]{0:T(128)S(1)} %copy-done.2, f32[4]{0:T(128)S(1)} %copy-done.3, bf16[512,1024]{1,0:T(8,128)(2,1)S(1)} %convert_element_type.3.own, bf16[512,1024]{1,0:T(8,128)(2,1)S(1)} %collective-permute-done.20.other, bf16[256,1024]{1,0:T(8,128)(2,1)S(1)} %pad_maximum_fusion.1.members), custom_call_target="tpu_custom_call" | custom-call | flops 536870912 | bytes 1024 | tf_op jit(solution)/shard_map/pallas_call | solution.py:245
  70.8 1.6 %shard_map.100 = f32[1,512]{1,0:T(1,128)S(1)} custom-call(s32[1,1024]{1,0:T(1,128)S(1)} %bitcast.8, f32[4]{0:T(128)S(1)} %copy-done.2, f32[4]{0:T(128)S(1)} %copy-done.3, bf16[512,1024]{1,0:T(8,128)(2,1)S(1)} %convert_element_type.3.own, bf16[512,1024]{1,0:T(8,128)(2,1)S(1)} %collective-permute-done.20.other, ...), custom_call_target="tpu_custom_call" | custom-call | flops 536870912 | bytes 2048 | tf_op jit(solution)/shard_map/pallas_call | solution.py:260
  73.0 3.1 %collective-permute-done.21 = f32[3,512]{1,0:T(4,128)S(1)} collective-permute-done((f32[3,512]{1,0:T(4,128)S(1)}, f32[3,512]{1,0:T(4,128)S(1)}, u32[]{:S(2)}, u32[]{:S(2)}) %collective-permute-start.21) | collective-permute-done | bytes 6176 | tf_op jit(solution)/shard_map/ppermute | solution.py:18
  76.9 2.9 %collective-permute-done.22 = f32[3,512]{1,0:T(4,128)S(1)} collective-permute-done((f32[3,512]{1,0:T(4,128)S(1)}, f32[3,512]{1,0:T(4,128)S(1)}, u32[]{:S(2)}, u32[]{:S(2)}) %collective-permute-start.22) | collective-permute-done | bytes 6176 | tf_op jit(solution)/shard_map/ppermute | solution.py:18
  80.4 3.0 %collective-permute-done.23 = f32[3,512]{1,0:T(4,128)S(1)} collective-permute-done((f32[3,512]{1,0:T(4,128)S(1)}, f32[3,512]{1,0:T(4,128)S(1)}, u32[]{:S(2)}, u32[]{:S(2)}) %collective-permute-start.23) | collective-permute-done | bytes 6176 | tf_op jit(solution)/shard_map/ppermute | solution.py:18
  83.5 2.1 %collective-permute-start.24 = (f32[3,512]{1,0:T(4,128)S(1)}, f32[3,512]{1,0:T(4,128)S(1)}, u32[]{:S(2)}, u32[]{:S(2)}) collective-permute-start(f32[3,512]{1,0:T(4,128)S(1)} %max.14), channel_id=1, source_target_pairs={{0,16},{1,17},{2,18},{3,19},{4,20},{5,21},{6,22},{7,23},{8,24},{9,... | collective-permute-start | bytes 18440 | tf_op jit(solution)/shard_map/ppermute | solution.py:18
  85.6 2.5 %collective-permute-done.24 = f32[3,512]{1,0:T(4,128)S(1)} collective-permute-done((f32[3,512]{1,0:T(4,128)S(1)}, f32[3,512]{1,0:T(4,128)S(1)}, u32[]{:S(2)}, u32[]{:S(2)}) %collective-permute-start.24) | collective-permute-done | bytes 6176 | tf_op jit(solution)/shard_map/ppermute | solution.py:18
  (67 shorter events, 14.9 us)
Async XLA Ops:
  0.6 9.1 %collective-permute-start.6 = (bf16[32,1024]{1,0:T(8,128)(2,1)}, bf16[32,1024]{1,0:T(8,128)(2,1)S(1)}, u32[]{:S(2)}, u32[]{:S(2)}) collective-permute-start(bf16[32,1024]{1,0:T(8,128)(2,1)} %bitcast.11), channel_id=1, source_target_pairs={{0,2},{1,3},{2,0},{3,1},{4,6},{5,7},{6,4},{7,5},{8,10},{9,11},{10,... | collective-permute-start | bytes 196616 | tf_op jit(solution)/shard_map/ppermute | solution.py:18
  5.4 5.9 %collective-permute-start.4 = (bf16[64,512]{1,0:T(8,128)(2,1)S(1)}, bf16[64,512]{1,0:T(8,128)(2,1)S(1)}, u32[]{:S(2)}, u32[]{:S(2)}) collective-permute-start(bf16[64,512]{1,0:T(8,128)(2,1)S(1)} %get-tuple-element.39), channel_id=1, source_target_pairs={{0,1},{1,0},{2,3},{3,2},{4,5},{5,4},{6,7},{7,6},{8,9},{9,8},{10,11... | collective-permute-start | bytes 196616 | tf_op jit(solution)/shard_map/ppermute | solution.py:18
  5.9 14.4 %collective-permute-start.8 = (bf16[512,512]{1,0:T(8,128)(2,1)}, bf16[512,512]{1,0:T(8,128)(2,1)S(1)}, u32[]{:S(2)}, u32[]{:S(2)}) collective-permute-start(bf16[512,512]{1,0:T(8,128)(2,1)} %bitcast.5), channel_id=1, source_target_pairs={{0,1},{1,0},{2,3},{3,2},{4,5},{5,4},{6,7},{7,6},{8,9},{9,8},{10,11... | collective-permute-start | bytes 1572872 | tf_op jit(solution)/shard_map/ppermute | solution.py:18
  6.0 11.0 %collective-permute-start.3 = (bf16[32,1024]{1,0:T(8,128)(2,1)S(1)}, bf16[32,1024]{1,0:T(8,128)(2,1)S(1)}, u32[]{:S(2)}, u32[]{:S(2)}) collective-permute-start(bf16[32,1024]{1,0:T(8,128)(2,1)S(1)} %pad_maximum_fusion.5), channel_id=1, source_target_pairs={{0,24},{1,25},{2,26},{3,27},{4,28},{5,29},{6,30},{7,31},{8,16},{9,... | collective-permute-start | bytes 196616 | tf_op jit(solution)/shard_map/ppermute | solution.py:18
  9.7 7.3 %collective-permute-start.2 = (bf16[32,1024]{1,0:T(8,128)(2,1)S(1)}, bf16[32,1024]{1,0:T(8,128)(2,1)S(1)}, u32[]{:S(2)}, u32[]{:S(2)}) collective-permute-start(bf16[32,1024]{1,0:T(8,128)(2,1)S(1)} %pad_maximum_fusion.5), channel_id=1, source_target_pairs={{0,16},{1,17},{2,18},{3,19},{4,20},{5,21},{6,22},{7,23},{8,24},{9,... | collective-permute-start | bytes 196616 | tf_op jit(solution)/shard_map/ppermute | solution.py:18
  9.7 4.8 %collective-permute-start.1 = (bf16[32,1024]{1,0:T(8,128)(2,1)S(1)}, bf16[32,1024]{1,0:T(8,128)(2,1)S(1)}, u32[]{:S(2)}, u32[]{:S(2)}) collective-permute-start(bf16[32,1024]{1,0:T(8,128)(2,1)S(1)} %pad_maximum_fusion.5), channel_id=1, source_target_pairs={{0,8},{1,9},{2,10},{3,11},{4,12},{5,13},{6,14},{7,15},{8,0},{9,1},... | collective-permute-start | bytes 196616 | tf_op jit(solution)/shard_map/ppermute | solution.py:18
  11.4 5.7 %collective-permute-start.7 = (bf16[64,1024]{1,0:T(8,128)(2,1)S(1)}, bf16[64,1024]{1,0:T(8,128)(2,1)S(1)}, u32[]{:S(2)}, u32[]{:S(2)}) collective-permute-start(bf16[64,1024]{1,0:T(8,128)(2,1)S(1)} %pad_maximum_fusion.4), channel_id=1, source_target_pairs={{0,4},{1,5},{2,6},{3,7},{4,0},{5,1},{6,2},{7,3},{8,12},{9,13},{10,... | collective-permute-start | bytes 393224 | tf_op jit(solution)/shard_map/ppermute | solution.py:18
  14.5 5.8 %collective-permute-start.5 = (bf16[128,512]{1,0:T(8,128)(2,1)S(1)}, bf16[128,512]{1,0:T(8,128)(2,1)S(1)}, u32[]{:S(2)}, u32[]{:S(2)}) collective-permute-start(bf16[128,512]{1,0:T(8,128)(2,1)S(1)} %maximum_select_fusion), channel_id=1, source_target_pairs={{0,8},{1,9},{2,10},{3,11},{4,12},{5,13},{6,14},{7,15},{8,0},{9,1},... | collective-permute-start | bytes 393224 | tf_op jit(solution)/shard_map/ppermute | solution.py:18
  21.1 13.9 %collective-permute-start.12 = (bf16[256,512]{1,0:T(8,128)(2,1)S(1)}, bf16[256,512]{1,0:T(8,128)(2,1)S(1)}, u32[]{:S(2)}, u32[]{:S(2)}) collective-permute-start(bf16[256,512]{1,0:T(8,128)(2,1)S(1)} %pad_maximum_fusion.2), channel_id=1, source_target_pairs={{0,16},{1,17},{2,18},{3,19},{4,20},{5,21},{6,22},{7,23},{8,24},{9,... | collective-permute-start | bytes 786440 | tf_op jit(solution)/shard_map/ppermute | solution.py:18
  22.9 12.1 %collective-permute-start.13 = (bf16[128,1024]{1,0:T(8,128)(2,1)S(1)}, bf16[128,1024]{1,0:T(8,128)(2,1)S(1)}, u32[]{:S(2)}, u32[]{:S(2)}) collective-permute-start(bf16[128,1024]{1,0:T(8,128)(2,1)S(1)} %pad_maximum_fusion.3), channel_id=1, source_target_pairs={{0,8},{1,9},{2,10},{3,11},{4,12},{5,13},{6,14},{7,15},{8,0},{9,1},... | collective-permute-start | bytes 786440 | tf_op jit(solution)/shard_map/ppermute | solution.py:18
  24.6 10.5 %collective-permute-start.11 = (bf16[128,1024]{1,0:T(8,128)(2,1)S(1)}, bf16[128,1024]{1,0:T(8,128)(2,1)S(1)}, u32[]{:S(2)}, u32[]{:S(2)}) collective-permute-start(bf16[128,1024]{1,0:T(8,128)(2,1)S(1)} %constant_dynamic-update-slice_fusion.w0), channel_id=1, source_target_pairs={{0,6},{1,7},{2,4},{3,5},{4,2},{5,3},{6,0},{7,1},{8,14},{9,15},{10,... | collective-permute-start | bytes 786440 | tf_op jit(solution)/shard_map/ppermute | solution.py:18
  26.1 11.8 %collective-permute-start.10 = (bf16[128,1024]{1,0:T(8,128)(2,1)S(1)}, bf16[128,1024]{1,0:T(8,128)(2,1)S(1)}, u32[]{:S(2)}, u32[]{:S(2)}) collective-permute-start(bf16[128,1024]{1,0:T(8,128)(2,1)S(1)} %constant_dynamic-update-slice_fusion.w0), channel_id=1, source_target_pairs={{0,4},{1,5},{2,6},{3,7},{4,0},{5,1},{6,2},{7,3},{8,12},{9,13},{10,... | collective-permute-start | bytes 786440 | tf_op jit(solution)/shard_map/ppermute | solution.py:18
  26.6 11.4 %collective-permute-start.9 = (bf16[128,1024]{1,0:T(8,128)(2,1)S(1)}, bf16[128,1024]{1,0:T(8,128)(2,1)S(1)}, u32[]{:S(2)}, u32[]{:S(2)}) collective-permute-start(bf16[128,1024]{1,0:T(8,128)(2,1)S(1)} %constant_dynamic-update-slice_fusion.w0), channel_id=1, source_target_pairs={{0,2},{1,3},{2,0},{3,1},{4,6},{5,7},{6,4},{7,5},{8,10},{9,11},{10,... | collective-permute-start | bytes 786440 | tf_op jit(solution)/shard_map/ppermute | solution.py:18
  39.4 27.2 %collective-permute-start.14 = (bf16[1024,1024]{1,0:T(8,128)(2,1)S(1)}, bf16[1024,1024]{1,0:T(8,128)(2,1)S(1)}, u32[]{:S(2)}, u32[]{:S(2)}) collective-permute-start(bf16[1024,1024]{1,0:T(8,128)(2,1)S(1)} %shard_map.96.mine), channel_id=1, source_target_pairs={{0,1},{1,0},{2,3},{3,2},{4,5},{5,4},{6,7},{7,6},{8,9},{9,8},{10,11... | collective-permute-start | bytes 6291464 | tf_op jit(solution)/shard_map/ppermute | solution.py:18
  39.4 26.2 %collective-permute-start.17 = (bf16[256,1024]{1,0:T(8,128)(2,1)S(1)}, bf16[256,1024]{1,0:T(8,128)(2,1)S(1)}, u32[]{:S(2)}, u32[]{:S(2)}) collective-permute-start(bf16[256,1024]{1,0:T(8,128)(2,1)S(1)} %pad_maximum_fusion.1.members), channel_id=1, source_target_pairs={{0,16},{1,17},{2,18},{3,19},{4,20},{5,21},{6,22},{7,23},{8,24},{9,... | collective-permute-start | bytes 1572872 | tf_op jit(solution)/shard_map/ppermute | solution.py:18
  40.4 25.3 %collective-permute-start.16 = (bf16[512,512]{1,0:T(8,128)(2,1)S(1)}, bf16[512,512]{1,0:T(8,128)(2,1)S(1)}, u32[]{:S(2)}, u32[]{:S(2)}) collective-permute-start(bf16[512,512]{1,0:T(8,128)(2,1)S(1)} %pad_maximum_fusion.w0), channel_id=1, source_target_pairs={{0,6},{1,7},{2,4},{3,5},{4,2},{5,3},{6,0},{7,1},{8,14},{9,15},{10,... | collective-permute-start | bytes 1572872 | tf_op jit(solution)/shard_map/ppermute | solution.py:18
  41.8 24.7 %collective-permute-start.15 = (bf16[512,512]{1,0:T(8,128)(2,1)S(1)}, bf16[512,512]{1,0:T(8,128)(2,1)S(1)}, u32[]{:S(2)}, u32[]{:S(2)}) collective-permute-start(bf16[512,512]{1,0:T(8,128)(2,1)S(1)} %pad_maximum_fusion.w0), channel_id=1, source_target_pairs={{0,4},{1,5},{2,6},{3,7},{4,0},{5,1},{6,2},{7,3},{8,12},{9,13},{10,... | collective-permute-start | bytes 1572872 | tf_op jit(solution)/shard_map/ppermute | solution.py:18
  42.4 24.1 %collective-permute-start.18 = (bf16[512,512]{1,0:T(8,128)(2,1)S(1)}, bf16[512,512]{1,0:T(8,128)(2,1)S(1)}, u32[]{:S(2)}, u32[]{:S(2)}) collective-permute-start(bf16[512,512]{1,0:T(8,128)(2,1)S(1)} %pad_maximum_fusion.w0), channel_id=1, source_target_pairs={{0,2},{1,3},{2,0},{3,1},{4,6},{5,7},{6,4},{7,5},{8,10},{9,11},{10,... | collective-permute-start | bytes 1572872 | tf_op jit(solution)/shard_map/ppermute | solution.py:18
  65.6 3.7 %collective-permute-start.20 = (bf16[512,1024]{1,0:T(8,128)(2,1)S(1)}, bf16[512,1024]{1,0:T(8,128)(2,1)S(1)}, u32[]{:S(2)}, u32[]{:S(2)}) collective-permute-start(bf16[512,1024]{1,0:T(8,128)(2,1)S(1)} %convert_element_type.3.own), channel_id=1, source_target_pairs={{0,1},{1,0},{2,3},{3,2},{4,5},{5,4},{6,7},{7,6},{8,9},{9,8},{10,11... | collective-permute-start | bytes 3145736 | tf_op jit(solution)/shard_map/ppermute | solution.py:18
  69.2 20.1 %collective-permute-start.19 = (f32[512,512]{1,0:T(8,128)S(1)}, f32[512,512]{1,0:T(8,128)S(1)}, u32[]{:S(2)}, u32[]{:S(2)}) collective-permute-start(f32[512,512]{1,0:T(8,128)S(1)} %get-tuple-element.32), channel_id=1, source_target_pairs={{0,1},{1,0},{2,3},{3,2},{4,5},{5,4},{6,7},{7,6},{8,9},{9,8},{10,11... | collective-permute-start | bytes 3145736 | tf_op jit(solution)/shard_map/ppermute | solution.py:18
  72.4 3.7 %collective-permute-start.21 = (f32[3,512]{1,0:T(4,128)S(1)}, f32[3,512]{1,0:T(4,128)S(1)}, u32[]{:S(2)}, u32[]{:S(2)}) collective-permute-start(f32[3,512]{1,0:T(4,128)S(1)} %pad_maximum_fusion.6), channel_id=1, source_target_pairs={{0,2},{1,3},{2,0},{3,1},{4,6},{5,7},{6,4},{7,5},{8,10},{9,11},{10,... | collective-permute-start | bytes 18440 | tf_op jit(solution)/shard_map/ppermute | solution.py:18
  76.1 3.7 %collective-permute-start.22 = (f32[3,512]{1,0:T(4,128)S(1)}, f32[3,512]{1,0:T(4,128)S(1)}, u32[]{:S(2)}, u32[]{:S(2)}) collective-permute-start(f32[3,512]{1,0:T(4,128)S(1)} %fusion), channel_id=1, source_target_pairs={{0,4},{1,5},{2,6},{3,7},{4,0},{5,1},{6,2},{7,3},{8,12},{9,13},{10,... | collective-permute-start | bytes 18440 | tf_op jit(solution)/shard_map/ppermute | solution.py:18
  79.8 3.7 %collective-permute-start.23 = (f32[3,512]{1,0:T(4,128)S(1)}, f32[3,512]{1,0:T(4,128)S(1)}, u32[]{:S(2)}, u32[]{:S(2)}) collective-permute-start(f32[3,512]{1,0:T(4,128)S(1)} %max.13), channel_id=1, source_target_pairs={{0,8},{1,9},{2,10},{3,11},{4,12},{5,13},{6,14},{7,15},{8,0},{9,1},... | collective-permute-start | bytes 18440 | tf_op jit(solution)/shard_map/ppermute | solution.py:18
  83.5 4.6 %collective-permute-start.24 = (f32[3,512]{1,0:T(4,128)S(1)}, f32[3,512]{1,0:T(4,128)S(1)}, u32[]{:S(2)}, u32[]{:S(2)}) collective-permute-start(f32[3,512]{1,0:T(4,128)S(1)} %max.14), channel_id=1, source_target_pairs={{0,16},{1,17},{2,18},{3,19},{4,20},{5,21},{6,22},{7,23},{8,24},{9,... | collective-permute-start | bytes 18440 | tf_op jit(solution)/shard_map/ppermute | solution.py:18
  (7 other events, 35.8 us)

commit v3 on v2

--- a/solution.py
+++ b/solution.py
@@ -56,16 +56,18 @@
     return most + jnp.sum(product(parts, member), axis=0, keepdims=True)
 
 
-def near_score_kernel(idx, lo, step, own, other, members, best):
+def near_score_kernel(idx, lo, step, own, other, u0, u1, best):
     step_d, parts = score_parts(idx, lo, step)
-    best[...] = score(step_d, parts, own, other, members[...])
-
-
-def far_score_kernel(idx, lo, step, own, other, members, near, best):
+    members = jnp.concatenate([u0[...], u1[...]], axis=0)
+    best[...] = score(step_d, parts, own, other, members)
+
+
+def far_score_kernel(idx, lo, step, own, other, u0, u1, near, best):
     chip, _ = chip_and_core()
     step_d, parts = score_parts(idx, lo, step)
+    members = jnp.concatenate([u0[...], u1[...]], axis=0)
     found = jnp.concatenate(
-        [near[...], score(step_d, parts, own, other, members[...])], axis=1
+        [near[...], score(step_d, parts, own, other, members)], axis=1
     )
     total = found.shape[1]
     each = total // 16
@@ -110,7 +112,7 @@
 def add_up(keys, mine, theirs, pieces, finish):
     chip, core = chip_and_core()
     depth = mine.shape[1]
-    rows = pieces[0].shape[0] // 4
+    rows = pieces[0].shape[0] // len(keys[0])
     count = mine.shape[0]
     block = 256
     near = chip // 8 == core
@@ -121,9 +123,9 @@
             total = None
             for piece, chips in zip(pieces, keys):
                 left = []
-                for slot, key in enumerate(chips):
-                    source = first if slot < 2 else second
-                    start = at if (slot < 2) == first_is_mine else flip
+                for key in chips:
+                    source = first if key < 8 else second
+                    start = at if (key < 8) == first_is_mine else flip
                     column = pl.multiple_of((((chip ^ key) * rows) % depth), rows)
                     left.append(source[start : start + block, pl.ds(column, rows)])
                 product = jnp.dot(
@@ -141,16 +143,20 @@
         work(theirs, mine, False)
 
 
-def first_embed_kernel(keys, mine, theirs, w0, w1, partial):
+def first_embed_kernel(keys, mine, theirs, *refs):
+    *pieces, partial = refs
+
     def finish(at, total):
         partial[at : at + total.shape[0], :] = total
 
-    add_up(keys, mine, theirs, (w0, w1), finish)
-
-
-def last_embed_kernel(keys, mine, theirs, w0, w1, partial, own, other, bounds):
+    add_up(keys, mine, theirs, pieces, finish)
+
+
+def last_embed_kernel(keys, mine, theirs, *refs):
+    *pieces, partial, best, own, other, bounds = refs
     count = own.shape[0]
     bounds[...] = jnp.full(bounds.shape, -jnp.inf, F32)
+    bounds[2:3, :] = best[...]
 
     def finish(at, total):
         total = total + partial[at : at + total.shape[0], :]
@@ -163,7 +169,7 @@
         bounds[0:1, :] = jnp.maximum(bounds[0:1, :], top)
         bounds[1:2, :] = jnp.maximum(bounds[1:2, :], bottom)
 
-    add_up(keys, mine, theirs, (w0, w1), finish)
+    add_up(keys, mine, theirs, pieces, finish)
 
 
 def code_kernel(own, other, here, there, codes):
@@ -216,38 +222,24 @@
     in_column = cat(in_rows, *(move(in_rows, k) for k in (8, 16, 24)))
     here, there = half_columns(w_out, core), move(half_columns(w_out, 1 - core), 1)
     out_rows = jnp.where(core == 0, cat(here, there), cat(there, here))
-    out_pair = cat(out_rows, move(out_rows, 8))
     user_pair = cat(users[0], move(users[0], 2))
     user_plane = cat(user_pair, move(user_pair, 4))
-
     features = items[0]
     ordered = call(
         order_kernel, shape((2 * count, d_in), BF16), [VMEM, VMEM], 4 * count * d_in * d_in
     )(features, move(features, 1))
-    in_column, out_pair, user_plane, ordered, resident = lax.optimization_barrier(
-        (in_column, out_pair, user_plane, ordered, res_codes[0])
-    )
+    in_column, out_rows, user_plane, ordered, resident = lax.optimization_barrier(
+        (in_column, out_rows, user_plane, ordered, res_codes[0])
+    )
+
     in_pieces = [in_column] + [move(in_column, k) for k in (2, 4, 6)]
-    out_column = cat(out_pair, move(out_pair, 16))
-    near_users = cat(user_plane, move(user_plane, 8))
+    out_far = move(out_rows, 16)
+    out_column = cat(out_rows, move(out_rows, 8), out_far, move(out_far, 8))
     codes = resident.astype(BF16)
     codes_other = move(codes, 1)
-
-    *in_pieces, out_column, near_users = lax.optimization_barrier(
-        (*in_pieces, out_column, near_users)
-    )
-    out_pieces = [out_column] + [move(out_column, k) for k in (2, 4, 6)]
-    far_users = move(near_users, 16)
-    last_pieces, far_users = lax.optimization_barrier((out_pieces[2:], far_users))
-    ranges = (range_idx[None, :], range_lo, range_step)
-    members = near_users.shape[0]
-    score_flops = 4 * members * count * users.shape[2]
-    near_best = call(
-        near_score_kernel,
-        shape((1, members), F32),
-        [VMEM, SMEM, SMEM] + [VMEM] * 3,
-        score_flops,
-    )(*ranges, codes, codes_other, near_users)
+    *in_pieces, out_column, user_plane = lax.optimization_barrier(
+        (*in_pieces, out_column, user_plane)
+    )
 
     hidden = call(
         hidden_kernel,
@@ -255,34 +247,50 @@
         [VMEM] * 5,
         4 * count * d_in * wide,
     )(ordered, *in_pieces)
+    out_x, out_y = move(out_column, 2), move(out_column, 4)
+    user_near, user_far = move(user_plane, 8), move(user_plane, 16)
+    out_x, out_y, user_near, user_far, hidden = lax.optimization_barrier(
+        (out_x, out_y, user_near, user_far, hidden)
+    )
+    half = out_column.shape[0] // 2
+    out_low, out_high = move(out_y[:half], 2), move(out_x[half:], 4)
+    user_last = move(user_far, 8)
+
+    ranges = (range_idx[None, :], range_lo, range_step)
+    members = 2 * user_plane.shape[0]
+    score_flops = 4 * members * count * users.shape[2]
+    near_best = call(
+        near_score_kernel,
+        shape((1, members), F32),
+        [VMEM, SMEM, SMEM] + [VMEM] * 4,
+        score_flops,
+    )(*ranges, codes, codes_other, user_plane, user_near)
     hidden_other = move(hidden, 1)
-
     best = call(
         far_score_kernel,
         shape((1, 2 * members), F32),
-        [VMEM, SMEM, SMEM] + [VMEM] * 4,
+        [VMEM, SMEM, SMEM] + [VMEM] * 5,
         score_flops,
-    )(*ranges, codes, codes_other, far_users, near_best)
+    )(*ranges, codes, codes_other, user_far, user_last, near_best)
 
     partial = call(
-        functools.partial(first_embed_kernel, keys[:2]),
+        functools.partial(first_embed_kernel, keys[:3]),
         shape((2 * count, width), F32),
-        [VMEM] * 4,
-        4 * count * wide * width,
-    )(hidden, hidden_other, *out_pieces[:2])
-    own, other, bounds = call(
-        functools.partial(last_embed_kernel, keys[2:]),
+        [VMEM] * 5,
+        6 * count * wide * width,
+    )(hidden, hidden_other, out_column, out_x, out_y)
+    own, other, merged = call(
+        functools.partial(last_embed_kernel, (keys[3][:2], keys[3][2:])),
         (
             shape((count, width), F32),
             shape((count, width), F32),
-            shape((2, width), F32),
+            shape((3, width), F32),
         ),
-        [VMEM] * 5,
-        4 * count * wide * width,
-    )(hidden, hidden_other, *last_pieces, partial)
+        [VMEM] * 6,
+        2 * count * wide * width,
+    )(hidden, hidden_other, out_low, out_high, partial, best)
     received = move(other, 1)
 
-    merged = cat(bounds, best)
     for k in (2, 4, 8, 16):
         merged = jnp.maximum(merged, move(merged, k))
     bounds = merged[:2]

time: 90.8 us -> 82.2 us (0.905)
  waiting for transfers between devices: 48.2 us -> 41.4 us
  starting transfers between devices: 28 us -> 26.2 us
    ppermute x26 -> x29, waiting for transfers between devices: 48.2 us -> 41.4 us  [swap(): return lax.ppermute(x, axis, [(i, i ^ k) for i in range(n)])]
    ppermute x26 -> x29, starting transfers between devices: 28 us -> 26.2 us  [swap(): return lax.ppermute(x, axis, [(i, i ^ k) for i in range(n)])]
  transfers between devices with their start and end apart: 26 -> 29, of which waited for: 12 -> 16; matrix products, arithmetic and copies ran while one was open for 5% -> 5% of each run, Pallas kernels for 6% -> 8%
where the time goes in v3:
time: 82.2 us; the launch traced here: 81.9 us
  waiting for transfers between devices  41.4 us (50%)
  starting transfers between devices  26.2 us (32%)
  Pallas kernels  8.99 us (11%)
  local copies, waits for them, and re-layouts  2.35 us (3%)
  other arithmetic  2.02 us (2%)
  between operations  0.91 us (1%)
    ppermute x29, waiting for transfers between devices, swap(): return lax.ppermute(x, axis, [(i, i ^ k) for i in range(n)])  41.4 us
    ppermute x29, starting transfers between devices, swap(): return lax.ppermute(x, axis, [(i, i ^ k) for i in range(n)])  26.2 us
    pallas_call x1, Pallas kernels, by_permutes(): call(functools.partial(first_embed_kernel, keys[:3]), shape((2 * count, w...  1.87 us
    concatenate x4, other arithmetic, by_permutes(): cat = lambda *parts: jnp.concatenate(parts, axis=0)  1.74 us
  transfers between devices with their start and end apart: 29, of which 16 were waited for; matrix products, arithmetic and copies ran while one was open for 5% of the time, Pallas kernels for 8%

profile of v3, /device:TPU:0, one launch (start us, length us, event | category | flops | bytes accessed | tf_op | source)
XLA Modules:
  0.0 81.9 jit_solution(2619993533745303864)
XLA Ops:
  0.6 3.0 %collective-permute-start.5 = (bf16[32,1024]{1,0:T(8,128)(2,1)}, bf16[32,1024]{1,0:T(8,128)(2,1)S(1)}, u32[]{:S(2)}, u32[]{:S(2)}) collective-permute-start(bf16[32,1024]{1,0:T(8,128)(2,1)} %bitcast.11), channel_id=1, source_target_pairs={{0,2},{1,3},{2,0},{3,1},{4,6},{5,7},{6,4},{7,5},{8,10},{9,11},{10,... | collective-permute-start | bytes 196616 | tf_op jit(solution)/shard_map/ppermute | solution.py:18
  6.0 3.7 %collective-permute-start.3 = (bf16[32,1024]{1,0:T(8,128)(2,1)S(1)}, bf16[32,1024]{1,0:T(8,128)(2,1)S(1)}, u32[]{:S(2)}, u32[]{:S(2)}) collective-permute-start(bf16[32,1024]{1,0:T(8,128)(2,1)S(1)} %pad_maximum_fusion.3), channel_id=1, source_target_pairs={{0,24},{1,25},{2,26},{3,27},{4,28},{5,29},{6,30},{7,31},{8,16},{9,... | collective-permute-start | bytes 196616 | tf_op jit(solution)/shard_map/ppermute | solution.py:18
  11.4 1.6 %collective-permute-start.6 = (bf16[64,1024]{1,0:T(8,128)(2,1)S(1)}, bf16[64,1024]{1,0:T(8,128)(2,1)S(1)}, u32[]{:S(2)}, u32[]{:S(2)}) collective-permute-start(bf16[64,1024]{1,0:T(8,128)(2,1)S(1)} %pad_maximum_fusion.2), channel_id=1, source_target_pairs={{0,4},{1,5},{2,6},{3,7},{4,0},{5,1},{6,2},{7,3},{8,12},{9,13},{10,... | collective-permute-start | bytes 393224 | tf_op jit(solution)/shard_map/ppermute | solution.py:18
  13.0 1.5 %collective-permute-done.1 = bf16[32,1024]{1,0:T(8,128)(2,1)S(1)} collective-permute-done((bf16[32,1024]{1,0:T(8,128)(2,1)S(1)}, bf16[32,1024]{1,0:T(8,128)(2,1)S(1)}, u32[]{:S(2)}, u32[]{:S(2)}) %collective-permute-start.1) | collective-permute-done | bytes 65568 | tf_op jit(solution)/shard_map/ppermute | solution.py:18
  18.2 2.4 %collective-permute-start.12 = (bf16[128,512]{1,0:T(8,128)(2,1)S(1)}, bf16[128,512]{1,0:T(8,128)(2,1)S(1)}, u32[]{:S(2)}, u32[]{:S(2)}) collective-permute-start(bf16[128,512]{1,0:T(8,128)(2,1)S(1)} %maximum_select_fusion), channel_id=1, source_target_pairs={{0,16},{1,17},{2,18},{3,19},{4,20},{5,21},{6,22},{7,23},{8,24},{9,... | collective-permute-start | bytes 393224 | tf_op jit(solution)/shard_map/ppermute | solution.py:18
  20.6 1.5 %collective-permute-start.10 = (bf16[128,1024]{1,0:T(8,128)(2,1)S(1)}, bf16[128,1024]{1,0:T(8,128)(2,1)S(1)}, u32[]{:S(2)}, u32[]{:S(2)}) collective-permute-start(bf16[128,1024]{1,0:T(8,128)(2,1)S(1)} %constant_dynamic-update-slice_fusion.w0), channel_id=1, source_target_pairs={{0,6},{1,7},{2,4},{3,5},{4,2},{5,3},{6,0},{7,1},{8,14},{9,15},{10,... | collective-permute-start | bytes 786440 | tf_op jit(solution)/shard_map/ppermute | solution.py:18
  22.6 1.5 %collective-permute-start.8 = (bf16[128,1024]{1,0:T(8,128)(2,1)S(1)}, bf16[128,1024]{1,0:T(8,128)(2,1)S(1)}, u32[]{:S(2)}, u32[]{:S(2)}) collective-permute-start(bf16[128,1024]{1,0:T(8,128)(2,1)S(1)} %constant_dynamic-update-slice_fusion.w0), channel_id=1, source_target_pairs={{0,2},{1,3},{2,0},{3,1},{4,6},{5,7},{6,4},{7,5},{8,10},{9,11},{10,... | collective-permute-start | bytes 786440 | tf_op jit(solution)/shard_map/ppermute | solution.py:18
  24.1 1.7 %collective-permute-start.11 = (bf16[128,512]{1,0:T(8,128)(2,1)S(1)}, bf16[128,512]{1,0:T(8,128)(2,1)S(1)}, u32[]{:S(2)}, u32[]{:S(2)}) collective-permute-start(bf16[128,512]{1,0:T(8,128)(2,1)S(1)} %maximum_select_fusion), channel_id=1, source_target_pairs={{0,8},{1,9},{2,10},{3,11},{4,12},{5,13},{6,14},{7,15},{8,0},{9,1},... | collective-permute-start | bytes 393224 | tf_op jit(solution)/shard_map/ppermute | solution.py:18
  26.5 3.7 %collective-permute-done.11 = bf16[128,512]{1,0:T(8,128)(2,1)S(1)} collective-permute-done((bf16[128,512]{1,0:T(8,128)(2,1)S(1)}, bf16[128,512]{1,0:T(8,128)(2,1)S(1)}, u32[]{:S(2)}, u32[]{:S(2)}) %collective-permute-start.11) | collective-permute-done | bytes 131104 | tf_op jit(solution)/shard_map/ppermute | solution.py:18
  30.2 1.4 %collective-permute-done.13 = bf16[128,512]{1,0:T(8,128)(2,1)S(1)} collective-permute-done((bf16[128,512]{1,0:T(8,128)(2,1)S(1)}, bf16[128,512]{1,0:T(8,128)(2,1)S(1)}, u32[]{:S(2)}, u32[]{:S(2)}) %collective-permute-start.13) | collective-permute-done | bytes 131104 | tf_op jit(solution)/shard_map/ppermute | solution.py:18
  31.6 2.4 %collective-permute-done.9.w2 = bf16[128,1024]{1,0:T(8,128)(2,1)S(1)} collective-permute-done((bf16[128,1024]{1,0:T(8,128)(2,1)S(1)}, bf16[128,1024]{1,0:T(8,128)(2,1)S(1)}, u32[]{:S(2)}, u32[]{:S(2)}) %collective-permute-start.9) | collective-permute-done | bytes 262176 | tf_op jit(solution)/shard_map/ppermute | solution.py:18
  36.6 1.6 %collective-permute-start.16 = (bf16[128,1024]{1,0:T(8,128)(2,1)S(1)}, bf16[128,1024]{1,0:T(8,128)(2,1)S(1)}, u32[]{:S(2)}, u32[]{:S(2)}) collective-permute-start(bf16[128,1024]{1,0:T(8,128)(2,1)S(1)} %pad_maximum_fusion.1.u0), channel_id=1, source_target_pairs={{0,8},{1,9},{2,10},{3,11},{4,12},{5,13},{6,14},{7,15},{8,0},{9,1},... | collective-permute-start | bytes 786440 | tf_op jit(solution)/shard_map/ppermute | solution.py:18
  38.2 1.3 %shard_map.96.mine = bf16[1024,1024]{1,0:T(8,128)(2,1)S(1)} custom-call(bf16[1024,512]{1,0:T(8,128)(2,1)S(1)} %shard_map.95.features, bf16[128,1024]{1,0:T(8,128)(2,1)S(1)} %constant_dynamic-update-slice_fusion.w0, bf16[128,1024]{1,0:T(8,128)(2,1)S(1)} %collective-permute-done.8.w1, bf16[128,1024]{1,0:T(8,128)(2,1)S(1)} %collective-permute-done.9.w2, ...), custom_call_target="tpu_custom_call" | custom-call | flops 1073741824 | bytes 2097152 | tf_op jit(solution)/shard_map/pallas_call | solution.py:244
  39.6 10.7 %collective-permute-done.17.u0 = bf16[128,1024]{1,0:T(8,128)(2,1)S(1)} collective-permute-done((bf16[128,1024]{1,0:T(8,128)(2,1)S(1)}, bf16[128,1024]{1,0:T(8,128)(2,1)S(1)}, u32[]{:S(2)}, u32[]{:S(2)}) %collective-permute-start.17) | collective-permute-done | bytes 262176 | tf_op jit(solution)/shard_map/ppermute | solution.py:18
  51.6 1.6 %collective-permute-start.19 = (bf16[256,512]{1,0:T(8,128)(2,1)S(1)}, bf16[256,512]{1,0:T(8,128)(2,1)S(1)}, u32[]{:S(2)}, u32[]{:S(2)}) collective-permute-start(bf16[256,512]{1,0:T(8,128)(2,1)S(1)} %slice.12), channel_id=1, source_target_pairs={{0,2},{1,3},{2,0},{3,1},{4,6},{5,7},{6,4},{7,5},{8,10},{9,11},{10,... | collective-permute-start | bytes 786440 | tf_op jit(solution)/shard_map/ppermute | solution.py:18
  53.3 2.7 %collective-permute-done.21.other = bf16[512,1024]{1,0:T(8,128)(2,1)S(1)} collective-permute-done((bf16[512,1024]{1,0:T(8,128)(2,1)S(1)}, bf16[512,1024]{1,0:T(8,128)(2,1)S(1)}, u32[]{:S(2)}, u32[]{:S(2)}) %collective-permute-start.21) | collective-permute-done | bytes 1048608 | tf_op jit(solution)/shard_map/ppermute | solution.py:18
  56.0 1.5 %shard_map.98.near = f32[1,256]{1,0:T(1,128)S(1)} custom-call(s32[1,1024]{1,0:T(1,128)S(1)} %bitcast.7, f32[4]{0:T(128)S(1)} %copy-done.2, f32[4]{0:T(128)S(1)} %copy-done.3, bf16[512,1024]{1,0:T(8,128)(2,1)S(1)} %convert_element_type.3.own, bf16[512,1024]{1,0:T(8,128)(2,1)S(1)} %collective-permute-done.21.other, ...), custom_call_target="tpu_custom_call" | custom-call | flops 536870912 | bytes 1024 | tf_op jit(solution)/shard_map/pallas_call | solution.py:262
  57.5 2.0 %collective-permute-done.22.u1 = bf16[128,1024]{1,0:T(8,128)(2,1)S(1)} collective-permute-done((bf16[128,1024]{1,0:T(8,128)(2,1)S(1)}, bf16[128,1024]{1,0:T(8,128)(2,1)S(1)}, u32[]{:S(2)}, u32[]{:S(2)}) %collective-permute-start.22) | collective-permute-done | bytes 262176 | tf_op jit(solution)/shard_map/ppermute | solution.py:18
  59.5 1.6 %shard_map.99.refs_3_ = f32[1,512]{1,0:T(1,128)S(1)} custom-call(s32[1,1024]{1,0:T(1,128)S(1)} %bitcast.8, f32[4]{0:T(128)S(1)} %copy-done.2, f32[4]{0:T(128)S(1)} %copy-done.3, bf16[512,1024]{1,0:T(8,128)(2,1)S(1)} %convert_element_type.3.own, bf16[512,1024]{1,0:T(8,128)(2,1)S(1)} %collective-permute-done.21.other, ...), custom_call_target="tpu_custom_call" | custom-call | flops 536870912 | bytes 2048 | tf_op jit(solution)/shard_map/pallas_call | solution.py:269
  61.1 1.9 %shard_map.97.refs_2_ = f32[1024,512]{1,0:T(8,128)S(1)} custom-call(bf16[1024,1024]{1,0:T(8,128)(2,1)S(1)} %shard_map.96.mine, bf16[1024,1024]{1,0:T(8,128)(2,1)S(1)} %collective-permute-done.18.theirs, bf16[512,512]{1,0:T(8,128)(2,1)S(1)} %pad_maximum_fusion.refs_0_, bf16[512,512]{1,0:T(8,128)(2,1)S(1)} %collective-permute-done.14.refs_1_, ...), custom_call_target="tpu_custom_call" | custom-call | flops 1610612736 | bytes 2097152 | tf_op jit(solution)/shard_map/pallas_call | solution.py:276
  64.2 3.4 %collective-permute-done.24 = f32[3,512]{1,0:T(4,128)S(1)} collective-permute-done((f32[3,512]{1,0:T(4,128)S(1)}, f32[3,512]{1,0:T(4,128)S(1)}, u32[]{:S(2)}, u32[]{:S(2)}) %collective-permute-start.24) | collective-permute-done | bytes 6176 | tf_op jit(solution)/shard_map/ppermute | solution.py:18
  68.0 3.3 %collective-permute-done.25 = f32[3,512]{1,0:T(4,128)S(1)} collective-permute-done((f32[3,512]{1,0:T(4,128)S(1)}, f32[3,512]{1,0:T(4,128)S(1)}, u32[]{:S(2)}, u32[]{:S(2)}) %collective-permute-start.25) | collective-permute-done | bytes 6176 | tf_op jit(solution)/shard_map/ppermute | solution.py:18
  71.5 3.4 %collective-permute-done.26 = f32[3,512]{1,0:T(4,128)S(1)} collective-permute-done((f32[3,512]{1,0:T(4,128)S(1)}, f32[3,512]{1,0:T(4,128)S(1)}, u32[]{:S(2)}, u32[]{:S(2)}) %collective-permute-start.26) | collective-permute-done | bytes 6176 | tf_op jit(solution)/shard_map/ppermute | solution.py:18
  75.9 3.6 %collective-permute-done.27 = f32[3,512]{1,0:T(4,128)S(1)} collective-permute-done((f32[3,512]{1,0:T(4,128)S(1)}, f32[3,512]{1,0:T(4,128)S(1)}, u32[]{:S(2)}, u32[]{:S(2)}) %collective-permute-start.27) | collective-permute-done | bytes 6176 | tf_op jit(solution)/shard_map/ppermute | solution.py:18
  (72 shorter events, 18.0 us)
Async XLA Ops:
  0.6 9.1 %collective-permute-start.5 = (bf16[32,1024]{1,0:T(8,128)(2,1)}, bf16[32,1024]{1,0:T(8,128)(2,1)S(1)}, u32[]{:S(2)}, u32[]{:S(2)}) collective-permute-start(bf16[32,1024]{1,0:T(8,128)(2,1)} %bitcast.11), channel_id=1, source_target_pairs={{0,2},{1,3},{2,0},{3,1},{4,6},{5,7},{6,4},{7,5},{8,10},{9,11},{10,... | collective-permute-start | bytes 196616 | tf_op jit(solution)/shard_map/ppermute | solution.py:18
  5.4 5.9 %collective-permute-start.4 = (bf16[64,512]{1,0:T(8,128)(2,1)S(1)}, bf16[64,512]{1,0:T(8,128)(2,1)S(1)}, u32[]{:S(2)}, u32[]{:S(2)}) collective-permute-start(bf16[64,512]{1,0:T(8,128)(2,1)S(1)} %get-tuple-element.43), channel_id=1, source_target_pairs={{0,1},{1,0},{2,3},{3,2},{4,5},{5,4},{6,7},{7,6},{8,9},{9,8},{10,11... | collective-permute-start | bytes 196616 | tf_op jit(solution)/shard_map/ppermute | solution.py:18
  5.9 11.5 %collective-permute-start.7 = (bf16[512,512]{1,0:T(8,128)(2,1)}, bf16[512,512]{1,0:T(8,128)(2,1)S(1)}, u32[]{:S(2)}, u32[]{:S(2)}) collective-permute-start(bf16[512,512]{1,0:T(8,128)(2,1)} %bitcast.5), channel_id=1, source_target_pairs={{0,1},{1,0},{2,3},{3,2},{4,5},{5,4},{6,7},{7,6},{8,9},{9,8},{10,11... | collective-permute-start | bytes 1572872 | tf_op jit(solution)/shard_map/ppermute | solution.py:18
  6.0 9.7 %collective-permute-start.3 = (bf16[32,1024]{1,0:T(8,128)(2,1)S(1)}, bf16[32,1024]{1,0:T(8,128)(2,1)S(1)}, u32[]{:S(2)}, u32[]{:S(2)}) collective-permute-start(bf16[32,1024]{1,0:T(8,128)(2,1)S(1)} %pad_maximum_fusion.3), channel_id=1, source_target_pairs={{0,24},{1,25},{2,26},{3,27},{4,28},{5,29},{6,30},{7,31},{8,16},{9,... | collective-permute-start | bytes 196616 | tf_op jit(solution)/shard_map/ppermute | solution.py:18
  9.7 6.1 %collective-permute-start.2 = (bf16[32,1024]{1,0:T(8,128)(2,1)S(1)}, bf16[32,1024]{1,0:T(8,128)(2,1)S(1)}, u32[]{:S(2)}, u32[]{:S(2)}) collective-permute-start(bf16[32,1024]{1,0:T(8,128)(2,1)S(1)} %pad_maximum_fusion.3), channel_id=1, source_target_pairs={{0,16},{1,17},{2,18},{3,19},{4,20},{5,21},{6,22},{7,23},{8,24},{9,... | collective-permute-start | bytes 196616 | tf_op jit(solution)/shard_map/ppermute | solution.py:18
  9.7 4.8 %collective-permute-start.1 = (bf16[32,1024]{1,0:T(8,128)(2,1)S(1)}, bf16[32,1024]{1,0:T(8,128)(2,1)S(1)}, u32[]{:S(2)}, u32[]{:S(2)}) collective-permute-start(bf16[32,1024]{1,0:T(8,128)(2,1)S(1)} %pad_maximum_fusion.3), channel_id=1, source_target_pairs={{0,8},{1,9},{2,10},{3,11},{4,12},{5,13},{6,14},{7,15},{8,0},{9,1},... | collective-permute-start | bytes 196616 | tf_op jit(solution)/shard_map/ppermute | solution.py:18
  11.4 5.2 %collective-permute-start.6 = (bf16[64,1024]{1,0:T(8,128)(2,1)S(1)}, bf16[64,1024]{1,0:T(8,128)(2,1)S(1)}, u32[]{:S(2)}, u32[]{:S(2)}) collective-permute-start(bf16[64,1024]{1,0:T(8,128)(2,1)S(1)} %pad_maximum_fusion.2), channel_id=1, source_target_pairs={{0,4},{1,5},{2,6},{3,7},{4,0},{5,1},{6,2},{7,3},{8,12},{9,13},{10,... | collective-permute-start | bytes 393224 | tf_op jit(solution)/shard_map/ppermute | solution.py:18
  18.2 8.2 %collective-permute-start.12 = (bf16[128,512]{1,0:T(8,128)(2,1)S(1)}, bf16[128,512]{1,0:T(8,128)(2,1)S(1)}, u32[]{:S(2)}, u32[]{:S(2)}) collective-permute-start(bf16[128,512]{1,0:T(8,128)(2,1)S(1)} %maximum_select_fusion), channel_id=1, source_target_pairs={{0,16},{1,17},{2,18},{3,19},{4,20},{5,21},{6,22},{7,23},{8,24},{9,... | collective-permute-start | bytes 393224 | tf_op jit(solution)/shard_map/ppermute | solution.py:18
  20.6 11.0 %collective-permute-start.10 = (bf16[128,1024]{1,0:T(8,128)(2,1)S(1)}, bf16[128,1024]{1,0:T(8,128)(2,1)S(1)}, u32[]{:S(2)}, u32[]{:S(2)}) collective-permute-start(bf16[128,1024]{1,0:T(8,128)(2,1)S(1)} %constant_dynamic-update-slice_fusion.w0), channel_id=1, source_target_pairs={{0,6},{1,7},{2,4},{3,5},{4,2},{5,3},{6,0},{7,1},{8,14},{9,15},{10,... | collective-permute-start | bytes 786440 | tf_op jit(solution)/shard_map/ppermute | solution.py:18
  22.1 12.0 %collective-permute-start.9 = (bf16[128,1024]{1,0:T(8,128)(2,1)S(1)}, bf16[128,1024]{1,0:T(8,128)(2,1)S(1)}, u32[]{:S(2)}, u32[]{:S(2)}) collective-permute-start(bf16[128,1024]{1,0:T(8,128)(2,1)S(1)} %constant_dynamic-update-slice_fusion.w0), channel_id=1, source_target_pairs={{0,4},{1,5},{2,6},{3,7},{4,0},{5,1},{6,2},{7,3},{8,12},{9,13},{10,... | collective-permute-start | bytes 786440 | tf_op jit(solution)/shard_map/ppermute | solution.py:18
  22.6 11.6 %collective-permute-start.8 = (bf16[128,1024]{1,0:T(8,128)(2,1)S(1)}, bf16[128,1024]{1,0:T(8,128)(2,1)S(1)}, u32[]{:S(2)}, u32[]{:S(2)}) collective-permute-start(bf16[128,1024]{1,0:T(8,128)(2,1)S(1)} %constant_dynamic-update-slice_fusion.w0), channel_id=1, source_target_pairs={{0,2},{1,3},{2,0},{3,1},{4,6},{5,7},{6,4},{7,5},{8,10},{9,11},{10,... | collective-permute-start | bytes 786440 | tf_op jit(solution)/shard_map/ppermute | solution.py:18
  24.1 6.1 %collective-permute-start.11 = (bf16[128,512]{1,0:T(8,128)(2,1)S(1)}, bf16[128,512]{1,0:T(8,128)(2,1)S(1)}, u32[]{:S(2)}, u32[]{:S(2)}) collective-permute-start(bf16[128,512]{1,0:T(8,128)(2,1)S(1)} %maximum_select_fusion), channel_id=1, source_target_pairs={{0,8},{1,9},{2,10},{3,11},{4,12},{5,13},{6,14},{7,15},{8,0},{9,1},... | collective-permute-start | bytes 393224 | tf_op jit(solution)/shard_map/ppermute | solution.py:18
  26.4 5.2 %collective-permute-start.13 = (bf16[128,512]{1,0:T(8,128)(2,1)S(1)}, bf16[128,512]{1,0:T(8,128)(2,1)S(1)}, u32[]{:S(2)}, u32[]{:S(2)}) collective-permute-start(bf16[128,512]{1,0:T(8,128)(2,1)S(1)} %collective-permute-done.12), channel_id=1, source_target_pairs={{0,8},{1,9},{2,10},{3,11},{4,12},{5,13},{6,14},{7,15},{8,0},{9,1},... | collective-permute-start | bytes 393224 | tf_op jit(solution)/shard_map/ppermute | solution.py:18
  34.1 16.1 %collective-permute-start.15 = (bf16[512,512]{1,0:T(8,128)(2,1)S(1)}, bf16[512,512]{1,0:T(8,128)(2,1)S(1)}, u32[]{:S(2)}, u32[]{:S(2)}) collective-permute-start(bf16[512,512]{1,0:T(8,128)(2,1)S(1)} %pad_maximum_fusion.refs_0_), channel_id=1, source_target_pairs={{0,4},{1,5},{2,6},{3,7},{4,0},{5,1},{6,2},{7,3},{8,12},{9,13},{10,... | collective-permute-start | bytes 1572872 | tf_op jit(solution)/shard_map/ppermute | solution.py:18
  34.9 15.4 %collective-permute-start.14 = (bf16[512,512]{1,0:T(8,128)(2,1)S(1)}, bf16[512,512]{1,0:T(8,128)(2,1)S(1)}, u32[]{:S(2)}, u32[]{:S(2)}) collective-permute-start(bf16[512,512]{1,0:T(8,128)(2,1)S(1)} %pad_maximum_fusion.refs_0_), channel_id=1, source_target_pairs={{0,2},{1,3},{2,0},{3,1},{4,6},{5,7},{6,4},{7,5},{8,10},{9,11},{10,... | collective-permute-start | bytes 1572872 | tf_op jit(solution)/shard_map/ppermute | solution.py:18
  36.1 14.2 %collective-permute-start.17 = (bf16[128,1024]{1,0:T(8,128)(2,1)S(1)}, bf16[128,1024]{1,0:T(8,128)(2,1)S(1)}, u32[]{:S(2)}, u32[]{:S(2)}) collective-permute-start(bf16[128,1024]{1,0:T(8,128)(2,1)S(1)} %pad_maximum_fusion.1.u0), channel_id=1, source_target_pairs={{0,16},{1,17},{2,18},{3,19},{4,20},{5,21},{6,22},{7,23},{8,24},{9,... | collective-permute-start | bytes 786440 | tf_op jit(solution)/shard_map/ppermute | solution.py:18
  36.6 13.7 %collective-permute-start.16 = (bf16[128,1024]{1,0:T(8,128)(2,1)S(1)}, bf16[128,1024]{1,0:T(8,128)(2,1)S(1)}, u32[]{:S(2)}, u32[]{:S(2)}) collective-permute-start(bf16[128,1024]{1,0:T(8,128)(2,1)S(1)} %pad_maximum_fusion.1.u0), channel_id=1, source_target_pairs={{0,8},{1,9},{2,10},{3,11},{4,12},{5,13},{6,14},{7,15},{8,0},{9,1},... | collective-permute-start | bytes 786440 | tf_op jit(solution)/shard_map/ppermute | solution.py:18
  50.3 10.8 %collective-permute-start.18 = (bf16[1024,1024]{1,0:T(8,128)(2,1)S(1)}, bf16[1024,1024]{1,0:T(8,128)(2,1)S(1)}, u32[]{:S(2)}, u32[]{:S(2)}) collective-permute-start(bf16[1024,1024]{1,0:T(8,128)(2,1)S(1)} %shard_map.96.mine), channel_id=1, source_target_pairs={{0,1},{1,0},{2,3},{3,2},{4,5},{5,4},{6,7},{7,6},{8,9},{9,8},{10,11... | collective-permute-start | bytes 6291464 | tf_op jit(solution)/shard_map/ppermute | solution.py:18
  50.6 5.4 %collective-permute-start.21 = (bf16[512,1024]{1,0:T(8,128)(2,1)S(1)}, bf16[512,1024]{1,0:T(8,128)(2,1)S(1)}, u32[]{:S(2)}, u32[]{:S(2)}) collective-permute-start(bf16[512,1024]{1,0:T(8,128)(2,1)S(1)} %convert_element_type.3.own), channel_id=1, source_target_pairs={{0,1},{1,0},{2,3},{3,2},{4,5},{5,4},{6,7},{7,6},{8,9},{9,8},{10,11... | collective-permute-start | bytes 3145736 | tf_op jit(solution)/shard_map/ppermute | solution.py:18
  51.2 8.3 %collective-permute-start.22 = (bf16[128,1024]{1,0:T(8,128)(2,1)S(1)}, bf16[128,1024]{1,0:T(8,128)(2,1)S(1)}, u32[]{:S(2)}, u32[]{:S(2)}) collective-permute-start(bf16[128,1024]{1,0:T(8,128)(2,1)S(1)} %collective-permute-done.17.u0), channel_id=1, source_target_pairs={{0,8},{1,9},{2,10},{3,11},{4,12},{5,13},{6,14},{7,15},{8,0},{9,1},... | collective-permute-start | bytes 786440 | tf_op jit(solution)/shard_map/ppermute | solution.py:18
  51.2 11.7 %collective-permute-start.20 = (bf16[256,512]{1,0:T(8,128)(2,1)S(1)}, bf16[256,512]{1,0:T(8,128)(2,1)S(1)}, u32[]{:S(2)}, u32[]{:S(2)}) collective-permute-start(bf16[256,512]{1,0:T(8,128)(2,1)S(1)} %slice.13), channel_id=1, source_target_pairs={{0,4},{1,5},{2,6},{3,7},{4,0},{5,1},{6,2},{7,3},{8,12},{9,13},{10,... | collective-permute-start | bytes 786440 | tf_op jit(solution)/shard_map/ppermute | solution.py:18
  51.6 11.3 %collective-permute-start.19 = (bf16[256,512]{1,0:T(8,128)(2,1)S(1)}, bf16[256,512]{1,0:T(8,128)(2,1)S(1)}, u32[]{:S(2)}, u32[]{:S(2)}) collective-permute-start(bf16[256,512]{1,0:T(8,128)(2,1)S(1)} %slice.12), channel_id=1, source_target_pairs={{0,2},{1,3},{2,0},{3,1},{4,6},{5,7},{6,4},{7,5},{8,10},{9,11},{10,... | collective-permute-start | bytes 786440 | tf_op jit(solution)/shard_map/ppermute | solution.py:18
  63.8 16.9 %collective-permute-start.23 = (f32[512,512]{1,0:T(8,128)S(1)}, f32[512,512]{1,0:T(8,128)S(1)}, u32[]{:S(2)}, u32[]{:S(2)}) collective-permute-start(f32[512,512]{1,0:T(8,128)S(1)} %get-tuple-element.38), channel_id=1, source_target_pairs={{0,1},{1,0},{2,3},{3,2},{4,5},{5,4},{6,7},{7,6},{8,9},{9,8},{10,11... | collective-permute-start | bytes 3145736 | tf_op jit(solution)/shard_map/ppermute | solution.py:18
  74.9 4.5 %collective-permute-start.27 = (f32[3,512]{1,0:T(4,128)S(1)}, f32[3,512]{1,0:T(4,128)S(1)}, u32[]{:S(2)}, u32[]{:S(2)}) collective-permute-start(f32[3,512]{1,0:T(4,128)S(1)} %max.14), channel_id=1, source_target_pairs={{0,16},{1,17},{2,18},{3,19},{4,20},{5,21},{6,22},{7,23},{8,24},{9,... | collective-permute-start | bytes 18440 | tf_op jit(solution)/shard_map/ppermute | solution.py:18
  (10 other events, 98.9 us)

commit v4 on v3

--- a/solution.py
+++ b/solution.py
@@ -209,6 +209,12 @@
     return lax.dynamic_slice_in_dim(x, core * width, width, 1)
 
 
+def most(x, others):
+    for other in others:
+        x = jnp.maximum(x, other)
+    return x
+
+
 def by_permutes(n, n_rep, items, w_in, w_out, users, res_codes, range_idx, range_lo, range_step):
     move = lambda x, k: swap(x, "fsdp", n, k)
     cat = lambda *parts: jnp.concatenate(parts, axis=0)
@@ -266,6 +272,13 @@
         score_flops,
     )(*ranges, codes, codes_other, user_plane, user_near)
     hidden_other = move(hidden, 1)
+    partial = call(
+        functools.partial(first_embed_kernel, keys[:3]),
+        shape((2 * count, width), F32),
+        [VMEM] * 5,
+        6 * count * wide * width,
+    )(hidden, hidden_other, out_column, out_x, out_y)
+    near_best, partial = lax.optimization_barrier((near_best, partial))
     best = call(
         far_score_kernel,
         shape((1, 2 * members), F32),
@@ -273,12 +286,6 @@
         score_flops,
     )(*ranges, codes, codes_other, user_far, user_last, near_best)
 
-    partial = call(
-        functools.partial(first_embed_kernel, keys[:3]),
-        shape((2 * count, width), F32),
-        [VMEM] * 5,
-        6 * count * wide * width,
-    )(hidden, hidden_other, out_column, out_x, out_y)
     own, other, merged = call(
         functools.partial(last_embed_kernel, (keys[3][:2], keys[3][2:])),
         (
@@ -291,8 +298,8 @@
     )(hidden, hidden_other, out_low, out_high, partial, best)
     received = move(other, 1)
 
-    for k in (2, 4, 8, 16):
-        merged = jnp.maximum(merged, move(merged, k))
+    for keys in ((8, 16, 24), (2, 4, 6)):
+        merged = most(merged, [move(merged, k) for k in keys])
     bounds = merged[:2]
     if n_rep > 1:
         bounds = lax.pmax(bounds, "rep")

time: 82.2 us -> 78.4 us (0.954)
  waiting for transfers between devices: 41.4 us -> 31.5 us
  starting transfers between devices: 26.2 us -> 32.3 us
    ppermute x29 -> x31, waiting for transfers between devices: 41.4 us -> 31.5 us  [swap(): return lax.ppermute(x, axis, [(i, i ^ k) for i in range(n)])]
    ppermute x29 -> x31, starting transfers between devices: 26.2 us -> 32.3 us  [swap(): return lax.ppermute(x, axis, [(i, i ^ k) for i in range(n)])]
  transfers between devices with their start and end apart: 29 -> 31, of which waited for: 16 -> 16; matrix products, arithmetic and copies ran while one was open for 5% -> 5% of each run, Pallas kernels for 8% -> 8%
where the time goes in v4:
time: 78.4 us; the launch traced here: 78.1 us
  starting transfers between devices  32.3 us (41%)
  waiting for transfers between devices  31.5 us (40%)
  Pallas kernels  8.99 us (11%)
  local copies, waits for them, and re-layouts  2.41 us (3%)
  other arithmetic  2.03 us (3%)
  between operations  0.91 us (1%)
    ppermute x31, starting transfers between devices, swap(): return lax.ppermute(x, axis, [(i, i ^ k) for i in range(n)])  32.3 us
    ppermute x31, waiting for transfers between devices, swap(): return lax.ppermute(x, axis, [(i, i ^ k) for i in range(n)])  31.5 us
    pallas_call x1, Pallas kernels, by_permutes(): call(functools.partial(first_embed_kernel, keys[:3]), shape((2 * count, w...  1.88 us
    concatenate x4, other arithmetic, by_permutes(): cat = lambda *parts: jnp.concatenate(parts, axis=0)  1.74 us
    pallas_call x1, Pallas kernels, by_permutes(): call(far_score_kernel, shape((1, 2 * members), F32), [VMEM, SMEM, SMEM] +...  1.61 us
  transfers between devices with their start and end apart: 31, of which 16 were waited for; matrix products, arithmetic and copies ran while one was open for 5% of the time, Pallas kernels for 8%

profile of v4, /device:TPU:0, one launch (start us, length us, event | category | flops | bytes accessed | tf_op | source)
XLA Modules:
  0.0 78.1 jit_solution(11916151210673599390)
XLA Ops:
  3.0 2.9 %collective-permute-start.5 = (bf16[32,1024]{1,0:T(8,128)(2,1)}, bf16[32,1024]{1,0:T(8,128)(2,1)S(1)}, u32[]{:S(2)}, u32[]{:S(2)}) collective-permute-start(bf16[32,1024]{1,0:T(8,128)(2,1)} %bitcast.11), channel_id=1, source_target_pairs={{0,2},{1,3},{2,0},{3,1},{4,6},{5,7},{6,4},{7,5},{8,10},{9,11},{10,... | collective-permute-start | bytes 196616 | tf_op jit(solution)/shard_map/ppermute | solution.py:18
  6.0 1.6 %collective-permute-start.1 = (bf16[32,1024]{1,0:T(8,128)(2,1)S(1)}, bf16[32,1024]{1,0:T(8,128)(2,1)S(1)}, u32[]{:S(2)}, u32[]{:S(2)}) collective-permute-start(bf16[32,1024]{1,0:T(8,128)(2,1)S(1)} %pad_maximum_fusion.3), channel_id=1, source_target_pairs={{0,8},{1,9},{2,10},{3,11},{4,12},{5,13},{6,14},{7,15},{8,0},{9,1},... | collective-permute-start | bytes 196616 | tf_op jit(solution)/shard_map/ppermute | solution.py:18
  7.6 2.6 %collective-permute-start.2 = (bf16[32,1024]{1,0:T(8,128)(2,1)S(1)}, bf16[32,1024]{1,0:T(8,128)(2,1)S(1)}, u32[]{:S(2)}, u32[]{:S(2)}) collective-permute-start(bf16[32,1024]{1,0:T(8,128)(2,1)S(1)} %pad_maximum_fusion.3), channel_id=1, source_target_pairs={{0,16},{1,17},{2,18},{3,19},{4,20},{5,21},{6,22},{7,23},{8,24},{9,... | collective-permute-start | bytes 196616 | tf_op jit(solution)/shard_map/ppermute | solution.py:18
  10.2 2.3 %collective-permute-start.3 = (bf16[32,1024]{1,0:T(8,128)(2,1)S(1)}, bf16[32,1024]{1,0:T(8,128)(2,1)S(1)}, u32[]{:S(2)}, u32[]{:S(2)}) collective-permute-start(bf16[32,1024]{1,0:T(8,128)(2,1)S(1)} %pad_maximum_fusion.3), channel_id=1, source_target_pairs={{0,24},{1,25},{2,26},{3,27},{4,28},{5,29},{6,30},{7,31},{8,16},{9,... | collective-permute-start | bytes 196616 | tf_op jit(solution)/shard_map/ppermute | solution.py:18
  13.4 1.6 %collective-permute-start.6 = (bf16[64,1024]{1,0:T(8,128)(2,1)S(1)}, bf16[64,1024]{1,0:T(8,128)(2,1)S(1)}, u32[]{:S(2)}, u32[]{:S(2)}) collective-permute-start(bf16[64,1024]{1,0:T(8,128)(2,1)S(1)} %pad_maximum_fusion.2), channel_id=1, source_target_pairs={{0,4},{1,5},{2,6},{3,7},{4,0},{5,1},{6,2},{7,3},{8,12},{9,13},{10,... | collective-permute-start | bytes 393224 | tf_op jit(solution)/shard_map/ppermute | solution.py:18
  16.3 2.1 %collective-permute-done.6 = bf16[64,1024]{1,0:T(8,128)(2,1)S(1)} collective-permute-done((bf16[64,1024]{1,0:T(8,128)(2,1)S(1)}, bf16[64,1024]{1,0:T(8,128)(2,1)S(1)}, u32[]{:S(2)}, u32[]{:S(2)}) %collective-permute-start.6) | collective-permute-done | bytes 131104 | tf_op jit(solution)/shard_map/ppermute | solution.py:18
  20.3 2.4 %collective-permute-start.10 = (bf16[128,1024]{1,0:T(8,128)(2,1)S(1)}, bf16[128,1024]{1,0:T(8,128)(2,1)S(1)}, u32[]{:S(2)}, u32[]{:S(2)}) collective-permute-start(bf16[128,1024]{1,0:T(8,128)(2,1)S(1)} %constant_dynamic-update-slice_fusion.w0), channel_id=1, source_target_pairs={{0,6},{1,7},{2,4},{3,5},{4,2},{5,3},{6,0},{7,1},{8,14},{9,15},{10,... | collective-permute-start | bytes 786440 | tf_op jit(solution)/shard_map/ppermute | solution.py:18
  23.7 2.1 %collective-permute-start.11 = (bf16[128,512]{1,0:T(8,128)(2,1)S(1)}, bf16[128,512]{1,0:T(8,128)(2,1)S(1)}, u32[]{:S(2)}, u32[]{:S(2)}) collective-permute-start(bf16[128,512]{1,0:T(8,128)(2,1)S(1)} %maximum_select_fusion), channel_id=1, source_target_pairs={{0,8},{1,9},{2,10},{3,11},{4,12},{5,13},{6,14},{7,15},{8,0},{9,1},... | collective-permute-start | bytes 393224 | tf_op jit(solution)/shard_map/ppermute | solution.py:18
  27.2 2.8 %collective-permute-done.11 = bf16[128,512]{1,0:T(8,128)(2,1)S(1)} collective-permute-done((bf16[128,512]{1,0:T(8,128)(2,1)S(1)}, bf16[128,512]{1,0:T(8,128)(2,1)S(1)}, u32[]{:S(2)}, u32[]{:S(2)}) %collective-permute-start.11) | collective-permute-done | bytes 131104 | tf_op jit(solution)/shard_map/ppermute | solution.py:18
  29.9 2.4 %collective-permute-done.13 = bf16[128,512]{1,0:T(8,128)(2,1)S(1)} collective-permute-done((bf16[128,512]{1,0:T(8,128)(2,1)S(1)}, bf16[128,512]{1,0:T(8,128)(2,1)S(1)}, u32[]{:S(2)}, u32[]{:S(2)}) %collective-permute-start.13) | collective-permute-done | bytes 131104 | tf_op jit(solution)/shard_map/ppermute | solution.py:18
  32.3 1.9 %collective-permute-done.8.w1 = bf16[128,1024]{1,0:T(8,128)(2,1)S(1)} collective-permute-done((bf16[128,1024]{1,0:T(8,128)(2,1)S(1)}, bf16[128,1024]{1,0:T(8,128)(2,1)S(1)}, u32[]{:S(2)}, u32[]{:S(2)}) %collective-permute-start.8) | collective-permute-done | bytes 262176 | tf_op jit(solution)/shard_map/ppermute | solution.py:18
  34.4 1.4 %collective-permute-start.15 = (bf16[512,512]{1,0:T(8,128)(2,1)S(1)}, bf16[512,512]{1,0:T(8,128)(2,1)S(1)}, u32[]{:S(2)}, u32[]{:S(2)}) collective-permute-start(bf16[512,512]{1,0:T(8,128)(2,1)S(1)} %pad_maximum_fusion.refs_0_), channel_id=1, source_target_pairs={{0,4},{1,5},{2,6},{3,7},{4,0},{5,1},{6,2},{7,3},{8,12},{9,13},{10,... | collective-permute-start | bytes 1572872 | tf_op jit(solution)/shard_map/ppermute | solution.py:18
  35.9 1.7 %collective-permute-start.16 = (bf16[128,1024]{1,0:T(8,128)(2,1)S(1)}, bf16[128,1024]{1,0:T(8,128)(2,1)S(1)}, u32[]{:S(2)}, u32[]{:S(2)}) collective-permute-start(bf16[128,1024]{1,0:T(8,128)(2,1)S(1)} %pad_maximum_fusion.1.u0), channel_id=1, source_target_pairs={{0,8},{1,9},{2,10},{3,11},{4,12},{5,13},{6,14},{7,15},{8,0},{9,1},... | collective-permute-start | bytes 786440 | tf_op jit(solution)/shard_map/ppermute | solution.py:18
  39.8 7.3 %collective-permute-done.16.u1 = bf16[128,1024]{1,0:T(8,128)(2,1)S(1)} collective-permute-done((bf16[128,1024]{1,0:T(8,128)(2,1)S(1)}, bf16[128,1024]{1,0:T(8,128)(2,1)S(1)}, u32[]{:S(2)}, u32[]{:S(2)}) %collective-permute-start.16) | collective-permute-done | bytes 262176 | tf_op jit(solution)/shard_map/ppermute | solution.py:18
  47.1 4.2 %collective-permute-done.17.u0 = bf16[128,1024]{1,0:T(8,128)(2,1)S(1)} collective-permute-done((bf16[128,1024]{1,0:T(8,128)(2,1)S(1)}, bf16[128,1024]{1,0:T(8,128)(2,1)S(1)}, u32[]{:S(2)}, u32[]{:S(2)}) %collective-permute-start.17) | collective-permute-done | bytes 262176 | tf_op jit(solution)/shard_map/ppermute | solution.py:18
  52.2 1.6 %collective-permute-start.19 = (bf16[256,512]{1,0:T(8,128)(2,1)S(1)}, bf16[256,512]{1,0:T(8,128)(2,1)S(1)}, u32[]{:S(2)}, u32[]{:S(2)}) collective-permute-start(bf16[256,512]{1,0:T(8,128)(2,1)S(1)} %slice.12), channel_id=1, source_target_pairs={{0,2},{1,3},{2,0},{3,1},{4,6},{5,7},{6,4},{7,5},{8,10},{9,11},{10,... | collective-permute-start | bytes 786440 | tf_op jit(solution)/shard_map/ppermute | solution.py:18
  54.2 2.8 %collective-permute-done.21.other = bf16[512,1024]{1,0:T(8,128)(2,1)S(1)} collective-permute-done((bf16[512,1024]{1,0:T(8,128)(2,1)S(1)}, bf16[512,1024]{1,0:T(8,128)(2,1)S(1)}, u32[]{:S(2)}, u32[]{:S(2)}) %collective-permute-start.21) | collective-permute-done | bytes 1048608 | tf_op jit(solution)/shard_map/ppermute | solution.py:18
  57.0 1.5 %shard_map.97.near = f32[1,256]{1,0:T(1,128)S(1)} custom-call(s32[1,1024]{1,0:T(1,128)S(1)} %bitcast.7, f32[4]{0:T(128)S(1)} %copy-done.2, f32[4]{0:T(128)S(1)} %copy-done.3, bf16[512,1024]{1,0:T(8,128)(2,1)S(1)} %convert_element_type.3.own, bf16[512,1024]{1,0:T(8,128)(2,1)S(1)} %collective-permute-done.21.other, ...), custom_call_target="tpu_custom_call" | custom-call | flops 536870912 | bytes 1024 | tf_op jit(solution)/shard_map/pallas_call | solution.py:268
  58.5 1.9 %shard_map.98.refs_2_ = f32[1024,512]{1,0:T(8,128)S(1)} custom-call(bf16[1024,1024]{1,0:T(8,128)(2,1)S(1)} %shard_map.96.mine, bf16[1024,1024]{1,0:T(8,128)(2,1)S(1)} %collective-permute-done.18.theirs, bf16[512,512]{1,0:T(8,128)(2,1)S(1)} %pad_maximum_fusion.refs_0_, bf16[512,512]{1,0:T(8,128)(2,1)S(1)} %collective-permute-done.14.refs_1_, ...), custom_call_target="tpu_custom_call" | custom-call | flops 1610612736 | bytes 2097152 | tf_op jit(solution)/shard_map/pallas_call | solution.py:275
  60.5 1.6 %shard_map.99.refs_3_ = f32[1,512]{1,0:T(1,128)S(1)} custom-call(s32[1,1024]{1,0:T(1,128)S(1)} %bitcast.8, f32[4]{0:T(128)S(1)} %copy-done.2, f32[4]{0:T(128)S(1)} %copy-done.3, bf16[512,1024]{1,0:T(8,128)(2,1)S(1)} %convert_element_type.3.own, bf16[512,1024]{1,0:T(8,128)(2,1)S(1)} %collective-permute-done.21.other, ...), custom_call_target="tpu_custom_call" | custom-call | flops 536870912 | bytes 2048 | tf_op jit(solution)/shard_map/pallas_call | solution.py:282
  63.0 1.5 %collective-permute-start.24 = (f32[3,512]{1,0:T(4,128)S(1)}, f32[3,512]{1,0:T(4,128)S(1)}, u32[]{:S(2)}, u32[]{:S(2)}) collective-permute-start(f32[3,512]{1,0:T(4,128)S(1)} %get-tuple-element.43), channel_id=1, source_target_pairs={{0,8},{1,9},{2,10},{3,11},{4,12},{5,13},{6,14},{7,15},{8,0},{9,1},... | collective-permute-start | bytes 18440 | tf_op jit(solution)/shard_map/ppermute | solution.py:18
  64.8 2.6 %collective-permute-start.26 = (f32[3,512]{1,0:T(4,128)S(1)}, f32[3,512]{1,0:T(4,128)S(1)}, u32[]{:S(2)}, u32[]{:S(2)}) collective-permute-start(f32[3,512]{1,0:T(4,128)S(1)} %get-tuple-element.43), channel_id=1, source_target_pairs={{0,24},{1,25},{2,26},{3,27},{4,28},{5,29},{6,30},{7,31},{8,16},{9,... | collective-permute-start | bytes 18440 | tf_op jit(solution)/shard_map/ppermute | solution.py:18
  67.4 1.7 %collective-permute-done.25 = f32[3,512]{1,0:T(4,128)S(1)} collective-permute-done((f32[3,512]{1,0:T(4,128)S(1)}, f32[3,512]{1,0:T(4,128)S(1)}, u32[]{:S(2)}, u32[]{:S(2)}) %collective-permute-start.25) | collective-permute-done | bytes 6176 | tf_op jit(solution)/shard_map/ppermute | solution.py:18
  71.2 2.6 %collective-permute-start.29 = (f32[3,512]{1,0:T(4,128)S(1)}, f32[3,512]{1,0:T(4,128)S(1)}, u32[]{:S(2)}, u32[]{:S(2)}) collective-permute-start(f32[3,512]{1,0:T(4,128)S(1)} %maximum_maximum_fusion.1), channel_id=1, source_target_pairs={{0,6},{1,7},{2,4},{3,5},{4,2},{5,3},{6,0},{7,1},{8,14},{9,15},{10,... | collective-permute-start | bytes 18440 | tf_op jit(solution)/shard_map/ppermute | solution.py:18
  (74 shorter events, 20.1 us)
Async XLA Ops:
  2.9 10.5 %collective-permute-start.4 = (bf16[64,512]{1,0:T(8,128)(2,1)S(1)}, bf16[64,512]{1,0:T(8,128)(2,1)S(1)}, u32[]{:S(2)}, u32[]{:S(2)}) collective-permute-start(bf16[64,512]{1,0:T(8,128)(2,1)S(1)} %get-tuple-element.47), channel_id=1, source_target_pairs={{0,1},{1,0},{2,3},{3,2},{4,5},{5,4},{6,7},{7,6},{8,9},{9,8},{10,11... | collective-permute-start | bytes 196616 | tf_op jit(solution)/shard_map/ppermute | solution.py:18
  3.0 7.2 %collective-permute-start.5 = (bf16[32,1024]{1,0:T(8,128)(2,1)}, bf16[32,1024]{1,0:T(8,128)(2,1)S(1)}, u32[]{:S(2)}, u32[]{:S(2)}) collective-permute-start(bf16[32,1024]{1,0:T(8,128)(2,1)} %bitcast.11), channel_id=1, source_target_pairs={{0,2},{1,3},{2,0},{3,1},{4,6},{5,7},{6,4},{7,5},{8,10},{9,11},{10,... | collective-permute-start | bytes 196616 | tf_op jit(solution)/shard_map/ppermute | solution.py:18
  6.0 13.3 %collective-permute-start.7 = (bf16[512,512]{1,0:T(8,128)(2,1)}, bf16[512,512]{1,0:T(8,128)(2,1)S(1)}, u32[]{:S(2)}, u32[]{:S(2)}) collective-permute-start(bf16[512,512]{1,0:T(8,128)(2,1)} %bitcast.5), channel_id=1, source_target_pairs={{0,1},{1,0},{2,3},{3,2},{4,5},{5,4},{6,7},{7,6},{8,9},{9,8},{10,11... | collective-permute-start | bytes 1572872 | tf_op jit(solution)/shard_map/ppermute | solution.py:18
  6.0 9.0 %collective-permute-start.1 = (bf16[32,1024]{1,0:T(8,128)(2,1)S(1)}, bf16[32,1024]{1,0:T(8,128)(2,1)S(1)}, u32[]{:S(2)}, u32[]{:S(2)}) collective-permute-start(bf16[32,1024]{1,0:T(8,128)(2,1)S(1)} %pad_maximum_fusion.3), channel_id=1, source_target_pairs={{0,8},{1,9},{2,10},{3,11},{4,12},{5,13},{6,14},{7,15},{8,0},{9,1},... | collective-permute-start | bytes 196616 | tf_op jit(solution)/shard_map/ppermute | solution.py:18
  7.6 7.4 %collective-permute-start.2 = (bf16[32,1024]{1,0:T(8,128)(2,1)S(1)}, bf16[32,1024]{1,0:T(8,128)(2,1)S(1)}, u32[]{:S(2)}, u32[]{:S(2)}) collective-permute-start(bf16[32,1024]{1,0:T(8,128)(2,1)S(1)} %pad_maximum_fusion.3), channel_id=1, source_target_pairs={{0,16},{1,17},{2,18},{3,19},{4,20},{5,21},{6,22},{7,23},{8,24},{9,... | collective-permute-start | bytes 196616 | tf_op jit(solution)/shard_map/ppermute | solution.py:18
  10.2 6.1 %collective-permute-start.3 = (bf16[32,1024]{1,0:T(8,128)(2,1)S(1)}, bf16[32,1024]{1,0:T(8,128)(2,1)S(1)}, u32[]{:S(2)}, u32[]{:S(2)}) collective-permute-start(bf16[32,1024]{1,0:T(8,128)(2,1)S(1)} %pad_maximum_fusion.3), channel_id=1, source_target_pairs={{0,24},{1,25},{2,26},{3,27},{4,28},{5,29},{6,30},{7,31},{8,16},{9,... | collective-permute-start | bytes 196616 | tf_op jit(solution)/shard_map/ppermute | solution.py:18
  13.4 5.0 %collective-permute-start.6 = (bf16[64,1024]{1,0:T(8,128)(2,1)S(1)}, bf16[64,1024]{1,0:T(8,128)(2,1)S(1)}, u32[]{:S(2)}, u32[]{:S(2)}) collective-permute-start(bf16[64,1024]{1,0:T(8,128)(2,1)S(1)} %pad_maximum_fusion.2), channel_id=1, source_target_pairs={{0,4},{1,5},{2,6},{3,7},{4,0},{5,1},{6,2},{7,3},{8,12},{9,13},{10,... | collective-permute-start | bytes 393224 | tf_op jit(solution)/shard_map/ppermute | solution.py:18
  20.1 7.1 %collective-permute-start.12 = (bf16[128,512]{1,0:T(8,128)(2,1)S(1)}, bf16[128,512]{1,0:T(8,128)(2,1)S(1)}, u32[]{:S(2)}, u32[]{:S(2)}) collective-permute-start(bf16[128,512]{1,0:T(8,128)(2,1)S(1)} %maximum_select_fusion), channel_id=1, source_target_pairs={{0,16},{1,17},{2,18},{3,19},{4,20},{5,21},{6,22},{7,23},{8,24},{9,... | collective-permute-start | bytes 393224 | tf_op jit(solution)/shard_map/ppermute | solution.py:18
  20.3 12.1 %collective-permute-start.10 = (bf16[128,1024]{1,0:T(8,128)(2,1)S(1)}, bf16[128,1024]{1,0:T(8,128)(2,1)S(1)}, u32[]{:S(2)}, u32[]{:S(2)}) collective-permute-start(bf16[128,1024]{1,0:T(8,128)(2,1)S(1)} %constant_dynamic-update-slice_fusion.w0), channel_id=1, source_target_pairs={{0,6},{1,7},{2,4},{3,5},{4,2},{5,3},{6,0},{7,1},{8,14},{9,15},{10,... | collective-permute-start | bytes 786440 | tf_op jit(solution)/shard_map/ppermute | solution.py:18
  22.7 11.5 %collective-permute-start.8 = (bf16[128,1024]{1,0:T(8,128)(2,1)S(1)}, bf16[128,1024]{1,0:T(8,128)(2,1)S(1)}, u32[]{:S(2)}, u32[]{:S(2)}) collective-permute-start(bf16[128,1024]{1,0:T(8,128)(2,1)S(1)} %constant_dynamic-update-slice_fusion.w0), channel_id=1, source_target_pairs={{0,2},{1,3},{2,0},{3,1},{4,6},{5,7},{6,4},{7,5},{8,10},{9,11},{10,... | collective-permute-start | bytes 786440 | tf_op jit(solution)/shard_map/ppermute | solution.py:18
  23.2 11.0 %collective-permute-start.9 = (bf16[128,1024]{1,0:T(8,128)(2,1)S(1)}, bf16[128,1024]{1,0:T(8,128)(2,1)S(1)}, u32[]{:S(2)}, u32[]{:S(2)}) collective-permute-start(bf16[128,1024]{1,0:T(8,128)(2,1)S(1)} %constant_dynamic-update-slice_fusion.w0), channel_id=1, source_target_pairs={{0,4},{1,5},{2,6},{3,7},{4,0},{5,1},{6,2},{7,3},{8,12},{9,13},{10,... | collective-permute-start | bytes 786440 | tf_op jit(solution)/shard_map/ppermute | solution.py:18
  23.7 6.2 %collective-permute-start.11 = (bf16[128,512]{1,0:T(8,128)(2,1)S(1)}, bf16[128,512]{1,0:T(8,128)(2,1)S(1)}, u32[]{:S(2)}, u32[]{:S(2)}) collective-permute-start(bf16[128,512]{1,0:T(8,128)(2,1)S(1)} %maximum_select_fusion), channel_id=1, source_target_pairs={{0,8},{1,9},{2,10},{3,11},{4,12},{5,13},{6,14},{7,15},{8,0},{9,1},... | collective-permute-start | bytes 393224 | tf_op jit(solution)/shard_map/ppermute | solution.py:18
  27.2 5.1 %collective-permute-start.13 = (bf16[128,512]{1,0:T(8,128)(2,1)S(1)}, bf16[128,512]{1,0:T(8,128)(2,1)S(1)}, u32[]{:S(2)}, u32[]{:S(2)}) collective-permute-start(bf16[128,512]{1,0:T(8,128)(2,1)S(1)} %collective-permute-done.12), channel_id=1, source_target_pairs={{0,8},{1,9},{2,10},{3,11},{4,12},{5,13},{6,14},{7,15},{8,0},{9,1},... | collective-permute-start | bytes 393224 | tf_op jit(solution)/shard_map/ppermute | solution.py:18
  34.2 17.1 %collective-permute-start.14 = (bf16[512,512]{1,0:T(8,128)(2,1)S(1)}, bf16[512,512]{1,0:T(8,128)(2,1)S(1)}, u32[]{:S(2)}, u32[]{:S(2)}) collective-permute-start(bf16[512,512]{1,0:T(8,128)(2,1)S(1)} %pad_maximum_fusion.refs_0_), channel_id=1, source_target_pairs={{0,2},{1,3},{2,0},{3,1},{4,6},{5,7},{6,4},{7,5},{8,10},{9,11},{10,... | collective-permute-start | bytes 1572872 | tf_op jit(solution)/shard_map/ppermute | solution.py:18
  34.4 16.9 %collective-permute-start.15 = (bf16[512,512]{1,0:T(8,128)(2,1)S(1)}, bf16[512,512]{1,0:T(8,128)(2,1)S(1)}, u32[]{:S(2)}, u32[]{:S(2)}) collective-permute-start(bf16[512,512]{1,0:T(8,128)(2,1)S(1)} %pad_maximum_fusion.refs_0_), channel_id=1, source_target_pairs={{0,4},{1,5},{2,6},{3,7},{4,0},{5,1},{6,2},{7,3},{8,12},{9,13},{10,... | collective-permute-start | bytes 1572872 | tf_op jit(solution)/shard_map/ppermute | solution.py:18
  35.9 11.3 %collective-permute-start.16 = (bf16[128,1024]{1,0:T(8,128)(2,1)S(1)}, bf16[128,1024]{1,0:T(8,128)(2,1)S(1)}, u32[]{:S(2)}, u32[]{:S(2)}) collective-permute-start(bf16[128,1024]{1,0:T(8,128)(2,1)S(1)} %pad_maximum_fusion.1.u0), channel_id=1, source_target_pairs={{0,8},{1,9},{2,10},{3,11},{4,12},{5,13},{6,14},{7,15},{8,0},{9,1},... | collective-permute-start | bytes 786440 | tf_op jit(solution)/shard_map/ppermute | solution.py:18
  37.6 13.8 %collective-permute-start.17 = (bf16[128,1024]{1,0:T(8,128)(2,1)S(1)}, bf16[128,1024]{1,0:T(8,128)(2,1)S(1)}, u32[]{:S(2)}, u32[]{:S(2)}) collective-permute-start(bf16[128,1024]{1,0:T(8,128)(2,1)S(1)} %pad_maximum_fusion.1.u0), channel_id=1, source_target_pairs={{0,16},{1,17},{2,18},{3,19},{4,20},{5,21},{6,22},{7,23},{8,24},{9,... | collective-permute-start | bytes 786440 | tf_op jit(solution)/shard_map/ppermute | solution.py:18
  51.4 7.2 %collective-permute-start.18 = (bf16[1024,1024]{1,0:T(8,128)(2,1)S(1)}, bf16[1024,1024]{1,0:T(8,128)(2,1)S(1)}, u32[]{:S(2)}, u32[]{:S(2)}) collective-permute-start(bf16[1024,1024]{1,0:T(8,128)(2,1)S(1)} %shard_map.96.mine), channel_id=1, source_target_pairs={{0,1},{1,0},{2,3},{3,2},{4,5},{5,4},{6,7},{7,6},{8,9},{9,8},{10,11... | collective-permute-start | bytes 6291464 | tf_op jit(solution)/shard_map/ppermute | solution.py:18
  51.6 5.4 %collective-permute-start.21 = (bf16[512,1024]{1,0:T(8,128)(2,1)S(1)}, bf16[512,1024]{1,0:T(8,128)(2,1)S(1)}, u32[]{:S(2)}, u32[]{:S(2)}) collective-permute-start(bf16[512,1024]{1,0:T(8,128)(2,1)S(1)} %convert_element_type.3.own), channel_id=1, source_target_pairs={{0,1},{1,0},{2,3},{3,2},{4,5},{5,4},{6,7},{7,6},{8,9},{9,8},{10,11... | collective-permute-start | bytes 3145736 | tf_op jit(solution)/shard_map/ppermute | solution.py:18
  52.2 8.3 %collective-permute-start.22 = (bf16[128,1024]{1,0:T(8,128)(2,1)S(1)}, bf16[128,1024]{1,0:T(8,128)(2,1)S(1)}, u32[]{:S(2)}, u32[]{:S(2)}) collective-permute-start(bf16[128,1024]{1,0:T(8,128)(2,1)S(1)} %collective-permute-done.17.u0), channel_id=1, source_target_pairs={{0,8},{1,9},{2,10},{3,11},{4,12},{5,13},{6,14},{7,15},{8,0},{9,1},... | collective-permute-start | bytes 786440 | tf_op jit(solution)/shard_map/ppermute | solution.py:18
  52.2 9.9 %collective-permute-start.19 = (bf16[256,512]{1,0:T(8,128)(2,1)S(1)}, bf16[256,512]{1,0:T(8,128)(2,1)S(1)}, u32[]{:S(2)}, u32[]{:S(2)}) collective-permute-start(bf16[256,512]{1,0:T(8,128)(2,1)S(1)} %slice.12), channel_id=1, source_target_pairs={{0,2},{1,3},{2,0},{3,1},{4,6},{5,7},{6,4},{7,5},{8,10},{9,11},{10,... | collective-permute-start | bytes 786440 | tf_op jit(solution)/shard_map/ppermute | solution.py:18
  53.8 8.3 %collective-permute-start.20 = (bf16[256,512]{1,0:T(8,128)(2,1)S(1)}, bf16[256,512]{1,0:T(8,128)(2,1)S(1)}, u32[]{:S(2)}, u32[]{:S(2)}) collective-permute-start(bf16[256,512]{1,0:T(8,128)(2,1)S(1)} %slice.13), channel_id=1, source_target_pairs={{0,4},{1,5},{2,6},{3,7},{4,0},{5,1},{6,2},{7,3},{8,12},{9,13},{10,... | collective-permute-start | bytes 786440 | tf_op jit(solution)/shard_map/ppermute | solution.py:18
  62.9 14.1 %collective-permute-start.23 = (f32[512,512]{1,0:T(8,128)S(1)}, f32[512,512]{1,0:T(8,128)S(1)}, u32[]{:S(2)}, u32[]{:S(2)}) collective-permute-start(f32[512,512]{1,0:T(8,128)S(1)} %get-tuple-element.42), channel_id=1, source_target_pairs={{0,1},{1,0},{2,3},{3,2},{4,5},{5,4},{6,7},{7,6},{8,9},{9,8},{10,11... | collective-permute-start | bytes 3145736 | tf_op jit(solution)/shard_map/ppermute | solution.py:18
  64.8 5.4 %collective-permute-start.26 = (f32[3,512]{1,0:T(4,128)S(1)}, f32[3,512]{1,0:T(4,128)S(1)}, u32[]{:S(2)}, u32[]{:S(2)}) collective-permute-start(f32[3,512]{1,0:T(4,128)S(1)} %get-tuple-element.43), channel_id=1, source_target_pairs={{0,24},{1,25},{2,26},{3,27},{4,28},{5,29},{6,30},{7,31},{8,16},{9,... | collective-permute-start | bytes 18440 | tf_op jit(solution)/shard_map/ppermute | solution.py:18
  (12 other events, 115.9 us)

commit v5 on v4

--- a/solution.py
+++ b/solution.py
@@ -83,30 +83,29 @@
     best[...] = found
 
 
-def order_kernel(own, other, ordered):
+def order(slots, depth):
     chip, core = chip_and_core()
+    each = depth // slots
+    row = lax.broadcasted_iota(jnp.int32, (depth, depth), 0)
+    slot = lax.broadcasted_iota(jnp.int32, (depth, depth), 1) // each
+    place = lax.broadcasted_iota(jnp.int32, (depth, depth), 1) % each
+    key = slot // 8 + 4 * ((slot // 2) % 4)
+    source = ((chip ^ key) * 2 + (core + slot) % 2) * each + place
+    return jnp.where(row == source, 1.0, 0.0).astype(BF16)
+
+
+def hidden_kernel(slots, own, other, w0, w1, w2, w3, hidden):
     count, depth = own.shape
-    each = depth // 32
-    row = lax.broadcasted_iota(jnp.int32, (depth, depth), 0)
-    col = lax.broadcasted_iota(jnp.int32, (depth, depth), 1)
-    slot = col // each
-    key = slot // 8 + 4 * ((slot // 2) % 4)
-    source = ((chip ^ key) * 2 + (core + slot) % 2) * each + col % each
-    pick = jnp.where(row == source, 1.0, 0.0).astype(BF16)
-    for at, features in ((0, own), (count, other)):
-        ordered[at : at + count, :] = jnp.dot(
-            features[...], pick, preferred_element_type=F32
-        ).astype(BF16)
-
-
-def hidden_kernel(features, w0, w1, w2, w3, hidden):
+    pick = order(slots, depth)
     weights = jnp.concatenate([w[...] for w in (w0, w1, w2, w3)], axis=0)
     block = 256
-    for at in range(0, features.shape[0], block):
-        v = 0.5 * jnp.dot(
-            features[at : at + block, :], weights, preferred_element_type=F32
-        )
-        hidden[at : at + block, :] = (v * (1.0 + jnp.tanh(v))).astype(BF16)
+    for start, features in ((0, own), (count, other)):
+        for at in range(0, count, block):
+            ordered = jnp.dot(
+                features[at : at + block, :], pick, preferred_element_type=F32
+            ).astype(BF16)
+            v = 0.5 * jnp.dot(ordered, weights, preferred_element_type=F32)
+            hidden[start + at : start + at + block, :] = (v * (1.0 + jnp.tanh(v))).astype(BF16)
 
 
 def add_up(keys, mine, theirs, pieces, finish):
@@ -231,11 +230,9 @@
     user_pair = cat(users[0], move(users[0], 2))
     user_plane = cat(user_pair, move(user_pair, 4))
     features = items[0]
-    ordered = call(
-        order_kernel, shape((2 * count, d_in), BF16), [VMEM, VMEM], 4 * count * d_in * d_in
-    )(features, move(features, 1))
-    in_column, out_rows, user_plane, ordered, resident = lax.optimization_barrier(
-        (in_column, out_rows, user_plane, ordered, res_codes[0])
+    features_other = move(features, 1)
+    in_column, out_rows, features_other, resident = lax.optimization_barrier(
+        (in_column, out_rows, features_other, res_codes[0])
     )
 
     in_pieces = [in_column] + [move(in_column, k) for k in (2, 4, 6)]
@@ -248,11 +245,11 @@
     )
 
     hidden = call(
-        hidden_kernel,
+        functools.partial(hidden_kernel, n),
         shape((2 * count, wide), BF16),
-        [VMEM] * 5,
+        [VMEM] * 6,
         4 * count * d_in * wide,
-    )(ordered, *in_pieces)
+    )(features, features_other, *in_pieces)
     out_x, out_y = move(out_column, 2), move(out_column, 4)
     user_near, user_far = move(user_plane, 8), move(user_plane, 16)
     out_x, out_y, user_near, user_far, hidden = lax.optimization_barrier(

time: 78.4 us -> 74.2 us (0.946)
  waiting for transfers between devices: 31.5 us -> 26 us
  starting transfers between devices: 32.3 us -> 33.3 us
    ppermute x31, waiting for transfers between devices: 31.5 us -> 26 us  [swap(): return lax.ppermute(x, axis, [(i, i ^ k) for i in range(n)])]
    ppermute x31, starting transfers between devices: 32.3 us -> 33.3 us  [swap(): return lax.ppermute(x, axis, [(i, i ^ k) for i in range(n)])]
    pallas_call x2 -> x1, Pallas kernels: 2.09 us -> 2.34 us  [by_permutes(): call(functools.partial(hidden_kernel, n), shape((2 * count, wide), BF16),...]
  transfers between devices with their start and end apart: 31 -> 31, of which waited for: 16 -> 15; matrix products, arithmetic and copies ran while one was open for 5% -> 5% of each run, Pallas kernels for 8% -> 10%
where the time goes in v5:
time: 74.2 us; the launch traced here: 73.9 us
  starting transfers between devices  33.3 us (45%)
  waiting for transfers between devices  26 us (35%)
  Pallas kernels  9.24 us (12%)
  local copies, waits for them, and re-layouts  2.41 us (3%)
  other arithmetic  2.03 us (3%)
  between operations  0.9 us (1%)
    ppermute x31, starting transfers between devices, swap(): return lax.ppermute(x, axis, [(i, i ^ k) for i in range(n)])  33.3 us
    ppermute x31, waiting for transfers between devices, swap(): return lax.ppermute(x, axis, [(i, i ^ k) for i in range(n)])  26 us
    pallas_call x1, Pallas kernels, by_permutes(): call(functools.partial(hidden_kernel, n), shape((2 * count, wide), BF16),...  2.34 us
    pallas_call x1, Pallas kernels, by_permutes(): call(functools.partial(first_embed_kernel, keys[:3]), shape((2 * count, w...  1.87 us
    concatenate x4, other arithmetic, by_permutes(): cat = lambda *parts: jnp.concatenate(parts, axis=0)  1.75 us
    pallas_call x1, Pallas kernels, by_permutes(): call(far_score_kernel, shape((1, 2 * members), F32), [VMEM, SMEM, SMEM] +...  1.61 us
  transfers between devices with their start and end apart: 31, of which 15 were waited for; matrix products, arithmetic and copies ran while one was open for 5% of the time, Pallas kernels for 10%

profile of v5, /device:TPU:0, one launch (start us, length us, event | category | flops | bytes accessed | tf_op | source)
XLA Modules:
  0.0 73.9 jit_solution(8811572047845166692)
XLA Ops:
  3.5 2.6 %collective-permute-start.12 = (bf16[32,1024]{1,0:T(8,128)(2,1)}, bf16[32,1024]{1,0:T(8,128)(2,1)S(1)}, u32[]{:S(2)}, u32[]{:S(2)}) collective-permute-start(bf16[32,1024]{1,0:T(8,128)(2,1)} %bitcast.11), channel_id=1, source_target_pairs={{0,2},{1,3},{2,0},{3,1},{4,6},{5,7},{6,4},{7,5},{8,10},{9,11},{10,... | collective-permute-start | bytes 196616 | tf_op jit(solution)/shard_map/ppermute | solution.py:18
  6.0 1.6 %collective-permute-start.1 = (bf16[32,1024]{1,0:T(8,128)(2,1)S(1)}, bf16[32,1024]{1,0:T(8,128)(2,1)S(1)}, u32[]{:S(2)}, u32[]{:S(2)}) collective-permute-start(bf16[32,1024]{1,0:T(8,128)(2,1)S(1)} %pad_maximum_fusion.3), channel_id=1, source_target_pairs={{0,8},{1,9},{2,10},{3,11},{4,12},{5,13},{6,14},{7,15},{8,0},{9,1},... | collective-permute-start | bytes 196616 | tf_op jit(solution)/shard_map/ppermute | solution.py:18
  7.7 2.6 %collective-permute-start.2 = (bf16[32,1024]{1,0:T(8,128)(2,1)S(1)}, bf16[32,1024]{1,0:T(8,128)(2,1)S(1)}, u32[]{:S(2)}, u32[]{:S(2)}) collective-permute-start(bf16[32,1024]{1,0:T(8,128)(2,1)S(1)} %pad_maximum_fusion.3), channel_id=1, source_target_pairs={{0,16},{1,17},{2,18},{3,19},{4,20},{5,21},{6,22},{7,23},{8,24},{9,... | collective-permute-start | bytes 196616 | tf_op jit(solution)/shard_map/ppermute | solution.py:18
  10.3 2.5 %collective-permute-start.3 = (bf16[32,1024]{1,0:T(8,128)(2,1)S(1)}, bf16[32,1024]{1,0:T(8,128)(2,1)S(1)}, u32[]{:S(2)}, u32[]{:S(2)}) collective-permute-start(bf16[32,1024]{1,0:T(8,128)(2,1)S(1)} %pad_maximum_fusion.3), channel_id=1, source_target_pairs={{0,24},{1,25},{2,26},{3,27},{4,28},{5,29},{6,30},{7,31},{8,16},{9,... | collective-permute-start | bytes 196616 | tf_op jit(solution)/shard_map/ppermute | solution.py:18
  13.7 1.6 %collective-permute-start.13 = (bf16[64,1024]{1,0:T(8,128)(2,1)S(1)}, bf16[64,1024]{1,0:T(8,128)(2,1)S(1)}, u32[]{:S(2)}, u32[]{:S(2)}) collective-permute-start(bf16[64,1024]{1,0:T(8,128)(2,1)S(1)} %pad_maximum_fusion.2), channel_id=1, source_target_pairs={{0,4},{1,5},{2,6},{3,7},{4,0},{5,1},{6,2},{7,3},{8,12},{9,13},{10,... | collective-permute-start | bytes 393224 | tf_op jit(solution)/shard_map/ppermute | solution.py:18
  16.5 2.2 %collective-permute-start.10 = (bf16[128,512]{1,0:T(8,128)(2,1)S(1)}, bf16[128,512]{1,0:T(8,128)(2,1)S(1)}, u32[]{:S(2)}, u32[]{:S(2)}) collective-permute-start(bf16[128,512]{1,0:T(8,128)(2,1)S(1)} %maximum_select_fusion), channel_id=1, source_target_pairs={{0,16},{1,17},{2,18},{3,19},{4,20},{5,21},{6,22},{7,23},{8,24},{9,... | collective-permute-start | bytes 393224 | tf_op jit(solution)/shard_map/ppermute | solution.py:18
  18.7 1.5 %collective-permute-start.7 = (bf16[128,1024]{1,0:T(8,128)(2,1)S(1)}, bf16[128,1024]{1,0:T(8,128)(2,1)S(1)}, u32[]{:S(2)}, u32[]{:S(2)}) collective-permute-start(bf16[128,1024]{1,0:T(8,128)(2,1)S(1)} %constant_dynamic-update-slice_fusion.w0), channel_id=1, source_target_pairs={{0,4},{1,5},{2,6},{3,7},{4,0},{5,1},{6,2},{7,3},{8,12},{9,13},{10,... | collective-permute-start | bytes 786440 | tf_op jit(solution)/shard_map/ppermute | solution.py:18
  20.2 2.0 %collective-permute-start.8 = (bf16[128,1024]{1,0:T(8,128)(2,1)S(1)}, bf16[128,1024]{1,0:T(8,128)(2,1)S(1)}, u32[]{:S(2)}, u32[]{:S(2)}) collective-permute-start(bf16[128,1024]{1,0:T(8,128)(2,1)S(1)} %constant_dynamic-update-slice_fusion.w0), channel_id=1, source_target_pairs={{0,6},{1,7},{2,4},{3,5},{4,2},{5,3},{6,0},{7,1},{8,14},{9,15},{10,... | collective-permute-start | bytes 786440 | tf_op jit(solution)/shard_map/ppermute | solution.py:18
  25.1 3.1 %collective-permute-done.9 = bf16[128,512]{1,0:T(8,128)(2,1)S(1)} collective-permute-done((bf16[128,512]{1,0:T(8,128)(2,1)S(1)}, bf16[128,512]{1,0:T(8,128)(2,1)S(1)}, u32[]{:S(2)}, u32[]{:S(2)}) %collective-permute-start.9) | collective-permute-done | bytes 131104 | tf_op jit(solution)/shard_map/ppermute | solution.py:18
  28.2 1.4 %collective-permute-done.11 = bf16[128,512]{1,0:T(8,128)(2,1)S(1)} collective-permute-done((bf16[128,512]{1,0:T(8,128)(2,1)S(1)}, bf16[128,512]{1,0:T(8,128)(2,1)S(1)}, u32[]{:S(2)}, u32[]{:S(2)}) %collective-permute-start.11) | collective-permute-done | bytes 131104 | tf_op jit(solution)/shard_map/ppermute | solution.py:18
  29.6 2.3 %collective-permute-done.8.w3 = bf16[128,1024]{1,0:T(8,128)(2,1)S(1)} collective-permute-done((bf16[128,1024]{1,0:T(8,128)(2,1)S(1)}, bf16[128,1024]{1,0:T(8,128)(2,1)S(1)}, u32[]{:S(2)}, u32[]{:S(2)}) %collective-permute-start.8) | collective-permute-done | bytes 262176 | tf_op jit(solution)/shard_map/ppermute | solution.py:18
  32.7 1.5 %collective-permute-start.15 = (bf16[512,512]{1,0:T(8,128)(2,1)S(1)}, bf16[512,512]{1,0:T(8,128)(2,1)S(1)}, u32[]{:S(2)}, u32[]{:S(2)}) collective-permute-start(bf16[512,512]{1,0:T(8,128)(2,1)S(1)} %pad_maximum_fusion.refs_0_), channel_id=1, source_target_pairs={{0,4},{1,5},{2,6},{3,7},{4,0},{5,1},{6,2},{7,3},{8,12},{9,13},{10,... | collective-permute-start | bytes 1572872 | tf_op jit(solution)/shard_map/ppermute | solution.py:18
  36.0 2.3 %shard_map.95.mine = bf16[1024,1024]{1,0:T(8,128)(2,1)S(1)} custom-call(bf16[512,512]{1,0:T(8,128)(2,1)S(1)} %bitcast.6, bf16[512,512]{1,0:T(8,128)(2,1)S(1)} %collective-permute-done.5.other, bf16[128,1024]{1,0:T(8,128)(2,1)S(1)} %constant_dynamic-update-slice_fusion.w0, bf16[128,1024]{1,0:T(8,128)(2,1)S(1)} %collective-permute-done.6.w1, ...), custom_call_target="tpu_custom_call" | custom-call | flops 1073741824 | bytes 2097152 | tf_op jit(solution)/shard_map/pallas_call | solution.py:247
  38.4 5.0 %collective-permute-done.16.u1 = bf16[128,1024]{1,0:T(8,128)(2,1)S(1)} collective-permute-done((bf16[128,1024]{1,0:T(8,128)(2,1)S(1)}, bf16[128,1024]{1,0:T(8,128)(2,1)S(1)}, u32[]{:S(2)}, u32[]{:S(2)}) %collective-permute-start.16) | collective-permute-done | bytes 262176 | tf_op jit(solution)/shard_map/ppermute | solution.py:18
  43.4 2.6 %collective-permute-done.17.u0 = bf16[128,1024]{1,0:T(8,128)(2,1)S(1)} collective-permute-done((bf16[128,1024]{1,0:T(8,128)(2,1)S(1)}, bf16[128,1024]{1,0:T(8,128)(2,1)S(1)}, u32[]{:S(2)}, u32[]{:S(2)}) %collective-permute-start.17) | collective-permute-done | bytes 262176 | tf_op jit(solution)/shard_map/ppermute | solution.py:18
  48.8 2.9 %collective-permute-done.21.other = bf16[512,1024]{1,0:T(8,128)(2,1)S(1)} collective-permute-done((bf16[512,1024]{1,0:T(8,128)(2,1)S(1)}, bf16[512,1024]{1,0:T(8,128)(2,1)S(1)}, u32[]{:S(2)}, u32[]{:S(2)}) %collective-permute-start.21) | collective-permute-done | bytes 1048608 | tf_op jit(solution)/shard_map/ppermute | solution.py:18
  51.7 1.5 %shard_map.96.near = f32[1,256]{1,0:T(1,128)S(1)} custom-call(s32[1,1024]{1,0:T(1,128)S(1)} %bitcast.7, f32[4]{0:T(128)S(1)} %copy-done.2, f32[4]{0:T(128)S(1)} %copy-done.3, bf16[512,1024]{1,0:T(8,128)(2,1)S(1)} %convert_element_type.3.own, bf16[512,1024]{1,0:T(8,128)(2,1)S(1)} %collective-permute-done.21.other, ...), custom_call_target="tpu_custom_call" | custom-call | flops 536870912 | bytes 1024 | tf_op jit(solution)/shard_map/pallas_call | solution.py:265
  53.2 1.9 %shard_map.97.refs_2_ = f32[1024,512]{1,0:T(8,128)S(1)} custom-call(bf16[1024,1024]{1,0:T(8,128)(2,1)S(1)} %shard_map.95.mine, bf16[1024,1024]{1,0:T(8,128)(2,1)S(1)} %collective-permute-done.18.theirs, bf16[512,512]{1,0:T(8,128)(2,1)S(1)} %pad_maximum_fusion.refs_0_, bf16[512,512]{1,0:T(8,128)(2,1)S(1)} %collective-permute-done.14.refs_1_, ...), custom_call_target="tpu_custom_call" | custom-call | flops 1610612736 | bytes 2097152 | tf_op jit(solution)/shard_map/pallas_call | solution.py:272
  55.1 1.6 %shard_map.98.refs_3_ = f32[1,512]{1,0:T(1,128)S(1)} custom-call(s32[1,1024]{1,0:T(1,128)S(1)} %bitcast.8, f32[4]{0:T(128)S(1)} %copy-done.2, f32[4]{0:T(128)S(1)} %copy-done.3, bf16[512,1024]{1,0:T(8,128)(2,1)S(1)} %convert_element_type.3.own, bf16[512,1024]{1,0:T(8,128)(2,1)S(1)} %collective-permute-done.21.other, ...), custom_call_target="tpu_custom_call" | custom-call | flops 536870912 | bytes 2048 | tf_op jit(solution)/shard_map/pallas_call | solution.py:279
  59.6 2.5 %collective-permute-start.26 = (f32[3,512]{1,0:T(4,128)S(1)}, f32[3,512]{1,0:T(4,128)S(1)}, u32[]{:S(2)}, u32[]{:S(2)}) collective-permute-start(f32[3,512]{1,0:T(4,128)S(1)} %get-tuple-element.41), channel_id=1, source_target_pairs={{0,24},{1,25},{2,26},{3,27},{4,28},{5,29},{6,30},{7,31},{8,16},{9,... | collective-permute-start | bytes 18440 | tf_op jit(solution)/shard_map/ppermute | solution.py:18
  62.1 1.4 %collective-permute-done.25 = f32[3,512]{1,0:T(4,128)S(1)} collective-permute-done((f32[3,512]{1,0:T(4,128)S(1)}, f32[3,512]{1,0:T(4,128)S(1)}, u32[]{:S(2)}, u32[]{:S(2)}) %collective-permute-start.25) | collective-permute-done | bytes 6176 | tf_op jit(solution)/shard_map/ppermute | solution.py:18
  63.5 1.6 %collective-permute-done.26 = f32[3,512]{1,0:T(4,128)S(1)} collective-permute-done((f32[3,512]{1,0:T(4,128)S(1)}, f32[3,512]{1,0:T(4,128)S(1)}, u32[]{:S(2)}, u32[]{:S(2)}) %collective-permute-start.26) | collective-permute-done | bytes 6176 | tf_op jit(solution)/shard_map/ppermute | solution.py:18
  66.9 1.6 %collective-permute-start.29 = (f32[3,512]{1,0:T(4,128)S(1)}, f32[3,512]{1,0:T(4,128)S(1)}, u32[]{:S(2)}, u32[]{:S(2)}) collective-permute-start(f32[3,512]{1,0:T(4,128)S(1)} %maximum_maximum_fusion.1), channel_id=1, source_target_pairs={{0,6},{1,7},{2,4},{3,5},{4,2},{5,3},{6,0},{7,1},{8,14},{9,15},{10,... | collective-permute-start | bytes 18440 | tf_op jit(solution)/shard_map/ppermute | solution.py:18
  70.0 1.5 %collective-permute-done.29 = f32[3,512]{1,0:T(4,128)S(1)} collective-permute-done((f32[3,512]{1,0:T(4,128)S(1)}, f32[3,512]{1,0:T(4,128)S(1)}, u32[]{:S(2)}, u32[]{:S(2)}) %collective-permute-start.29) | collective-permute-done | bytes 6176 | tf_op jit(solution)/shard_map/ppermute | solution.py:18
  (73 shorter events, 21.9 us)
Async XLA Ops:
  2.9 10.8 %collective-permute-start.4 = (bf16[64,512]{1,0:T(8,128)(2,1)S(1)}, bf16[64,512]{1,0:T(8,128)(2,1)S(1)}, u32[]{:S(2)}, u32[]{:S(2)}) collective-permute-start(bf16[64,512]{1,0:T(8,128)(2,1)S(1)} %get-tuple-element.45), channel_id=1, source_target_pairs={{0,1},{1,0},{2,3},{3,2},{4,5},{5,4},{6,7},{7,6},{8,9},{9,8},{10,11... | collective-permute-start | bytes 196616 | tf_op jit(solution)/shard_map/ppermute | solution.py:18
  3.0 13.4 %collective-permute-start.5 = (bf16[512,512]{1,0:T(8,128)(2,1)}, bf16[512,512]{1,0:T(8,128)(2,1)S(1)}, u32[]{:S(2)}, u32[]{:S(2)}) collective-permute-start(bf16[512,512]{1,0:T(8,128)(2,1)} %bitcast.5), channel_id=1, source_target_pairs={{0,1},{1,0},{2,3},{3,2},{4,5},{5,4},{6,7},{7,6},{8,9},{9,8},{10,11... | collective-permute-start | bytes 1572872 | tf_op jit(solution)/shard_map/ppermute | solution.py:18
  3.5 6.8 %collective-permute-start.12 = (bf16[32,1024]{1,0:T(8,128)(2,1)}, bf16[32,1024]{1,0:T(8,128)(2,1)S(1)}, u32[]{:S(2)}, u32[]{:S(2)}) collective-permute-start(bf16[32,1024]{1,0:T(8,128)(2,1)} %bitcast.11), channel_id=1, source_target_pairs={{0,2},{1,3},{2,0},{3,1},{4,6},{5,7},{6,4},{7,5},{8,10},{9,11},{10,... | collective-permute-start | bytes 196616 | tf_op jit(solution)/shard_map/ppermute | solution.py:18
  6.0 9.2 %collective-permute-start.1 = (bf16[32,1024]{1,0:T(8,128)(2,1)S(1)}, bf16[32,1024]{1,0:T(8,128)(2,1)S(1)}, u32[]{:S(2)}, u32[]{:S(2)}) collective-permute-start(bf16[32,1024]{1,0:T(8,128)(2,1)S(1)} %pad_maximum_fusion.3), channel_id=1, source_target_pairs={{0,8},{1,9},{2,10},{3,11},{4,12},{5,13},{6,14},{7,15},{8,0},{9,1},... | collective-permute-start | bytes 196616 | tf_op jit(solution)/shard_map/ppermute | solution.py:18
  7.7 7.6 %collective-permute-start.2 = (bf16[32,1024]{1,0:T(8,128)(2,1)S(1)}, bf16[32,1024]{1,0:T(8,128)(2,1)S(1)}, u32[]{:S(2)}, u32[]{:S(2)}) collective-permute-start(bf16[32,1024]{1,0:T(8,128)(2,1)S(1)} %pad_maximum_fusion.3), channel_id=1, source_target_pairs={{0,16},{1,17},{2,18},{3,19},{4,20},{5,21},{6,22},{7,23},{8,24},{9,... | collective-permute-start | bytes 196616 | tf_op jit(solution)/shard_map/ppermute | solution.py:18
  10.3 6.2 %collective-permute-start.3 = (bf16[32,1024]{1,0:T(8,128)(2,1)S(1)}, bf16[32,1024]{1,0:T(8,128)(2,1)S(1)}, u32[]{:S(2)}, u32[]{:S(2)}) collective-permute-start(bf16[32,1024]{1,0:T(8,128)(2,1)S(1)} %pad_maximum_fusion.3), channel_id=1, source_target_pairs={{0,24},{1,25},{2,26},{3,27},{4,28},{5,29},{6,30},{7,31},{8,16},{9,... | collective-permute-start | bytes 196616 | tf_op jit(solution)/shard_map/ppermute | solution.py:18
  13.7 8.5 %collective-permute-start.13 = (bf16[64,1024]{1,0:T(8,128)(2,1)S(1)}, bf16[64,1024]{1,0:T(8,128)(2,1)S(1)}, u32[]{:S(2)}, u32[]{:S(2)}) collective-permute-start(bf16[64,1024]{1,0:T(8,128)(2,1)S(1)} %pad_maximum_fusion.2), channel_id=1, source_target_pairs={{0,4},{1,5},{2,6},{3,7},{4,0},{5,1},{6,2},{7,3},{8,12},{9,13},{10,... | collective-permute-start | bytes 393224 | tf_op jit(solution)/shard_map/ppermute | solution.py:18
  16.5 7.7 %collective-permute-start.10 = (bf16[128,512]{1,0:T(8,128)(2,1)S(1)}, bf16[128,512]{1,0:T(8,128)(2,1)S(1)}, u32[]{:S(2)}, u32[]{:S(2)}) collective-permute-start(bf16[128,512]{1,0:T(8,128)(2,1)S(1)} %maximum_select_fusion), channel_id=1, source_target_pairs={{0,16},{1,17},{2,18},{3,19},{4,20},{5,21},{6,22},{7,23},{8,24},{9,... | collective-permute-start | bytes 393224 | tf_op jit(solution)/shard_map/ppermute | solution.py:18
  18.6 11.0 %collective-permute-start.6 = (bf16[128,1024]{1,0:T(8,128)(2,1)S(1)}, bf16[128,1024]{1,0:T(8,128)(2,1)S(1)}, u32[]{:S(2)}, u32[]{:S(2)}) collective-permute-start(bf16[128,1024]{1,0:T(8,128)(2,1)S(1)} %constant_dynamic-update-slice_fusion.w0), channel_id=1, source_target_pairs={{0,2},{1,3},{2,0},{3,1},{4,6},{5,7},{6,4},{7,5},{8,10},{9,11},{10,... | collective-permute-start | bytes 786440 | tf_op jit(solution)/shard_map/ppermute | solution.py:18
  18.7 11.0 %collective-permute-start.7 = (bf16[128,1024]{1,0:T(8,128)(2,1)S(1)}, bf16[128,1024]{1,0:T(8,128)(2,1)S(1)}, u32[]{:S(2)}, u32[]{:S(2)}) collective-permute-start(bf16[128,1024]{1,0:T(8,128)(2,1)S(1)} %constant_dynamic-update-slice_fusion.w0), channel_id=1, source_target_pairs={{0,4},{1,5},{2,6},{3,7},{4,0},{5,1},{6,2},{7,3},{8,12},{9,13},{10,... | collective-permute-start | bytes 786440 | tf_op jit(solution)/shard_map/ppermute | solution.py:18
  20.2 11.7 %collective-permute-start.8 = (bf16[128,1024]{1,0:T(8,128)(2,1)S(1)}, bf16[128,1024]{1,0:T(8,128)(2,1)S(1)}, u32[]{:S(2)}, u32[]{:S(2)}) collective-permute-start(bf16[128,1024]{1,0:T(8,128)(2,1)S(1)} %constant_dynamic-update-slice_fusion.w0), channel_id=1, source_target_pairs={{0,6},{1,7},{2,4},{3,5},{4,2},{5,3},{6,0},{7,1},{8,14},{9,15},{10,... | collective-permute-start | bytes 786440 | tf_op jit(solution)/shard_map/ppermute | solution.py:18
  22.1 6.0 %collective-permute-start.9 = (bf16[128,512]{1,0:T(8,128)(2,1)S(1)}, bf16[128,512]{1,0:T(8,128)(2,1)S(1)}, u32[]{:S(2)}, u32[]{:S(2)}) collective-permute-start(bf16[128,512]{1,0:T(8,128)(2,1)S(1)} %maximum_select_fusion), channel_id=1, source_target_pairs={{0,8},{1,9},{2,10},{3,11},{4,12},{5,13},{6,14},{7,15},{8,0},{9,1},... | collective-permute-start | bytes 393224 | tf_op jit(solution)/shard_map/ppermute | solution.py:18
  24.2 5.4 %collective-permute-start.11 = (bf16[128,512]{1,0:T(8,128)(2,1)S(1)}, bf16[128,512]{1,0:T(8,128)(2,1)S(1)}, u32[]{:S(2)}, u32[]{:S(2)}) collective-permute-start(bf16[128,512]{1,0:T(8,128)(2,1)S(1)} %collective-permute-done.10), channel_id=1, source_target_pairs={{0,8},{1,9},{2,10},{3,11},{4,12},{5,13},{6,14},{7,15},{8,0},{9,1},... | collective-permute-start | bytes 393224 | tf_op jit(solution)/shard_map/ppermute | solution.py:18
  31.9 14.1 %collective-permute-start.14 = (bf16[512,512]{1,0:T(8,128)(2,1)S(1)}, bf16[512,512]{1,0:T(8,128)(2,1)S(1)}, u32[]{:S(2)}, u32[]{:S(2)}) collective-permute-start(bf16[512,512]{1,0:T(8,128)(2,1)S(1)} %pad_maximum_fusion.refs_0_), channel_id=1, source_target_pairs={{0,2},{1,3},{2,0},{3,1},{4,6},{5,7},{6,4},{7,5},{8,10},{9,11},{10,... | collective-permute-start | bytes 1572872 | tf_op jit(solution)/shard_map/ppermute | solution.py:18
  32.7 13.3 %collective-permute-start.15 = (bf16[512,512]{1,0:T(8,128)(2,1)S(1)}, bf16[512,512]{1,0:T(8,128)(2,1)S(1)}, u32[]{:S(2)}, u32[]{:S(2)}) collective-permute-start(bf16[512,512]{1,0:T(8,128)(2,1)S(1)} %pad_maximum_fusion.refs_0_), channel_id=1, source_target_pairs={{0,4},{1,5},{2,6},{3,7},{4,0},{5,1},{6,2},{7,3},{8,12},{9,13},{10,... | collective-permute-start | bytes 1572872 | tf_op jit(solution)/shard_map/ppermute | solution.py:18
  34.2 9.2 %collective-permute-start.16 = (bf16[128,1024]{1,0:T(8,128)(2,1)S(1)}, bf16[128,1024]{1,0:T(8,128)(2,1)S(1)}, u32[]{:S(2)}, u32[]{:S(2)}) collective-permute-start(bf16[128,1024]{1,0:T(8,128)(2,1)S(1)} %pad_maximum_fusion.1.u0), channel_id=1, source_target_pairs={{0,8},{1,9},{2,10},{3,11},{4,12},{5,13},{6,14},{7,15},{8,0},{9,1},... | collective-permute-start | bytes 786440 | tf_op jit(solution)/shard_map/ppermute | solution.py:18
  35.1 10.9 %collective-permute-start.17 = (bf16[128,1024]{1,0:T(8,128)(2,1)S(1)}, bf16[128,1024]{1,0:T(8,128)(2,1)S(1)}, u32[]{:S(2)}, u32[]{:S(2)}) collective-permute-start(bf16[128,1024]{1,0:T(8,128)(2,1)S(1)} %pad_maximum_fusion.1.u0), channel_id=1, source_target_pairs={{0,16},{1,17},{2,18},{3,19},{4,20},{5,21},{6,22},{7,23},{8,24},{9,... | collective-permute-start | bytes 786440 | tf_op jit(solution)/shard_map/ppermute | solution.py:18
  46.0 7.2 %collective-permute-start.18 = (bf16[1024,1024]{1,0:T(8,128)(2,1)S(1)}, bf16[1024,1024]{1,0:T(8,128)(2,1)S(1)}, u32[]{:S(2)}, u32[]{:S(2)}) collective-permute-start(bf16[1024,1024]{1,0:T(8,128)(2,1)S(1)} %shard_map.95.mine), channel_id=1, source_target_pairs={{0,1},{1,0},{2,3},{3,2},{4,5},{5,4},{6,7},{7,6},{8,9},{9,8},{10,11... | collective-permute-start | bytes 6291464 | tf_op jit(solution)/shard_map/ppermute | solution.py:18
  46.3 5.4 %collective-permute-start.21 = (bf16[512,1024]{1,0:T(8,128)(2,1)S(1)}, bf16[512,1024]{1,0:T(8,128)(2,1)S(1)}, u32[]{:S(2)}, u32[]{:S(2)}) collective-permute-start(bf16[512,1024]{1,0:T(8,128)(2,1)S(1)} %convert_element_type.3.own), channel_id=1, source_target_pairs={{0,1},{1,0},{2,3},{3,2},{4,5},{5,4},{6,7},{7,6},{8,9},{9,8},{10,11... | collective-permute-start | bytes 3145736 | tf_op jit(solution)/shard_map/ppermute | solution.py:18
  46.9 8.3 %collective-permute-start.22 = (bf16[128,1024]{1,0:T(8,128)(2,1)S(1)}, bf16[128,1024]{1,0:T(8,128)(2,1)S(1)}, u32[]{:S(2)}, u32[]{:S(2)}) collective-permute-start(bf16[128,1024]{1,0:T(8,128)(2,1)S(1)} %collective-permute-done.17.u0), channel_id=1, source_target_pairs={{0,8},{1,9},{2,10},{3,11},{4,12},{5,13},{6,14},{7,15},{8,0},{9,1},... | collective-permute-start | bytes 786440 | tf_op jit(solution)/shard_map/ppermute | solution.py:18
  46.9 9.9 %collective-permute-start.19 = (bf16[256,512]{1,0:T(8,128)(2,1)S(1)}, bf16[256,512]{1,0:T(8,128)(2,1)S(1)}, u32[]{:S(2)}, u32[]{:S(2)}) collective-permute-start(bf16[256,512]{1,0:T(8,128)(2,1)S(1)} %slice.12), channel_id=1, source_target_pairs={{0,2},{1,3},{2,0},{3,1},{4,6},{5,7},{6,4},{7,5},{8,10},{9,11},{10,... | collective-permute-start | bytes 786440 | tf_op jit(solution)/shard_map/ppermute | solution.py:18
  48.2 8.6 %collective-permute-start.20 = (bf16[256,512]{1,0:T(8,128)(2,1)S(1)}, bf16[256,512]{1,0:T(8,128)(2,1)S(1)}, u32[]{:S(2)}, u32[]{:S(2)}) collective-permute-start(bf16[256,512]{1,0:T(8,128)(2,1)S(1)} %slice.13), channel_id=1, source_target_pairs={{0,4},{1,5},{2,6},{3,7},{4,0},{5,1},{6,2},{7,3},{8,12},{9,13},{10,... | collective-permute-start | bytes 786440 | tf_op jit(solution)/shard_map/ppermute | solution.py:18
  57.6 15.2 %collective-permute-start.23 = (f32[512,512]{1,0:T(8,128)S(1)}, f32[512,512]{1,0:T(8,128)S(1)}, u32[]{:S(2)}, u32[]{:S(2)}) collective-permute-start(f32[512,512]{1,0:T(8,128)S(1)} %get-tuple-element.40), channel_id=1, source_target_pairs={{0,1},{1,0},{2,3},{3,2},{4,5},{5,4},{6,7},{7,6},{8,9},{9,8},{10,11... | collective-permute-start | bytes 3145736 | tf_op jit(solution)/shard_map/ppermute | solution.py:18
  59.6 5.4 %collective-permute-start.26 = (f32[3,512]{1,0:T(4,128)S(1)}, f32[3,512]{1,0:T(4,128)S(1)}, u32[]{:S(2)}, u32[]{:S(2)}) collective-permute-start(f32[3,512]{1,0:T(4,128)S(1)} %get-tuple-element.41), channel_id=1, source_target_pairs={{0,24},{1,25},{2,26},{3,27},{4,28},{5,29},{6,30},{7,31},{8,16},{9,... | collective-permute-start | bytes 18440 | tf_op jit(solution)/shard_map/ppermute | solution.py:18
  (12 other events, 118.4 us)

commit v6 on v5

--- a/solution.py
+++ b/solution.py
@@ -43,44 +43,41 @@
     return step_d, parts
 
 
-def score(step_d, parts, own, other, member):
+def score(step_d, parts, own, other, pieces):
+    chip, _ = chip_and_core()
     contract = (((1,), (1,)), ((), ()))
     product = lambda left, right: lax.dot_general(
         left, right, contract, preferred_element_type=F32
     )
-    folded = (member.astype(F32) * step_d).astype(BF16)
+    blocks = []
+    for piece in pieces:
+        rows = piece.shape[0] // 4
+        for place in range(4):
+            start = pl.multiple_of(((chip % 4) ^ place) * rows, rows)
+            blocks.append(piece[pl.ds(start, rows), :])
+    member = jnp.concatenate(blocks, axis=0)
+    folded = (member.astype(F32) * step_d[...]).astype(BF16)
     most = jnp.maximum(
         jnp.max(product(own[...], folded), axis=0, keepdims=True),
         jnp.max(product(other[...], folded), axis=0, keepdims=True),
     )
-    return most + jnp.sum(product(parts, member), axis=0, keepdims=True)
-
-
-def near_score_kernel(idx, lo, step, own, other, u0, u1, best):
-    step_d, parts = score_parts(idx, lo, step)
-    members = jnp.concatenate([u0[...], u1[...]], axis=0)
-    best[...] = score(step_d, parts, own, other, members)
-
-
-def far_score_kernel(idx, lo, step, own, other, u0, u1, near, best):
+    return most + jnp.sum(product(parts[...], member), axis=0, keepdims=True)
+
+
+def near_score_kernel(step_d, parts, own, other, u0, u1, u2, best):
+    best[...] = score(step_d, parts, own, other, (u0, u1, u2))
+
+
+def far_score_kernel(step_d, parts, own, other, u0, near, best):
     chip, _ = chip_and_core()
-    step_d, parts = score_parts(idx, lo, step)
-    members = jnp.concatenate([u0[...], u1[...]], axis=0)
-    found = jnp.concatenate(
-        [near[...], score(step_d, parts, own, other, members)], axis=1
-    )
-    total = found.shape[1]
-    each = total // 16
-    lane = lax.broadcasted_iota(jnp.int32, found.shape, 1)
-    for bit in (1, 2, 4, 8):
-        far = bit * each
-        crossed = jnp.where(
-            (lane // far) % 2 == 1,
-            pltpu.roll(found, far, 1),
-            pltpu.roll(found, total - far, 1),
-        )
-        found = jnp.where((chip // bit) % 2 == 1, crossed, found)
-    best[...] = found
+    each = best.shape[1] // 4
+    found = [near[:, at * each : (at + 1) * each] for at in range(3)]
+    found.append(score(step_d, parts, own, other, (u0,)))
+    for bit in (1, 2):
+        crossed = (chip // (4 * bit)) % 2 == 1
+        found = [jnp.where(crossed, found[at ^ bit], found[at]) for at in range(4)]
+    for at in range(4):
+        best[:, at * each : (at + 1) * each] = found[at]
 
 
 def order(slots, depth):
@@ -94,7 +91,8 @@
     return jnp.where(row == source, 1.0, 0.0).astype(BF16)
 
 
-def hidden_kernel(slots, own, other, w0, w1, w2, w3, hidden):
+def hidden_kernel(slots, idx, lo, step, own, other, w0, w1, w2, w3, hidden, step_d, parts):
+    step_d[...], parts[...] = score_parts(idx, lo, step)
     count, depth = own.shape
     pick = order(slots, depth)
     weights = jnp.concatenate([w[...] for w in (w0, w1, w2, w3)], axis=0)
@@ -244,12 +242,13 @@
         (*in_pieces, out_column, user_plane)
     )
 
-    hidden = call(
+    dims = users.shape[2]
+    hidden, *ranges = call(
         functools.partial(hidden_kernel, n),
-        shape((2 * count, wide), BF16),
-        [VMEM] * 6,
+        (shape((2 * count, wide), BF16), shape((1, dims), F32), shape((16, dims), BF16)),
+        [VMEM, SMEM, SMEM] + [VMEM] * 6,
         4 * count * d_in * wide,
-    )(features, features_other, *in_pieces)
+    )(range_idx[None, :], range_lo, range_step, features, features_other, *in_pieces)
     out_x, out_y = move(out_column, 2), move(out_column, 4)
     user_near, user_far = move(user_plane, 8), move(user_plane, 16)
     out_x, out_y, user_near, user_far, hidden = lax.optimization_barrier(
@@ -259,15 +258,8 @@
     out_low, out_high = move(out_y[:half], 2), move(out_x[half:], 4)
     user_last = move(user_far, 8)
 
-    ranges = (range_idx[None, :], range_lo, range_step)
-    members = 2 * user_plane.shape[0]
-    score_flops = 4 * members * count * users.shape[2]
-    near_best = call(
-        near_score_kernel,
-        shape((1, members), F32),
-        [VMEM, SMEM, SMEM] + [VMEM] * 4,
-        score_flops,
-    )(*ranges, codes, codes_other, user_plane, user_near)
+    members = user_plane.shape[0]
+    score_flops = 4 * members * count * dims
     hidden_other = move(hidden, 1)
     partial = call(
         functools.partial(first_embed_kernel, keys[:3]),
@@ -275,13 +267,19 @@
         [VMEM] * 5,
         6 * count * wide * width,
     )(hidden, hidden_other, out_column, out_x, out_y)
-    near_best, partial = lax.optimization_barrier((near_best, partial))
+    near_plane, partial = lax.optimization_barrier((user_plane, partial))
+    near_best = call(
+        near_score_kernel,
+        shape((1, 3 * members), F32),
+        [VMEM] * 7,
+        3 * score_flops,
+    )(*ranges, codes, codes_other, near_plane, user_near, user_far)
     best = call(
         far_score_kernel,
-        shape((1, 2 * members), F32),
-        [VMEM, SMEM, SMEM] + [VMEM] * 5,
+        shape((1, 4 * members), F32),
+        [VMEM] * 6,
         score_flops,
-    )(*ranges, codes, codes_other, user_far, user_last, near_best)
+    )(*ranges, codes, codes_other, user_last, near_best)
 
     own, other, merged = call(
         functools.partial(last_embed_kernel, (keys[3][:2], keys[3][2:])),

time: 74.2 us -> 72.7 us (0.980)
  waiting for transfers between devices: 26 us -> 24.9 us
    ppermute x31, waiting for transfers between devices: 26 us -> 24.9 us  [swap(): return lax.ppermute(x, axis, [(i, i ^ k) for i in range(n)])]
  transfers between devices with their start and end apart: 31 -> 31, of which waited for: 15 -> 17; matrix products, arithmetic and copies ran while one was open for 5% -> 5% of each run, Pallas kernels for 10% -> 10%
where the time goes in v6:
time: 72.7 us; the launch traced here: 72.4 us
  starting transfers between devices  33.3 us (46%)
  waiting for transfers between devices  24.9 us (34%)
  Pallas kernels  8.86 us (12%)
  local copies, waits for them, and re-layouts  2.39 us (3%)
  other arithmetic  2.03 us (3%)
  between operations  0.92 us (1%)
    ppermute x31, starting transfers between devices, swap(): return lax.ppermute(x, axis, [(i, i ^ k) for i in range(n)])  33.3 us
    ppermute x31, waiting for transfers between devices, swap(): return lax.ppermute(x, axis, [(i, i ^ k) for i in range(n)])  24.9 us
    pallas_call x1, Pallas kernels, by_permutes(): call(functools.partial(hidden_kernel, n), (shape((2 * count, wide), BF16)...  2.86 us
    pallas_call x1, Pallas kernels, by_permutes(): call(functools.partial(first_embed_kernel, keys[:3]), shape((2 * count, w...  1.84 us
    concatenate x4, other arithmetic, by_permutes(): cat = lambda *parts: jnp.concatenate(parts, axis=0)  1.75 us
    pallas_call x1, Pallas kernels, by_permutes(): call(near_score_kernel, shape((1, 3 * members), F32), [VMEM] * 7, 3 * sco...  1.47 us
  transfers between devices with their start and end apart: 31, of which 17 were waited for; matrix products, arithmetic and copies ran while one was open for 5% of the time, Pallas kernels for 10%

profile of v6, /device:TPU:0, one launch (start us, length us, event | category | flops | bytes accessed | tf_op | source)
XLA Modules:
  0.0 72.4 jit_solution(7571945237774146705)
XLA Ops:
  3.5 2.6 %collective-permute-start.12 = (bf16[32,1024]{1,0:T(8,128)(2,1)}, bf16[32,1024]{1,0:T(8,128)(2,1)S(1)}, u32[]{:S(2)}, u32[]{:S(2)}) collective-permute-start(bf16[32,1024]{1,0:T(8,128)(2,1)} %bitcast.10), channel_id=1, source_target_pairs={{0,2},{1,3},{2,0},{3,1},{4,6},{5,7},{6,4},{7,5},{8,10},{9,11},{10,... | collective-permute-start | bytes 196616 | tf_op jit(solution)/shard_map/ppermute | solution.py:18
  6.1 1.6 %collective-permute-start.1 = (bf16[32,1024]{1,0:T(8,128)(2,1)S(1)}, bf16[32,1024]{1,0:T(8,128)(2,1)S(1)}, u32[]{:S(2)}, u32[]{:S(2)}) collective-permute-start(bf16[32,1024]{1,0:T(8,128)(2,1)S(1)} %pad_maximum_fusion.3), channel_id=1, source_target_pairs={{0,8},{1,9},{2,10},{3,11},{4,12},{5,13},{6,14},{7,15},{8,0},{9,1},... | collective-permute-start | bytes 196616 | tf_op jit(solution)/shard_map/ppermute | solution.py:18
  7.7 2.6 %collective-permute-start.2 = (bf16[32,1024]{1,0:T(8,128)(2,1)S(1)}, bf16[32,1024]{1,0:T(8,128)(2,1)S(1)}, u32[]{:S(2)}, u32[]{:S(2)}) collective-permute-start(bf16[32,1024]{1,0:T(8,128)(2,1)S(1)} %pad_maximum_fusion.3), channel_id=1, source_target_pairs={{0,16},{1,17},{2,18},{3,19},{4,20},{5,21},{6,22},{7,23},{8,24},{9,... | collective-permute-start | bytes 196616 | tf_op jit(solution)/shard_map/ppermute | solution.py:18
  10.3 2.5 %collective-permute-start.3 = (bf16[32,1024]{1,0:T(8,128)(2,1)S(1)}, bf16[32,1024]{1,0:T(8,128)(2,1)S(1)}, u32[]{:S(2)}, u32[]{:S(2)}) collective-permute-start(bf16[32,1024]{1,0:T(8,128)(2,1)S(1)} %pad_maximum_fusion.3), channel_id=1, source_target_pairs={{0,24},{1,25},{2,26},{3,27},{4,28},{5,29},{6,30},{7,31},{8,16},{9,... | collective-permute-start | bytes 196616 | tf_op jit(solution)/shard_map/ppermute | solution.py:18
  13.7 1.6 %collective-permute-start.13 = (bf16[64,1024]{1,0:T(8,128)(2,1)S(1)}, bf16[64,1024]{1,0:T(8,128)(2,1)S(1)}, u32[]{:S(2)}, u32[]{:S(2)}) collective-permute-start(bf16[64,1024]{1,0:T(8,128)(2,1)S(1)} %pad_maximum_fusion.2), channel_id=1, source_target_pairs={{0,4},{1,5},{2,6},{3,7},{4,0},{5,1},{6,2},{7,3},{8,12},{9,13},{10,... | collective-permute-start | bytes 393224 | tf_op jit(solution)/shard_map/ppermute | solution.py:18
  16.5 2.2 %collective-permute-start.10 = (bf16[128,512]{1,0:T(8,128)(2,1)S(1)}, bf16[128,512]{1,0:T(8,128)(2,1)S(1)}, u32[]{:S(2)}, u32[]{:S(2)}) collective-permute-start(bf16[128,512]{1,0:T(8,128)(2,1)S(1)} %maximum_select_fusion), channel_id=1, source_target_pairs={{0,16},{1,17},{2,18},{3,19},{4,20},{5,21},{6,22},{7,23},{8,24},{9,... | collective-permute-start | bytes 393224 | tf_op jit(solution)/shard_map/ppermute | solution.py:18
  18.7 1.5 %collective-permute-start.7 = (bf16[128,1024]{1,0:T(8,128)(2,1)S(1)}, bf16[128,1024]{1,0:T(8,128)(2,1)S(1)}, u32[]{:S(2)}, u32[]{:S(2)}) collective-permute-start(bf16[128,1024]{1,0:T(8,128)(2,1)S(1)} %constant_dynamic-update-slice_fusion.w0), channel_id=1, source_target_pairs={{0,4},{1,5},{2,6},{3,7},{4,0},{5,1},{6,2},{7,3},{8,12},{9,13},{10,... | collective-permute-start | bytes 786440 | tf_op jit(solution)/shard_map/ppermute | solution.py:18
  20.2 2.0 %collective-permute-start.8 = (bf16[128,1024]{1,0:T(8,128)(2,1)S(1)}, bf16[128,1024]{1,0:T(8,128)(2,1)S(1)}, u32[]{:S(2)}, u32[]{:S(2)}) collective-permute-start(bf16[128,1024]{1,0:T(8,128)(2,1)S(1)} %constant_dynamic-update-slice_fusion.w0), channel_id=1, source_target_pairs={{0,6},{1,7},{2,4},{3,5},{4,2},{5,3},{6,0},{7,1},{8,14},{9,15},{10,... | collective-permute-start | bytes 786440 | tf_op jit(solution)/shard_map/ppermute | solution.py:18
  25.1 3.1 %collective-permute-done.9 = bf16[128,512]{1,0:T(8,128)(2,1)S(1)} collective-permute-done((bf16[128,512]{1,0:T(8,128)(2,1)S(1)}, bf16[128,512]{1,0:T(8,128)(2,1)S(1)}, u32[]{:S(2)}, u32[]{:S(2)}) %collective-permute-start.9) | collective-permute-done | bytes 131104 | tf_op jit(solution)/shard_map/ppermute | solution.py:18
  28.2 1.4 %collective-permute-done.11 = bf16[128,512]{1,0:T(8,128)(2,1)S(1)} collective-permute-done((bf16[128,512]{1,0:T(8,128)(2,1)S(1)}, bf16[128,512]{1,0:T(8,128)(2,1)S(1)}, u32[]{:S(2)}, u32[]{:S(2)}) %collective-permute-start.11) | collective-permute-done | bytes 131104 | tf_op jit(solution)/shard_map/ppermute | solution.py:18
  29.7 2.3 %collective-permute-done.8.w3 = bf16[128,1024]{1,0:T(8,128)(2,1)S(1)} collective-permute-done((bf16[128,1024]{1,0:T(8,128)(2,1)S(1)}, bf16[128,1024]{1,0:T(8,128)(2,1)S(1)}, u32[]{:S(2)}, u32[]{:S(2)}) %collective-permute-start.8) | collective-permute-done | bytes 262176 | tf_op jit(solution)/shard_map/ppermute | solution.py:18
  32.7 1.5 %collective-permute-start.15 = (bf16[512,512]{1,0:T(8,128)(2,1)S(1)}, bf16[512,512]{1,0:T(8,128)(2,1)S(1)}, u32[]{:S(2)}, u32[]{:S(2)}) collective-permute-start(bf16[512,512]{1,0:T(8,128)(2,1)S(1)} %pad_maximum_fusion.refs_0_), channel_id=1, source_target_pairs={{0,4},{1,5},{2,6},{3,7},{4,0},{5,1},{6,2},{7,3},{8,12},{9,13},{10,... | collective-permute-start | bytes 1572872 | tf_op jit(solution)/shard_map/ppermute | solution.py:18
  36.0 2.9 %shard_map.95 = (bf16[1024,1024]{1,0:T(8,128)(2,1)S(1)}, f32[1,1024]{1,0:T(1,128)S(1)}, bf16[16,1024]{1,0:T(8,128)(2,1)S(1)}) custom-call(s32[1,1024]{1,0:T(1,128)S(1)} %bitcast.7, f32[4]{0:T(128)S(1)} %copy-done.2, f32[4]{0:T(128)S(1)} %copy-done.3, bf16[512,512]{1,0:T(8,128)(2,1)S(1)} %bitcast.6, bf16[512,512]{1,0:T(8,128)(2,1)S(1)} %collective-permute-done.5.other, ...), custom_call_target="tpu_custom_call" | custom-call | flops 1073741824 | bytes 2134016 | tf_op jit(solution)/shard_map/pallas_call | solution.py:246
  38.9 4.5 %collective-permute-done.16.u1 = bf16[128,1024]{1,0:T(8,128)(2,1)S(1)} collective-permute-done((bf16[128,1024]{1,0:T(8,128)(2,1)S(1)}, bf16[128,1024]{1,0:T(8,128)(2,1)S(1)}, u32[]{:S(2)}, u32[]{:S(2)}) %collective-permute-start.16) | collective-permute-done | bytes 262176 | tf_op jit(solution)/shard_map/ppermute | solution.py:18
  43.4 2.6 %collective-permute-done.17.u2 = bf16[128,1024]{1,0:T(8,128)(2,1)S(1)} collective-permute-done((bf16[128,1024]{1,0:T(8,128)(2,1)S(1)}, bf16[128,1024]{1,0:T(8,128)(2,1)S(1)}, u32[]{:S(2)}, u32[]{:S(2)}) %collective-permute-start.17) | collective-permute-done | bytes 262176 | tf_op jit(solution)/shard_map/ppermute | solution.py:18
  46.9 1.3 %collective-permute-start.19 = (bf16[256,512]{1,0:T(8,128)(2,1)S(1)}, bf16[256,512]{1,0:T(8,128)(2,1)S(1)}, u32[]{:S(2)}, u32[]{:S(2)}) collective-permute-start(bf16[256,512]{1,0:T(8,128)(2,1)S(1)} %slice.12), channel_id=1, source_target_pairs={{0,2},{1,3},{2,0},{3,1},{4,6},{5,7},{6,4},{7,5},{8,10},{9,11},{10,... | collective-permute-start | bytes 786440 | tf_op jit(solution)/shard_map/ppermute | solution.py:18
  48.9 1.4 %collective-permute-done.18.theirs = bf16[1024,1024]{1,0:T(8,128)(2,1)S(1)} collective-permute-done((bf16[1024,1024]{1,0:T(8,128)(2,1)S(1)}, bf16[1024,1024]{1,0:T(8,128)(2,1)S(1)}, u32[]{:S(2)}, u32[]{:S(2)}) %collective-permute-start.18) | collective-permute-done | bytes 2097184 | tf_op jit(solution)/shard_map/ppermute | solution.py:18
  50.2 1.8 %shard_map.96.refs_2_ = f32[1024,512]{1,0:T(8,128)S(1)} custom-call(bf16[1024,1024]{1,0:T(8,128)(2,1)S(1)} %get-tuple-element.35.mine, bf16[1024,1024]{1,0:T(8,128)(2,1)S(1)} %collective-permute-done.18.theirs, bf16[512,512]{1,0:T(8,128)(2,1)S(1)} %pad_maximum_fusion.refs_0_, bf16[512,512]{1,0:T(8,128)(2,1)S(1)} %collective-permute-done.14.refs_1_, ...), custom_call_target="tpu_custom_call" | custom-call | flops 1610612736 | bytes 2097152 | tf_op jit(solution)/shard_map/pallas_call | solution.py:264
  52.1 1.5 %shard_map.97.near = f32[1,384]{1,0:T(1,128)S(1)} custom-call(f32[1,1024]{1,0:T(1,128)S(1)} %get-tuple-element.39.step_d, bf16[16,1024]{1,0:T(8,128)(2,1)S(1)} %get-tuple-element.40.parts, bf16[512,1024]{1,0:T(8,128)(2,1)S(1)} %convert_element_type.3.own, bf16[512,1024]{1,0:T(8,128)(2,1)S(1)} %collective-permute-done.21.other, ...), custom_call_target="tpu_custom_call" | custom-call | flops 805306368 | bytes 1536 | tf_op jit(solution)/shard_map/pallas_call | solution.py:271
  53.5 1.6 %collective-permute-done.22.u0 = bf16[128,1024]{1,0:T(8,128)(2,1)S(1)} collective-permute-done((bf16[128,1024]{1,0:T(8,128)(2,1)S(1)}, bf16[128,1024]{1,0:T(8,128)(2,1)S(1)}, u32[]{:S(2)}, u32[]{:S(2)}) %collective-permute-start.22) | collective-permute-done | bytes 262176 | tf_op jit(solution)/shard_map/ppermute | solution.py:18
  57.1 1.5 %collective-permute-start.26 = (f32[3,512]{1,0:T(4,128)S(1)}, f32[3,512]{1,0:T(4,128)S(1)}, u32[]{:S(2)}, u32[]{:S(2)}) collective-permute-start(f32[3,512]{1,0:T(4,128)S(1)} %get-tuple-element.47), channel_id=1, source_target_pairs={{0,24},{1,25},{2,26},{3,27},{4,28},{5,29},{6,30},{7,31},{8,16},{9,... | collective-permute-start | bytes 18440 | tf_op jit(solution)/shard_map/ppermute | solution.py:18
  58.7 1.7 %collective-permute-start.25 = (f32[3,512]{1,0:T(4,128)S(1)}, f32[3,512]{1,0:T(4,128)S(1)}, u32[]{:S(2)}, u32[]{:S(2)}) collective-permute-start(f32[3,512]{1,0:T(4,128)S(1)} %get-tuple-element.47), channel_id=1, source_target_pairs={{0,16},{1,17},{2,18},{3,19},{4,20},{5,21},{6,22},{7,23},{8,24},{9,... | collective-permute-start | bytes 18440 | tf_op jit(solution)/shard_map/ppermute | solution.py:18
  64.1 1.7 %collective-permute-start.29 = (f32[3,512]{1,0:T(4,128)S(1)}, f32[3,512]{1,0:T(4,128)S(1)}, u32[]{:S(2)}, u32[]{:S(2)}) collective-permute-start(f32[3,512]{1,0:T(4,128)S(1)} %maximum_maximum_fusion.1), channel_id=1, source_target_pairs={{0,6},{1,7},{2,4},{3,5},{4,2},{5,3},{6,0},{7,1},{8,14},{9,15},{10,... | collective-permute-start | bytes 18440 | tf_op jit(solution)/shard_map/ppermute | solution.py:18
  66.3 1.2 %collective-permute-start.27 = (f32[3,512]{1,0:T(4,128)S(1)}, f32[3,512]{1,0:T(4,128)S(1)}, u32[]{:S(2)}, u32[]{:S(2)}) collective-permute-start(f32[3,512]{1,0:T(4,128)S(1)} %maximum_maximum_fusion.1), channel_id=1, source_target_pairs={{0,2},{1,3},{2,0},{3,1},{4,6},{5,7},{6,4},{7,5},{8,10},{9,11},{10,... | collective-permute-start | bytes 18440 | tf_op jit(solution)/shard_map/ppermute | solution.py:18
  (73 shorter events, 22.9 us)
Async XLA Ops:
  2.9 10.8 %collective-permute-start.4 = (bf16[64,512]{1,0:T(8,128)(2,1)S(1)}, bf16[64,512]{1,0:T(8,128)(2,1)S(1)}, u32[]{:S(2)}, u32[]{:S(2)}) collective-permute-start(bf16[64,512]{1,0:T(8,128)(2,1)S(1)} %get-tuple-element.51), channel_id=1, source_target_pairs={{0,1},{1,0},{2,3},{3,2},{4,5},{5,4},{6,7},{7,6},{8,9},{9,8},{10,11... | collective-permute-start | bytes 196616 | tf_op jit(solution)/shard_map/ppermute | solution.py:18
  3.0 13.4 %collective-permute-start.5 = (bf16[512,512]{1,0:T(8,128)(2,1)}, bf16[512,512]{1,0:T(8,128)(2,1)S(1)}, u32[]{:S(2)}, u32[]{:S(2)}) collective-permute-start(bf16[512,512]{1,0:T(8,128)(2,1)} %bitcast.5), channel_id=1, source_target_pairs={{0,1},{1,0},{2,3},{3,2},{4,5},{5,4},{6,7},{7,6},{8,9},{9,8},{10,11... | collective-permute-start | bytes 1572872 | tf_op jit(solution)/shard_map/ppermute | solution.py:18
  3.5 6.8 %collective-permute-start.12 = (bf16[32,1024]{1,0:T(8,128)(2,1)}, bf16[32,1024]{1,0:T(8,128)(2,1)S(1)}, u32[]{:S(2)}, u32[]{:S(2)}) collective-permute-start(bf16[32,1024]{1,0:T(8,128)(2,1)} %bitcast.10), channel_id=1, source_target_pairs={{0,2},{1,3},{2,0},{3,1},{4,6},{5,7},{6,4},{7,5},{8,10},{9,11},{10,... | collective-permute-start | bytes 196616 | tf_op jit(solution)/shard_map/ppermute | solution.py:18
  6.1 9.2 %collective-permute-start.1 = (bf16[32,1024]{1,0:T(8,128)(2,1)S(1)}, bf16[32,1024]{1,0:T(8,128)(2,1)S(1)}, u32[]{:S(2)}, u32[]{:S(2)}) collective-permute-start(bf16[32,1024]{1,0:T(8,128)(2,1)S(1)} %pad_maximum_fusion.3), channel_id=1, source_target_pairs={{0,8},{1,9},{2,10},{3,11},{4,12},{5,13},{6,14},{7,15},{8,0},{9,1},... | collective-permute-start | bytes 196616 | tf_op jit(solution)/shard_map/ppermute | solution.py:18
  7.7 7.6 %collective-permute-start.2 = (bf16[32,1024]{1,0:T(8,128)(2,1)S(1)}, bf16[32,1024]{1,0:T(8,128)(2,1)S(1)}, u32[]{:S(2)}, u32[]{:S(2)}) collective-permute-start(bf16[32,1024]{1,0:T(8,128)(2,1)S(1)} %pad_maximum_fusion.3), channel_id=1, source_target_pairs={{0,16},{1,17},{2,18},{3,19},{4,20},{5,21},{6,22},{7,23},{8,24},{9,... | collective-permute-start | bytes 196616 | tf_op jit(solution)/shard_map/ppermute | solution.py:18
  10.3 6.2 %collective-permute-start.3 = (bf16[32,1024]{1,0:T(8,128)(2,1)S(1)}, bf16[32,1024]{1,0:T(8,128)(2,1)S(1)}, u32[]{:S(2)}, u32[]{:S(2)}) collective-permute-start(bf16[32,1024]{1,0:T(8,128)(2,1)S(1)} %pad_maximum_fusion.3), channel_id=1, source_target_pairs={{0,24},{1,25},{2,26},{3,27},{4,28},{5,29},{6,30},{7,31},{8,16},{9,... | collective-permute-start | bytes 196616 | tf_op jit(solution)/shard_map/ppermute | solution.py:18
  13.7 8.5 %collective-permute-start.13 = (bf16[64,1024]{1,0:T(8,128)(2,1)S(1)}, bf16[64,1024]{1,0:T(8,128)(2,1)S(1)}, u32[]{:S(2)}, u32[]{:S(2)}) collective-permute-start(bf16[64,1024]{1,0:T(8,128)(2,1)S(1)} %pad_maximum_fusion.2), channel_id=1, source_target_pairs={{0,4},{1,5},{2,6},{3,7},{4,0},{5,1},{6,2},{7,3},{8,12},{9,13},{10,... | collective-permute-start | bytes 393224 | tf_op jit(solution)/shard_map/ppermute | solution.py:18
  16.5 7.7 %collective-permute-start.10 = (bf16[128,512]{1,0:T(8,128)(2,1)S(1)}, bf16[128,512]{1,0:T(8,128)(2,1)S(1)}, u32[]{:S(2)}, u32[]{:S(2)}) collective-permute-start(bf16[128,512]{1,0:T(8,128)(2,1)S(1)} %maximum_select_fusion), channel_id=1, source_target_pairs={{0,16},{1,17},{2,18},{3,19},{4,20},{5,21},{6,22},{7,23},{8,24},{9,... | collective-permute-start | bytes 393224 | tf_op jit(solution)/shard_map/ppermute | solution.py:18
  18.7 11.0 %collective-permute-start.6 = (bf16[128,1024]{1,0:T(8,128)(2,1)S(1)}, bf16[128,1024]{1,0:T(8,128)(2,1)S(1)}, u32[]{:S(2)}, u32[]{:S(2)}) collective-permute-start(bf16[128,1024]{1,0:T(8,128)(2,1)S(1)} %constant_dynamic-update-slice_fusion.w0), channel_id=1, source_target_pairs={{0,2},{1,3},{2,0},{3,1},{4,6},{5,7},{6,4},{7,5},{8,10},{9,11},{10,... | collective-permute-start | bytes 786440 | tf_op jit(solution)/shard_map/ppermute | solution.py:18
  18.7 11.0 %collective-permute-start.7 = (bf16[128,1024]{1,0:T(8,128)(2,1)S(1)}, bf16[128,1024]{1,0:T(8,128)(2,1)S(1)}, u32[]{:S(2)}, u32[]{:S(2)}) collective-permute-start(bf16[128,1024]{1,0:T(8,128)(2,1)S(1)} %constant_dynamic-update-slice_fusion.w0), channel_id=1, source_target_pairs={{0,4},{1,5},{2,6},{3,7},{4,0},{5,1},{6,2},{7,3},{8,12},{9,13},{10,... | collective-permute-start | bytes 786440 | tf_op jit(solution)/shard_map/ppermute | solution.py:18
  20.2 11.7 %collective-permute-start.8 = (bf16[128,1024]{1,0:T(8,128)(2,1)S(1)}, bf16[128,1024]{1,0:T(8,128)(2,1)S(1)}, u32[]{:S(2)}, u32[]{:S(2)}) collective-permute-start(bf16[128,1024]{1,0:T(8,128)(2,1)S(1)} %constant_dynamic-update-slice_fusion.w0), channel_id=1, source_target_pairs={{0,6},{1,7},{2,4},{3,5},{4,2},{5,3},{6,0},{7,1},{8,14},{9,15},{10,... | collective-permute-start | bytes 786440 | tf_op jit(solution)/shard_map/ppermute | solution.py:18
  22.2 6.0 %collective-permute-start.9 = (bf16[128,512]{1,0:T(8,128)(2,1)S(1)}, bf16[128,512]{1,0:T(8,128)(2,1)S(1)}, u32[]{:S(2)}, u32[]{:S(2)}) collective-permute-start(bf16[128,512]{1,0:T(8,128)(2,1)S(1)} %maximum_select_fusion), channel_id=1, source_target_pairs={{0,8},{1,9},{2,10},{3,11},{4,12},{5,13},{6,14},{7,15},{8,0},{9,1},... | collective-permute-start | bytes 393224 | tf_op jit(solution)/shard_map/ppermute | solution.py:18
  24.2 5.4 %collective-permute-start.11 = (bf16[128,512]{1,0:T(8,128)(2,1)S(1)}, bf16[128,512]{1,0:T(8,128)(2,1)S(1)}, u32[]{:S(2)}, u32[]{:S(2)}) collective-permute-start(bf16[128,512]{1,0:T(8,128)(2,1)S(1)} %collective-permute-done.10), channel_id=1, source_target_pairs={{0,8},{1,9},{2,10},{3,11},{4,12},{5,13},{6,14},{7,15},{8,0},{9,1},... | collective-permute-start | bytes 393224 | tf_op jit(solution)/shard_map/ppermute | solution.py:18
  31.9 14.1 %collective-permute-start.14 = (bf16[512,512]{1,0:T(8,128)(2,1)S(1)}, bf16[512,512]{1,0:T(8,128)(2,1)S(1)}, u32[]{:S(2)}, u32[]{:S(2)}) collective-permute-start(bf16[512,512]{1,0:T(8,128)(2,1)S(1)} %pad_maximum_fusion.refs_0_), channel_id=1, source_target_pairs={{0,2},{1,3},{2,0},{3,1},{4,6},{5,7},{6,4},{7,5},{8,10},{9,11},{10,... | collective-permute-start | bytes 1572872 | tf_op jit(solution)/shard_map/ppermute | solution.py:18
  32.7 13.3 %collective-permute-start.15 = (bf16[512,512]{1,0:T(8,128)(2,1)S(1)}, bf16[512,512]{1,0:T(8,128)(2,1)S(1)}, u32[]{:S(2)}, u32[]{:S(2)}) collective-permute-start(bf16[512,512]{1,0:T(8,128)(2,1)S(1)} %pad_maximum_fusion.refs_0_), channel_id=1, source_target_pairs={{0,4},{1,5},{2,6},{3,7},{4,0},{5,1},{6,2},{7,3},{8,12},{9,13},{10,... | collective-permute-start | bytes 1572872 | tf_op jit(solution)/shard_map/ppermute | solution.py:18
  34.2 9.2 %collective-permute-start.16 = (bf16[128,1024]{1,0:T(8,128)(2,1)S(1)}, bf16[128,1024]{1,0:T(8,128)(2,1)S(1)}, u32[]{:S(2)}, u32[]{:S(2)}) collective-permute-start(bf16[128,1024]{1,0:T(8,128)(2,1)S(1)} %pad_maximum_fusion.1.u0), channel_id=1, source_target_pairs={{0,8},{1,9},{2,10},{3,11},{4,12},{5,13},{6,14},{7,15},{8,0},{9,1},... | collective-permute-start | bytes 786440 | tf_op jit(solution)/shard_map/ppermute | solution.py:18
  35.1 10.9 %collective-permute-start.17 = (bf16[128,1024]{1,0:T(8,128)(2,1)S(1)}, bf16[128,1024]{1,0:T(8,128)(2,1)S(1)}, u32[]{:S(2)}, u32[]{:S(2)}) collective-permute-start(bf16[128,1024]{1,0:T(8,128)(2,1)S(1)} %pad_maximum_fusion.1.u0), channel_id=1, source_target_pairs={{0,16},{1,17},{2,18},{3,19},{4,20},{5,21},{6,22},{7,23},{8,24},{9,... | collective-permute-start | bytes 786440 | tf_op jit(solution)/shard_map/ppermute | solution.py:18
  46.3 5.7 %collective-permute-start.21 = (bf16[512,1024]{1,0:T(8,128)(2,1)S(1)}, bf16[512,1024]{1,0:T(8,128)(2,1)S(1)}, u32[]{:S(2)}, u32[]{:S(2)}) collective-permute-start(bf16[512,1024]{1,0:T(8,128)(2,1)S(1)} %convert_element_type.3.own), channel_id=1, source_target_pairs={{0,1},{1,0},{2,3},{3,2},{4,5},{5,4},{6,7},{7,6},{8,9},{9,8},{10,11... | collective-permute-start | bytes 3145736 | tf_op jit(solution)/shard_map/ppermute | solution.py:18
  46.9 8.3 %collective-permute-start.22 = (bf16[128,1024]{1,0:T(8,128)(2,1)S(1)}, bf16[128,1024]{1,0:T(8,128)(2,1)S(1)}, u32[]{:S(2)}, u32[]{:S(2)}) collective-permute-start(bf16[128,1024]{1,0:T(8,128)(2,1)S(1)} %collective-permute-done.17.u2), channel_id=1, source_target_pairs={{0,8},{1,9},{2,10},{3,11},{4,12},{5,13},{6,14},{7,15},{8,0},{9,1},... | collective-permute-start | bytes 786440 | tf_op jit(solution)/shard_map/ppermute | solution.py:18
  46.9 9.0 %collective-permute-start.19 = (bf16[256,512]{1,0:T(8,128)(2,1)S(1)}, bf16[256,512]{1,0:T(8,128)(2,1)S(1)}, u32[]{:S(2)}, u32[]{:S(2)}) collective-permute-start(bf16[256,512]{1,0:T(8,128)(2,1)S(1)} %slice.12), channel_id=1, source_target_pairs={{0,2},{1,3},{2,0},{3,1},{4,6},{5,7},{6,4},{7,5},{8,10},{9,11},{10,... | collective-permute-start | bytes 786440 | tf_op jit(solution)/shard_map/ppermute | solution.py:18
  48.2 8.1 %collective-permute-start.20 = (bf16[256,512]{1,0:T(8,128)(2,1)S(1)}, bf16[256,512]{1,0:T(8,128)(2,1)S(1)}, u32[]{:S(2)}, u32[]{:S(2)}) collective-permute-start(bf16[256,512]{1,0:T(8,128)(2,1)S(1)} %slice.13), channel_id=1, source_target_pairs={{0,4},{1,5},{2,6},{3,7},{4,0},{5,1},{6,2},{7,3},{8,12},{9,13},{10,... | collective-permute-start | bytes 786440 | tf_op jit(solution)/shard_map/ppermute | solution.py:18
  57.1 14.2 %collective-permute-start.23 = (f32[512,512]{1,0:T(8,128)S(1)}, f32[512,512]{1,0:T(8,128)S(1)}, u32[]{:S(2)}, u32[]{:S(2)}) collective-permute-start(f32[512,512]{1,0:T(8,128)S(1)} %get-tuple-element.46), channel_id=1, source_target_pairs={{0,1},{1,0},{2,3},{3,2},{4,5},{5,4},{6,7},{7,6},{8,9},{9,8},{10,11... | collective-permute-start | bytes 3145736 | tf_op jit(solution)/shard_map/ppermute | solution.py:18
  57.1 5.6 %collective-permute-start.26 = (f32[3,512]{1,0:T(4,128)S(1)}, f32[3,512]{1,0:T(4,128)S(1)}, u32[]{:S(2)}, u32[]{:S(2)}) collective-permute-start(f32[3,512]{1,0:T(4,128)S(1)} %get-tuple-element.47), channel_id=1, source_target_pairs={{0,24},{1,25},{2,26},{3,27},{4,28},{5,29},{6,30},{7,31},{8,16},{9,... | collective-permute-start | bytes 18440 | tf_op jit(solution)/shard_map/ppermute | solution.py:18
  58.7 4.5 %collective-permute-start.25 = (f32[3,512]{1,0:T(4,128)S(1)}, f32[3,512]{1,0:T(4,128)S(1)}, u32[]{:S(2)}, u32[]{:S(2)}) collective-permute-start(f32[3,512]{1,0:T(4,128)S(1)} %get-tuple-element.47), channel_id=1, source_target_pairs={{0,16},{1,17},{2,18},{3,19},{4,20},{5,21},{6,22},{7,23},{8,24},{9,... | collective-permute-start | bytes 18440 | tf_op jit(solution)/shard_map/ppermute | solution.py:18
  (12 other events, 183.4 us)

commit v7 on v6

--- a/solution.py
+++ b/solution.py
@@ -223,6 +223,7 @@
 
     in_rows = cat(half_columns(w_in, core), move(half_columns(w_in, 1 - core), 1))
     in_column = cat(in_rows, *(move(in_rows, k) for k in (8, 16, 24)))
+    w_out, in_rows = lax.optimization_barrier((w_out, in_rows))
     here, there = half_columns(w_out, core), move(half_columns(w_out, 1 - core), 1)
     out_rows = jnp.where(core == 0, cat(here, there), cat(there, here))
     user_pair = cat(users[0], move(users[0], 2))

time: 72.7 us -> 71.8 us (0.988)
  starting transfers between devices: 33.3 us -> 31 us
  waiting for transfers between devices: 24.9 us -> 26.4 us
    ppermute x31, starting transfers between devices: 33.3 us -> 31 us  [swap(): return lax.ppermute(x, axis, [(i, i ^ k) for i in range(n)])]
    ppermute x31, waiting for transfers between devices: 24.9 us -> 26.4 us  [swap(): return lax.ppermute(x, axis, [(i, i ^ k) for i in range(n)])]
  transfers between devices with their start and end apart: 31 -> 31, of which waited for: 17 -> 18; matrix products, arithmetic and copies ran while one was open for 5% -> 5% of each run, Pallas kernels for 10% -> 10%
where the time goes in v7:
time: 71.8 us; the launch traced here: 71.6 us
  starting transfers between devices  31 us (43%)
  waiting for transfers between devices  26.4 us (37%)
  Pallas kernels  8.89 us (12%)
  local copies, waits for them, and re-layouts  2.39 us (3%)
  other arithmetic  2.03 us (3%)
  between operations  0.91 us (1%)
    ppermute x31, starting transfers between devices, swap(): return lax.ppermute(x, axis, [(i, i ^ k) for i in range(n)])  31 us
    ppermute x31, waiting for transfers between devices, swap(): return lax.ppermute(x, axis, [(i, i ^ k) for i in range(n)])  26.4 us
    pallas_call x1, Pallas kernels, by_permutes(): call(functools.partial(hidden_kernel, n), (shape((2 * count, wide), BF16)...  2.89 us
    pallas_call x1, Pallas kernels, by_permutes(): call(functools.partial(first_embed_kernel, keys[:3]), shape((2 * count, w...  1.83 us
    concatenate x4, other arithmetic, by_permutes(): cat = lambda *parts: jnp.concatenate(parts, axis=0)  1.75 us
    pallas_call x1, Pallas kernels, by_permutes(): call(near_score_kernel, shape((1, 3 * members), F32), [VMEM] * 7, 3 * sco...  1.47 us
  transfers between devices with their start and end apart: 31, of which 18 were waited for; matrix products, arithmetic and copies ran while one was open for 5% of the time, Pallas kernels for 10%

profile of v7, /device:TPU:0, one launch (start us, length us, event | category | flops | bytes accessed | tf_op | source)
XLA Modules:
  0.0 71.6 jit_solution(1826505128387352371)
XLA Ops:
  2.1 2.9 %collective-permute-start.12 = (bf16[32,1024]{1,0:T(8,128)(2,1)}, bf16[32,1024]{1,0:T(8,128)(2,1)S(1)}, u32[]{:S(2)}, u32[]{:S(2)}) collective-permute-start(bf16[32,1024]{1,0:T(8,128)(2,1)} %bitcast.10), channel_id=1, source_target_pairs={{0,2},{1,3},{2,0},{3,1},{4,6},{5,7},{6,4},{7,5},{8,10},{9,11},{10,... | collective-permute-start | bytes 196616 | tf_op jit(solution)/shard_map/ppermute | solution.py:18
  5.0 1.6 %collective-permute-start.1 = (bf16[32,1024]{1,0:T(8,128)(2,1)S(1)}, bf16[32,1024]{1,0:T(8,128)(2,1)S(1)}, u32[]{:S(2)}, u32[]{:S(2)}) collective-permute-start(bf16[32,1024]{1,0:T(8,128)(2,1)S(1)} %pad_maximum_fusion.3), channel_id=1, source_target_pairs={{0,8},{1,9},{2,10},{3,11},{4,12},{5,13},{6,14},{7,15},{8,0},{9,1},... | collective-permute-start | bytes 196616 | tf_op jit(solution)/shard_map/ppermute | solution.py:18
  6.7 2.6 %collective-permute-start.2 = (bf16[32,1024]{1,0:T(8,128)(2,1)S(1)}, bf16[32,1024]{1,0:T(8,128)(2,1)S(1)}, u32[]{:S(2)}, u32[]{:S(2)}) collective-permute-start(bf16[32,1024]{1,0:T(8,128)(2,1)S(1)} %pad_maximum_fusion.3), channel_id=1, source_target_pairs={{0,16},{1,17},{2,18},{3,19},{4,20},{5,21},{6,22},{7,23},{8,24},{9,... | collective-permute-start | bytes 196616 | tf_op jit(solution)/shard_map/ppermute | solution.py:18
  11.3 1.6 %collective-permute-start.13 = (bf16[64,1024]{1,0:T(8,128)(2,1)S(1)}, bf16[64,1024]{1,0:T(8,128)(2,1)S(1)}, u32[]{:S(2)}, u32[]{:S(2)}) collective-permute-start(bf16[64,1024]{1,0:T(8,128)(2,1)S(1)} %pad_maximum_fusion.2), channel_id=1, source_target_pairs={{0,4},{1,5},{2,6},{3,7},{4,0},{5,1},{6,2},{7,3},{8,12},{9,13},{10,... | collective-permute-start | bytes 393224 | tf_op jit(solution)/shard_map/ppermute | solution.py:18
  13.9 1.4 %collective-permute-done.3 = bf16[32,1024]{1,0:T(8,128)(2,1)S(1)} collective-permute-done((bf16[32,1024]{1,0:T(8,128)(2,1)S(1)}, bf16[32,1024]{1,0:T(8,128)(2,1)S(1)}, u32[]{:S(2)}, u32[]{:S(2)}) %collective-permute-start.3) | collective-permute-done | bytes 65568 | tf_op jit(solution)/shard_map/ppermute | solution.py:18
  15.4 1.6 %collective-permute-start.10 = (bf16[128,512]{1,0:T(8,128)(2,1)S(1)}, bf16[128,512]{1,0:T(8,128)(2,1)S(1)}, u32[]{:S(2)}, u32[]{:S(2)}) collective-permute-start(bf16[128,512]{1,0:T(8,128)(2,1)S(1)} %maximum_select_fusion), channel_id=1, source_target_pairs={{0,16},{1,17},{2,18},{3,19},{4,20},{5,21},{6,22},{7,23},{8,24},{9,... | collective-permute-start | bytes 393224 | tf_op jit(solution)/shard_map/ppermute | solution.py:18
  18.0 1.5 %collective-permute-start.7 = (bf16[128,1024]{1,0:T(8,128)(2,1)S(1)}, bf16[128,1024]{1,0:T(8,128)(2,1)S(1)}, u32[]{:S(2)}, u32[]{:S(2)}) collective-permute-start(bf16[128,1024]{1,0:T(8,128)(2,1)S(1)} %constant_dynamic-update-slice_fusion.w0), channel_id=1, source_target_pairs={{0,4},{1,5},{2,6},{3,7},{4,0},{5,1},{6,2},{7,3},{8,12},{9,13},{10,... | collective-permute-start | bytes 786440 | tf_op jit(solution)/shard_map/ppermute | solution.py:18
  21.3 1.6 %collective-permute-done.10 = bf16[128,512]{1,0:T(8,128)(2,1)S(1)} collective-permute-done((bf16[128,512]{1,0:T(8,128)(2,1)S(1)}, bf16[128,512]{1,0:T(8,128)(2,1)S(1)}, u32[]{:S(2)}, u32[]{:S(2)}) %collective-permute-start.10) | collective-permute-done | bytes 131104 | tf_op jit(solution)/shard_map/ppermute | solution.py:18
  23.8 2.8 %collective-permute-done.9 = bf16[128,512]{1,0:T(8,128)(2,1)S(1)} collective-permute-done((bf16[128,512]{1,0:T(8,128)(2,1)S(1)}, bf16[128,512]{1,0:T(8,128)(2,1)S(1)}, u32[]{:S(2)}, u32[]{:S(2)}) %collective-permute-start.9) | collective-permute-done | bytes 131104 | tf_op jit(solution)/shard_map/ppermute | solution.py:18
  26.5 1.8 %collective-permute-done.11 = bf16[128,512]{1,0:T(8,128)(2,1)S(1)} collective-permute-done((bf16[128,512]{1,0:T(8,128)(2,1)S(1)}, bf16[128,512]{1,0:T(8,128)(2,1)S(1)}, u32[]{:S(2)}, u32[]{:S(2)}) %collective-permute-start.11) | collective-permute-done | bytes 131104 | tf_op jit(solution)/shard_map/ppermute | solution.py:18
  31.2 1.2 %collective-permute-start.15 = (bf16[512,512]{1,0:T(8,128)(2,1)S(1)}, bf16[512,512]{1,0:T(8,128)(2,1)S(1)}, u32[]{:S(2)}, u32[]{:S(2)}) collective-permute-start(bf16[512,512]{1,0:T(8,128)(2,1)S(1)} %pad_maximum_fusion.refs_0_), channel_id=1, source_target_pairs={{0,4},{1,5},{2,6},{3,7},{4,0},{5,1},{6,2},{7,3},{8,12},{9,13},{10,... | collective-permute-start | bytes 1572872 | tf_op jit(solution)/shard_map/ppermute | solution.py:18
  33.3 1.5 %collective-permute-start.17 = (bf16[128,1024]{1,0:T(8,128)(2,1)S(1)}, bf16[128,1024]{1,0:T(8,128)(2,1)S(1)}, u32[]{:S(2)}, u32[]{:S(2)}) collective-permute-start(bf16[128,1024]{1,0:T(8,128)(2,1)S(1)} %pad_maximum_fusion.1.u0), channel_id=1, source_target_pairs={{0,16},{1,17},{2,18},{3,19},{4,20},{5,21},{6,22},{7,23},{8,24},{9,... | collective-permute-start | bytes 786440 | tf_op jit(solution)/shard_map/ppermute | solution.py:18
  34.9 2.9 %shard_map.95 = (bf16[1024,1024]{1,0:T(8,128)(2,1)S(1)}, f32[1,1024]{1,0:T(1,128)S(1)}, bf16[16,1024]{1,0:T(8,128)(2,1)S(1)}) custom-call(s32[1,1024]{1,0:T(1,128)S(1)} %bitcast.7, f32[4]{0:T(128)S(1)} %copy-done.2, f32[4]{0:T(128)S(1)} %copy-done.3, bf16[512,512]{1,0:T(8,128)(2,1)S(1)} %bitcast.6, bf16[512,512]{1,0:T(8,128)(2,1)S(1)} %collective-permute-done.5.other, ...), custom_call_target="tpu_custom_call" | custom-call | flops 1073741824 | bytes 2134016 | tf_op jit(solution)/shard_map/pallas_call | solution.py:247
  37.8 3.9 %collective-permute-done.16.u1 = bf16[128,1024]{1,0:T(8,128)(2,1)S(1)} collective-permute-done((bf16[128,1024]{1,0:T(8,128)(2,1)S(1)}, bf16[128,1024]{1,0:T(8,128)(2,1)S(1)}, u32[]{:S(2)}, u32[]{:S(2)}) %collective-permute-start.16) | collective-permute-done | bytes 262176 | tf_op jit(solution)/shard_map/ppermute | solution.py:18
  41.7 3.6 %collective-permute-done.17.u2 = bf16[128,1024]{1,0:T(8,128)(2,1)S(1)} collective-permute-done((bf16[128,1024]{1,0:T(8,128)(2,1)S(1)}, bf16[128,1024]{1,0:T(8,128)(2,1)S(1)}, u32[]{:S(2)}, u32[]{:S(2)}) %collective-permute-start.17) | collective-permute-done | bytes 262176 | tf_op jit(solution)/shard_map/ppermute | solution.py:18
  46.1 1.8 %collective-permute-start.19 = (bf16[256,512]{1,0:T(8,128)(2,1)S(1)}, bf16[256,512]{1,0:T(8,128)(2,1)S(1)}, u32[]{:S(2)}, u32[]{:S(2)}) collective-permute-start(bf16[256,512]{1,0:T(8,128)(2,1)S(1)} %slice.12), channel_id=1, source_target_pairs={{0,2},{1,3},{2,0},{3,1},{4,6},{5,7},{6,4},{7,5},{8,10},{9,11},{10,... | collective-permute-start | bytes 786440 | tf_op jit(solution)/shard_map/ppermute | solution.py:18
  49.4 1.8 %shard_map.96.refs_2_ = f32[1024,512]{1,0:T(8,128)S(1)} custom-call(bf16[1024,1024]{1,0:T(8,128)(2,1)S(1)} %get-tuple-element.37.mine, bf16[1024,1024]{1,0:T(8,128)(2,1)S(1)} %collective-permute-done.18.theirs, bf16[512,512]{1,0:T(8,128)(2,1)S(1)} %pad_maximum_fusion.refs_0_, bf16[512,512]{1,0:T(8,128)(2,1)S(1)} %collective-permute-done.14.refs_1_, ...), custom_call_target="tpu_custom_call" | custom-call | flops 1610612736 | bytes 2097152 | tf_op jit(solution)/shard_map/pallas_call | solution.py:265
  51.2 1.5 %shard_map.97.near = f32[1,384]{1,0:T(1,128)S(1)} custom-call(f32[1,1024]{1,0:T(1,128)S(1)} %get-tuple-element.41.step_d, bf16[16,1024]{1,0:T(8,128)(2,1)S(1)} %get-tuple-element.42.parts, bf16[512,1024]{1,0:T(8,128)(2,1)S(1)} %convert_element_type.3.own, bf16[512,1024]{1,0:T(8,128)(2,1)S(1)} %collective-permute-done.21.other, ...), custom_call_target="tpu_custom_call" | custom-call | flops 805306368 | bytes 1536 | tf_op jit(solution)/shard_map/pallas_call | solution.py:272
  52.7 1.6 %collective-permute-done.22.u0 = bf16[128,1024]{1,0:T(8,128)(2,1)S(1)} collective-permute-done((bf16[128,1024]{1,0:T(8,128)(2,1)S(1)}, bf16[128,1024]{1,0:T(8,128)(2,1)S(1)}, u32[]{:S(2)}, u32[]{:S(2)}) %collective-permute-start.22) | collective-permute-done | bytes 262176 | tf_op jit(solution)/shard_map/ppermute | solution.py:18
  56.8 1.6 %collective-permute-start.26 = (f32[3,512]{1,0:T(4,128)S(1)}, f32[3,512]{1,0:T(4,128)S(1)}, u32[]{:S(2)}, u32[]{:S(2)}) collective-permute-start(f32[3,512]{1,0:T(4,128)S(1)} %get-tuple-element.49), channel_id=1, source_target_pairs={{0,24},{1,25},{2,26},{3,27},{4,28},{5,29},{6,30},{7,31},{8,16},{9,... | collective-permute-start | bytes 18440 | tf_op jit(solution)/shard_map/ppermute | solution.py:18
  58.4 1.7 %collective-permute-start.25 = (f32[3,512]{1,0:T(4,128)S(1)}, f32[3,512]{1,0:T(4,128)S(1)}, u32[]{:S(2)}, u32[]{:S(2)}) collective-permute-start(f32[3,512]{1,0:T(4,128)S(1)} %get-tuple-element.49), channel_id=1, source_target_pairs={{0,16},{1,17},{2,18},{3,19},{4,20},{5,21},{6,22},{7,23},{8,24},{9,... | collective-permute-start | bytes 18440 | tf_op jit(solution)/shard_map/ppermute | solution.py:18
  60.1 1.2 %collective-permute-start.24 = (f32[3,512]{1,0:T(4,128)S(1)}, f32[3,512]{1,0:T(4,128)S(1)}, u32[]{:S(2)}, u32[]{:S(2)}) collective-permute-start(f32[3,512]{1,0:T(4,128)S(1)} %get-tuple-element.49), channel_id=1, source_target_pairs={{0,8},{1,9},{2,10},{3,11},{4,12},{5,13},{6,14},{7,15},{8,0},{9,1},... | collective-permute-start | bytes 18440 | tf_op jit(solution)/shard_map/ppermute | solution.py:18
  64.2 1.3 %collective-permute-start.28 = (f32[3,512]{1,0:T(4,128)S(1)}, f32[3,512]{1,0:T(4,128)S(1)}, u32[]{:S(2)}, u32[]{:S(2)}) collective-permute-start(f32[3,512]{1,0:T(4,128)S(1)} %maximum_maximum_fusion.1), channel_id=1, source_target_pairs={{0,4},{1,5},{2,6},{3,7},{4,0},{5,1},{6,2},{7,3},{8,12},{9,13},{10,... | collective-permute-start | bytes 18440 | tf_op jit(solution)/shard_map/ppermute | solution.py:18
  65.5 1.7 %collective-permute-start.27 = (f32[3,512]{1,0:T(4,128)S(1)}, f32[3,512]{1,0:T(4,128)S(1)}, u32[]{:S(2)}, u32[]{:S(2)}) collective-permute-start(f32[3,512]{1,0:T(4,128)S(1)} %maximum_maximum_fusion.1), channel_id=1, source_target_pairs={{0,2},{1,3},{2,0},{3,1},{4,6},{5,7},{6,4},{7,5},{8,10},{9,11},{10,... | collective-permute-start | bytes 18440 | tf_op jit(solution)/shard_map/ppermute | solution.py:18
  (73 shorter events, 23.9 us)
Async XLA Ops:
  2.0 13.4 %collective-permute-start.5 = (bf16[512,512]{1,0:T(8,128)(2,1)}, bf16[512,512]{1,0:T(8,128)(2,1)S(1)}, u32[]{:S(2)}, u32[]{:S(2)}) collective-permute-start(bf16[512,512]{1,0:T(8,128)(2,1)} %bitcast.5), channel_id=1, source_target_pairs={{0,1},{1,0},{2,3},{3,2},{4,5},{5,4},{6,7},{7,6},{8,9},{9,8},{10,11... | collective-permute-start | bytes 1572872 | tf_op jit(solution)/shard_map/ppermute | solution.py:18
  2.1 8.3 %collective-permute-start.12 = (bf16[32,1024]{1,0:T(8,128)(2,1)}, bf16[32,1024]{1,0:T(8,128)(2,1)S(1)}, u32[]{:S(2)}, u32[]{:S(2)}) collective-permute-start(bf16[32,1024]{1,0:T(8,128)(2,1)} %bitcast.10), channel_id=1, source_target_pairs={{0,2},{1,3},{2,0},{3,1},{4,6},{5,7},{6,4},{7,5},{8,10},{9,11},{10,... | collective-permute-start | bytes 196616 | tf_op jit(solution)/shard_map/ppermute | solution.py:18
  5.0 6.3 %collective-permute-start.1 = (bf16[32,1024]{1,0:T(8,128)(2,1)S(1)}, bf16[32,1024]{1,0:T(8,128)(2,1)S(1)}, u32[]{:S(2)}, u32[]{:S(2)}) collective-permute-start(bf16[32,1024]{1,0:T(8,128)(2,1)S(1)} %pad_maximum_fusion.3), channel_id=1, source_target_pairs={{0,8},{1,9},{2,10},{3,11},{4,12},{5,13},{6,14},{7,15},{8,0},{9,1},... | collective-permute-start | bytes 196616 | tf_op jit(solution)/shard_map/ppermute | solution.py:18
  6.7 7.2 %collective-permute-start.2 = (bf16[32,1024]{1,0:T(8,128)(2,1)S(1)}, bf16[32,1024]{1,0:T(8,128)(2,1)S(1)}, u32[]{:S(2)}, u32[]{:S(2)}) collective-permute-start(bf16[32,1024]{1,0:T(8,128)(2,1)S(1)} %pad_maximum_fusion.3), channel_id=1, source_target_pairs={{0,16},{1,17},{2,18},{3,19},{4,20},{5,21},{6,22},{7,23},{8,24},{9,... | collective-permute-start | bytes 196616 | tf_op jit(solution)/shard_map/ppermute | solution.py:18
  9.3 6.1 %collective-permute-start.3 = (bf16[32,1024]{1,0:T(8,128)(2,1)S(1)}, bf16[32,1024]{1,0:T(8,128)(2,1)S(1)}, u32[]{:S(2)}, u32[]{:S(2)}) collective-permute-start(bf16[32,1024]{1,0:T(8,128)(2,1)S(1)} %pad_maximum_fusion.3), channel_id=1, source_target_pairs={{0,24},{1,25},{2,26},{3,27},{4,28},{5,29},{6,30},{7,31},{8,16},{9,... | collective-permute-start | bytes 196616 | tf_op jit(solution)/shard_map/ppermute | solution.py:18
  10.4 4.9 %collective-permute-start.4 = (bf16[64,512]{1,0:T(8,128)(2,1)S(1)}, bf16[64,512]{1,0:T(8,128)(2,1)S(1)}, u32[]{:S(2)}, u32[]{:S(2)}) collective-permute-start(bf16[64,512]{1,0:T(8,128)(2,1)S(1)} %get-tuple-element.53), channel_id=1, source_target_pairs={{0,1},{1,0},{2,3},{3,2},{4,5},{5,4},{6,7},{7,6},{8,9},{9,8},{10,11... | collective-permute-start | bytes 196616 | tf_op jit(solution)/shard_map/ppermute | solution.py:18
  11.3 9.2 %collective-permute-start.13 = (bf16[64,1024]{1,0:T(8,128)(2,1)S(1)}, bf16[64,1024]{1,0:T(8,128)(2,1)S(1)}, u32[]{:S(2)}, u32[]{:S(2)}) collective-permute-start(bf16[64,1024]{1,0:T(8,128)(2,1)S(1)} %pad_maximum_fusion.2), channel_id=1, source_target_pairs={{0,4},{1,5},{2,6},{3,7},{4,0},{5,1},{6,2},{7,3},{8,12},{9,13},{10,... | collective-permute-start | bytes 393224 | tf_op jit(solution)/shard_map/ppermute | solution.py:18
  15.4 7.5 %collective-permute-start.10 = (bf16[128,512]{1,0:T(8,128)(2,1)S(1)}, bf16[128,512]{1,0:T(8,128)(2,1)S(1)}, u32[]{:S(2)}, u32[]{:S(2)}) collective-permute-start(bf16[128,512]{1,0:T(8,128)(2,1)S(1)} %maximum_select_fusion), channel_id=1, source_target_pairs={{0,16},{1,17},{2,18},{3,19},{4,20},{5,21},{6,22},{7,23},{8,24},{9,... | collective-permute-start | bytes 393224 | tf_op jit(solution)/shard_map/ppermute | solution.py:18
  17.0 11.4 %collective-permute-start.6 = (bf16[128,1024]{1,0:T(8,128)(2,1)S(1)}, bf16[128,1024]{1,0:T(8,128)(2,1)S(1)}, u32[]{:S(2)}, u32[]{:S(2)}) collective-permute-start(bf16[128,1024]{1,0:T(8,128)(2,1)S(1)} %constant_dynamic-update-slice_fusion.w0), channel_id=1, source_target_pairs={{0,2},{1,3},{2,0},{3,1},{4,6},{5,7},{6,4},{7,5},{8,10},{9,11},{10,... | collective-permute-start | bytes 786440 | tf_op jit(solution)/shard_map/ppermute | solution.py:18
  18.0 11.0 %collective-permute-start.7 = (bf16[128,1024]{1,0:T(8,128)(2,1)S(1)}, bf16[128,1024]{1,0:T(8,128)(2,1)S(1)}, u32[]{:S(2)}, u32[]{:S(2)}) collective-permute-start(bf16[128,1024]{1,0:T(8,128)(2,1)S(1)} %constant_dynamic-update-slice_fusion.w0), channel_id=1, source_target_pairs={{0,4},{1,5},{2,6},{3,7},{4,0},{5,1},{6,2},{7,3},{8,12},{9,13},{10,... | collective-permute-start | bytes 786440 | tf_op jit(solution)/shard_map/ppermute | solution.py:18
  19.5 10.6 %collective-permute-start.8 = (bf16[128,1024]{1,0:T(8,128)(2,1)S(1)}, bf16[128,1024]{1,0:T(8,128)(2,1)S(1)}, u32[]{:S(2)}, u32[]{:S(2)}) collective-permute-start(bf16[128,1024]{1,0:T(8,128)(2,1)S(1)} %constant_dynamic-update-slice_fusion.w0), channel_id=1, source_target_pairs={{0,6},{1,7},{2,4},{3,5},{4,2},{5,3},{6,0},{7,1},{8,14},{9,15},{10,... | collective-permute-start | bytes 786440 | tf_op jit(solution)/shard_map/ppermute | solution.py:18
  20.5 6.0 %collective-permute-start.9 = (bf16[128,512]{1,0:T(8,128)(2,1)S(1)}, bf16[128,512]{1,0:T(8,128)(2,1)S(1)}, u32[]{:S(2)}, u32[]{:S(2)}) collective-permute-start(bf16[128,512]{1,0:T(8,128)(2,1)S(1)} %maximum_select_fusion), channel_id=1, source_target_pairs={{0,8},{1,9},{2,10},{3,11},{4,12},{5,13},{6,14},{7,15},{8,0},{9,1},... | collective-permute-start | bytes 393224 | tf_op jit(solution)/shard_map/ppermute | solution.py:18
  22.9 5.5 %collective-permute-start.11 = (bf16[128,512]{1,0:T(8,128)(2,1)S(1)}, bf16[128,512]{1,0:T(8,128)(2,1)S(1)}, u32[]{:S(2)}, u32[]{:S(2)}) collective-permute-start(bf16[128,512]{1,0:T(8,128)(2,1)S(1)} %collective-permute-done.10), channel_id=1, source_target_pairs={{0,8},{1,9},{2,10},{3,11},{4,12},{5,13},{6,14},{7,15},{8,0},{9,1},... | collective-permute-start | bytes 393224 | tf_op jit(solution)/shard_map/ppermute | solution.py:18
  30.2 15.1 %collective-permute-start.14 = (bf16[512,512]{1,0:T(8,128)(2,1)S(1)}, bf16[512,512]{1,0:T(8,128)(2,1)S(1)}, u32[]{:S(2)}, u32[]{:S(2)}) collective-permute-start(bf16[512,512]{1,0:T(8,128)(2,1)S(1)} %pad_maximum_fusion.refs_0_), channel_id=1, source_target_pairs={{0,2},{1,3},{2,0},{3,1},{4,6},{5,7},{6,4},{7,5},{8,10},{9,11},{10,... | collective-permute-start | bytes 1572872 | tf_op jit(solution)/shard_map/ppermute | solution.py:18
  31.2 14.0 %collective-permute-start.15 = (bf16[512,512]{1,0:T(8,128)(2,1)S(1)}, bf16[512,512]{1,0:T(8,128)(2,1)S(1)}, u32[]{:S(2)}, u32[]{:S(2)}) collective-permute-start(bf16[512,512]{1,0:T(8,128)(2,1)S(1)} %pad_maximum_fusion.refs_0_), channel_id=1, source_target_pairs={{0,4},{1,5},{2,6},{3,7},{4,0},{5,1},{6,2},{7,3},{8,12},{9,13},{10,... | collective-permute-start | bytes 1572872 | tf_op jit(solution)/shard_map/ppermute | solution.py:18
  32.5 9.2 %collective-permute-start.16 = (bf16[128,1024]{1,0:T(8,128)(2,1)S(1)}, bf16[128,1024]{1,0:T(8,128)(2,1)S(1)}, u32[]{:S(2)}, u32[]{:S(2)}) collective-permute-start(bf16[128,1024]{1,0:T(8,128)(2,1)S(1)} %pad_maximum_fusion.1.u0), channel_id=1, source_target_pairs={{0,8},{1,9},{2,10},{3,11},{4,12},{5,13},{6,14},{7,15},{8,0},{9,1},... | collective-permute-start | bytes 786440 | tf_op jit(solution)/shard_map/ppermute | solution.py:18
  33.3 11.9 %collective-permute-start.17 = (bf16[128,1024]{1,0:T(8,128)(2,1)S(1)}, bf16[128,1024]{1,0:T(8,128)(2,1)S(1)}, u32[]{:S(2)}, u32[]{:S(2)}) collective-permute-start(bf16[128,1024]{1,0:T(8,128)(2,1)S(1)} %pad_maximum_fusion.1.u0), channel_id=1, source_target_pairs={{0,16},{1,17},{2,18},{3,19},{4,20},{5,21},{6,22},{7,23},{8,24},{9,... | collective-permute-start | bytes 786440 | tf_op jit(solution)/shard_map/ppermute | solution.py:18
  45.5 5.7 %collective-permute-start.21 = (bf16[512,1024]{1,0:T(8,128)(2,1)S(1)}, bf16[512,1024]{1,0:T(8,128)(2,1)S(1)}, u32[]{:S(2)}, u32[]{:S(2)}) collective-permute-start(bf16[512,1024]{1,0:T(8,128)(2,1)S(1)} %convert_element_type.3.own), channel_id=1, source_target_pairs={{0,1},{1,0},{2,3},{3,2},{4,5},{5,4},{6,7},{7,6},{8,9},{9,8},{10,11... | collective-permute-start | bytes 3145736 | tf_op jit(solution)/shard_map/ppermute | solution.py:18
  46.1 8.3 %collective-permute-start.22 = (bf16[128,1024]{1,0:T(8,128)(2,1)S(1)}, bf16[128,1024]{1,0:T(8,128)(2,1)S(1)}, u32[]{:S(2)}, u32[]{:S(2)}) collective-permute-start(bf16[128,1024]{1,0:T(8,128)(2,1)S(1)} %collective-permute-done.17.u2), channel_id=1, source_target_pairs={{0,8},{1,9},{2,10},{3,11},{4,12},{5,13},{6,14},{7,15},{8,0},{9,1},... | collective-permute-start | bytes 786440 | tf_op jit(solution)/shard_map/ppermute | solution.py:18
  46.1 9.0 %collective-permute-start.19 = (bf16[256,512]{1,0:T(8,128)(2,1)S(1)}, bf16[256,512]{1,0:T(8,128)(2,1)S(1)}, u32[]{:S(2)}, u32[]{:S(2)}) collective-permute-start(bf16[256,512]{1,0:T(8,128)(2,1)S(1)} %slice.12), channel_id=1, source_target_pairs={{0,2},{1,3},{2,0},{3,1},{4,6},{5,7},{6,4},{7,5},{8,10},{9,11},{10,... | collective-permute-start | bytes 786440 | tf_op jit(solution)/shard_map/ppermute | solution.py:18
  47.9 8.1 %collective-permute-start.20 = (bf16[256,512]{1,0:T(8,128)(2,1)S(1)}, bf16[256,512]{1,0:T(8,128)(2,1)S(1)}, u32[]{:S(2)}, u32[]{:S(2)}) collective-permute-start(bf16[256,512]{1,0:T(8,128)(2,1)S(1)} %slice.13), channel_id=1, source_target_pairs={{0,4},{1,5},{2,6},{3,7},{4,0},{5,1},{6,2},{7,3},{8,12},{9,13},{10,... | collective-permute-start | bytes 786440 | tf_op jit(solution)/shard_map/ppermute | solution.py:18
  56.8 13.7 %collective-permute-start.23 = (f32[512,512]{1,0:T(8,128)S(1)}, f32[512,512]{1,0:T(8,128)S(1)}, u32[]{:S(2)}, u32[]{:S(2)}) collective-permute-start(f32[512,512]{1,0:T(8,128)S(1)} %get-tuple-element.48), channel_id=1, source_target_pairs={{0,1},{1,0},{2,3},{3,2},{4,5},{5,4},{6,7},{7,6},{8,9},{9,8},{10,11... | collective-permute-start | bytes 3145736 | tf_op jit(solution)/shard_map/ppermute | solution.py:18
  56.8 5.5 %collective-permute-start.26 = (f32[3,512]{1,0:T(4,128)S(1)}, f32[3,512]{1,0:T(4,128)S(1)}, u32[]{:S(2)}, u32[]{:S(2)}) collective-permute-start(f32[3,512]{1,0:T(4,128)S(1)} %get-tuple-element.49), channel_id=1, source_target_pairs={{0,24},{1,25},{2,26},{3,27},{4,28},{5,29},{6,30},{7,31},{8,16},{9,... | collective-permute-start | bytes 18440 | tf_op jit(solution)/shard_map/ppermute | solution.py:18
  58.4 4.6 %collective-permute-start.25 = (f32[3,512]{1,0:T(4,128)S(1)}, f32[3,512]{1,0:T(4,128)S(1)}, u32[]{:S(2)}, u32[]{:S(2)}) collective-permute-start(f32[3,512]{1,0:T(4,128)S(1)} %get-tuple-element.49), channel_id=1, source_target_pairs={{0,16},{1,17},{2,18},{3,19},{4,20},{5,21},{6,22},{7,23},{8,24},{9,... | collective-permute-start | bytes 18440 | tf_op jit(solution)/shard_map/ppermute | solution.py:18
  (12 other events, 178.6 us)

commit v8 on v7

--- a/solution.py
+++ b/solution.py
@@ -169,16 +169,29 @@
     add_up(keys, mine, theirs, pieces, finish)
 
 
-def code_kernel(own, other, here, there, codes):
+def code_kernel(own, other, here, there, codes, held, sems):
     _, core = chip_and_core()
-    width = own.shape[1]
-    for values, bounds, part in ((own, here, core), (other, there, 1 - core)):
+    count, width = own.shape
+    block = count // 4
+    ranges = []
+    for bounds in (here, there):
         upper = bounds[0:1, :]
         lower = -bounds[1:2, :]
-        mid = (upper + lower) * 0.5
-        scale = 7.5 / ((upper - lower) * 0.5 + 1e-05)
-        at = pl.ds(pl.multiple_of(part * width, width), width)
-        codes[:, at] = ((values[...] - mid) * scale).astype(BF16)
+        ranges.append(
+            ((upper + lower) * 0.5, 7.5 / ((upper - lower) * 0.5 + 1e-05))
+        )
+    copies = []
+    for step in range(4):
+        rows = pl.ds(step * block, block)
+        for values, (mid, scale), part in zip((own, other), ranges, (core, 1 - core)):
+            at = pl.ds(pl.multiple_of(part * width, width), width)
+            held[rows, at] = ((values[rows, :] - mid) * scale).astype(BF16)
+        copies.append(
+            pltpu.make_async_copy(held.at[rows, :], codes.at[rows, :], sems.at[step])
+        )
+        copies[-1].start()
+    for copy in copies:
+        copy.wait()
 
 
 def call(kernel, out, specs, flops, limit=24):
@@ -299,8 +312,16 @@
     bounds = merged[:2]
     if n_rep > 1:
         bounds = lax.pmax(bounds, "rep")
-    new_codes = call(
-        code_kernel, shape((count, 2 * width), BF16), [VMEM] * 4, 4 * count * width
+    new_codes = pl.pallas_call(
+        code_kernel,
+        out_shape=shape((count, 2 * width), BF16),
+        in_specs=[VMEM] * 4,
+        out_specs=pl.BlockSpec(memory_space=pl.ANY),
+        scratch_shapes=[
+            pltpu.VMEM((count, 2 * width), BF16),
+            pltpu.SemaphoreType.DMA((4,)),
+        ],
+        compiler_params=pltpu.CompilerParams(vmem_limit_bytes=24 * MIB),
     )(own, received, bounds, move(bounds, 1))
     each = users.shape[1]
     mine = lax.dynamic_slice_in_dim(merged[2:], chip * each, each, 1)

time: 71.8 us -> 71.7 us (level)
  no operation moved by 1% of the time
where the time goes in v8:
time: 71.7 us; the launch traced here: 71.5 us
  starting transfers between devices  31 us (43%)
  waiting for transfers between devices  26.4 us (37%)
  Pallas kernels  8.79 us (12%)
  local copies, waits for them, and re-layouts  2.39 us (3%)
  other arithmetic  2.03 us (3%)
  between operations  0.91 us (1%)
    ppermute x31, starting transfers between devices, swap(): return lax.ppermute(x, axis, [(i, i ^ k) for i in range(n)])  31 us
    ppermute x31, waiting for transfers between devices, swap(): return lax.ppermute(x, axis, [(i, i ^ k) for i in range(n)])  26.4 us
    pallas_call x1, Pallas kernels, by_permutes(): call(functools.partial(hidden_kernel, n), (shape((2 * count, wide), BF16)...  2.89 us
    pallas_call x1, Pallas kernels, by_permutes(): call(functools.partial(first_embed_kernel, keys[:3]), shape((2 * count, w...  1.83 us
    concatenate x4, other arithmetic, by_permutes(): cat = lambda *parts: jnp.concatenate(parts, axis=0)  1.75 us
    pallas_call x1, Pallas kernels, by_permutes(): call(near_score_kernel, shape((1, 3 * members), F32), [VMEM] * 7, 3 * sco...  1.47 us
  transfers between devices with their start and end apart: 31, of which 18 were waited for; matrix products, arithmetic and copies ran while one was open for 5% of the time, Pallas kernels for 10%

profile of v8, /device:TPU:0, one launch (start us, length us, event | category | flops | bytes accessed | tf_op | source)
XLA Modules:
  0.0 71.5 jit_solution(3535278270702465328)
XLA Ops:
  2.1 2.9 %collective-permute-start.12 = (bf16[32,1024]{1,0:T(8,128)(2,1)}, bf16[32,1024]{1,0:T(8,128)(2,1)S(1)}, u32[]{:S(2)}, u32[]{:S(2)}) collective-permute-start(bf16[32,1024]{1,0:T(8,128)(2,1)} %bitcast.10), channel_id=1, source_target_pairs={{0,2},{1,3},{2,0},{3,1},{4,6},{5,7},{6,4},{7,5},{8,10},{9,11},{10,... | collective-permute-start | bytes 196616 | tf_op jit(solution)/shard_map/ppermute | solution.py:18
  5.0 1.6 %collective-permute-start.1 = (bf16[32,1024]{1,0:T(8,128)(2,1)S(1)}, bf16[32,1024]{1,0:T(8,128)(2,1)S(1)}, u32[]{:S(2)}, u32[]{:S(2)}) collective-permute-start(bf16[32,1024]{1,0:T(8,128)(2,1)S(1)} %pad_maximum_fusion.3), channel_id=1, source_target_pairs={{0,8},{1,9},{2,10},{3,11},{4,12},{5,13},{6,14},{7,15},{8,0},{9,1},... | collective-permute-start | bytes 196616 | tf_op jit(solution)/shard_map/ppermute | solution.py:18
  6.7 2.6 %collective-permute-start.2 = (bf16[32,1024]{1,0:T(8,128)(2,1)S(1)}, bf16[32,1024]{1,0:T(8,128)(2,1)S(1)}, u32[]{:S(2)}, u32[]{:S(2)}) collective-permute-start(bf16[32,1024]{1,0:T(8,128)(2,1)S(1)} %pad_maximum_fusion.3), channel_id=1, source_target_pairs={{0,16},{1,17},{2,18},{3,19},{4,20},{5,21},{6,22},{7,23},{8,24},{9,... | collective-permute-start | bytes 196616 | tf_op jit(solution)/shard_map/ppermute | solution.py:18
  11.3 1.6 %collective-permute-start.13 = (bf16[64,1024]{1,0:T(8,128)(2,1)S(1)}, bf16[64,1024]{1,0:T(8,128)(2,1)S(1)}, u32[]{:S(2)}, u32[]{:S(2)}) collective-permute-start(bf16[64,1024]{1,0:T(8,128)(2,1)S(1)} %pad_maximum_fusion.2), channel_id=1, source_target_pairs={{0,4},{1,5},{2,6},{3,7},{4,0},{5,1},{6,2},{7,3},{8,12},{9,13},{10,... | collective-permute-start | bytes 393224 | tf_op jit(solution)/shard_map/ppermute | solution.py:18
  13.9 1.4 %collective-permute-done.3 = bf16[32,1024]{1,0:T(8,128)(2,1)S(1)} collective-permute-done((bf16[32,1024]{1,0:T(8,128)(2,1)S(1)}, bf16[32,1024]{1,0:T(8,128)(2,1)S(1)}, u32[]{:S(2)}, u32[]{:S(2)}) %collective-permute-start.3) | collective-permute-done | bytes 65568 | tf_op jit(solution)/shard_map/ppermute | solution.py:18
  15.4 1.6 %collective-permute-start.10 = (bf16[128,512]{1,0:T(8,128)(2,1)S(1)}, bf16[128,512]{1,0:T(8,128)(2,1)S(1)}, u32[]{:S(2)}, u32[]{:S(2)}) collective-permute-start(bf16[128,512]{1,0:T(8,128)(2,1)S(1)} %maximum_select_fusion), channel_id=1, source_target_pairs={{0,16},{1,17},{2,18},{3,19},{4,20},{5,21},{6,22},{7,23},{8,24},{9,... | collective-permute-start | bytes 393224 | tf_op jit(solution)/shard_map/ppermute | solution.py:18
  18.0 1.5 %collective-permute-start.7 = (bf16[128,1024]{1,0:T(8,128)(2,1)S(1)}, bf16[128,1024]{1,0:T(8,128)(2,1)S(1)}, u32[]{:S(2)}, u32[]{:S(2)}) collective-permute-start(bf16[128,1024]{1,0:T(8,128)(2,1)S(1)} %constant_dynamic-update-slice_fusion.w0), channel_id=1, source_target_pairs={{0,4},{1,5},{2,6},{3,7},{4,0},{5,1},{6,2},{7,3},{8,12},{9,13},{10,... | collective-permute-start | bytes 786440 | tf_op jit(solution)/shard_map/ppermute | solution.py:18
  21.3 1.6 %collective-permute-done.10 = bf16[128,512]{1,0:T(8,128)(2,1)S(1)} collective-permute-done((bf16[128,512]{1,0:T(8,128)(2,1)S(1)}, bf16[128,512]{1,0:T(8,128)(2,1)S(1)}, u32[]{:S(2)}, u32[]{:S(2)}) %collective-permute-start.10) | collective-permute-done | bytes 131104 | tf_op jit(solution)/shard_map/ppermute | solution.py:18
  23.8 2.8 %collective-permute-done.9 = bf16[128,512]{1,0:T(8,128)(2,1)S(1)} collective-permute-done((bf16[128,512]{1,0:T(8,128)(2,1)S(1)}, bf16[128,512]{1,0:T(8,128)(2,1)S(1)}, u32[]{:S(2)}, u32[]{:S(2)}) %collective-permute-start.9) | collective-permute-done | bytes 131104 | tf_op jit(solution)/shard_map/ppermute | solution.py:18
  26.5 1.8 %collective-permute-done.11 = bf16[128,512]{1,0:T(8,128)(2,1)S(1)} collective-permute-done((bf16[128,512]{1,0:T(8,128)(2,1)S(1)}, bf16[128,512]{1,0:T(8,128)(2,1)S(1)}, u32[]{:S(2)}, u32[]{:S(2)}) %collective-permute-start.11) | collective-permute-done | bytes 131104 | tf_op jit(solution)/shard_map/ppermute | solution.py:18
  31.2 1.2 %collective-permute-start.15 = (bf16[512,512]{1,0:T(8,128)(2,1)S(1)}, bf16[512,512]{1,0:T(8,128)(2,1)S(1)}, u32[]{:S(2)}, u32[]{:S(2)}) collective-permute-start(bf16[512,512]{1,0:T(8,128)(2,1)S(1)} %pad_maximum_fusion.refs_0_), channel_id=1, source_target_pairs={{0,4},{1,5},{2,6},{3,7},{4,0},{5,1},{6,2},{7,3},{8,12},{9,13},{10,... | collective-permute-start | bytes 1572872 | tf_op jit(solution)/shard_map/ppermute | solution.py:18
  33.3 1.5 %collective-permute-start.17 = (bf16[128,1024]{1,0:T(8,128)(2,1)S(1)}, bf16[128,1024]{1,0:T(8,128)(2,1)S(1)}, u32[]{:S(2)}, u32[]{:S(2)}) collective-permute-start(bf16[128,1024]{1,0:T(8,128)(2,1)S(1)} %pad_maximum_fusion.1.u0), channel_id=1, source_target_pairs={{0,16},{1,17},{2,18},{3,19},{4,20},{5,21},{6,22},{7,23},{8,24},{9,... | collective-permute-start | bytes 786440 | tf_op jit(solution)/shard_map/ppermute | solution.py:18
  34.9 2.9 %shard_map.95 = (bf16[1024,1024]{1,0:T(8,128)(2,1)S(1)}, f32[1,1024]{1,0:T(1,128)S(1)}, bf16[16,1024]{1,0:T(8,128)(2,1)S(1)}) custom-call(s32[1,1024]{1,0:T(1,128)S(1)} %bitcast.7, f32[4]{0:T(128)S(1)} %copy-done.2, f32[4]{0:T(128)S(1)} %copy-done.3, bf16[512,512]{1,0:T(8,128)(2,1)S(1)} %bitcast.6, bf16[512,512]{1,0:T(8,128)(2,1)S(1)} %collective-permute-done.5.other, ...), custom_call_target="tpu_custom_call" | custom-call | flops 1073741824 | bytes 2134016 | tf_op jit(solution)/shard_map/pallas_call | solution.py:260
  37.8 3.9 %collective-permute-done.16.u1 = bf16[128,1024]{1,0:T(8,128)(2,1)S(1)} collective-permute-done((bf16[128,1024]{1,0:T(8,128)(2,1)S(1)}, bf16[128,1024]{1,0:T(8,128)(2,1)S(1)}, u32[]{:S(2)}, u32[]{:S(2)}) %collective-permute-start.16) | collective-permute-done | bytes 262176 | tf_op jit(solution)/shard_map/ppermute | solution.py:18
  41.7 3.6 %collective-permute-done.17.u2 = bf16[128,1024]{1,0:T(8,128)(2,1)S(1)} collective-permute-done((bf16[128,1024]{1,0:T(8,128)(2,1)S(1)}, bf16[128,1024]{1,0:T(8,128)(2,1)S(1)}, u32[]{:S(2)}, u32[]{:S(2)}) %collective-permute-start.17) | collective-permute-done | bytes 262176 | tf_op jit(solution)/shard_map/ppermute | solution.py:18
  46.1 1.8 %collective-permute-start.19 = (bf16[256,512]{1,0:T(8,128)(2,1)S(1)}, bf16[256,512]{1,0:T(8,128)(2,1)S(1)}, u32[]{:S(2)}, u32[]{:S(2)}) collective-permute-start(bf16[256,512]{1,0:T(8,128)(2,1)S(1)} %slice.12), channel_id=1, source_target_pairs={{0,2},{1,3},{2,0},{3,1},{4,6},{5,7},{6,4},{7,5},{8,10},{9,11},{10,... | collective-permute-start | bytes 786440 | tf_op jit(solution)/shard_map/ppermute | solution.py:18
  49.4 1.8 %shard_map.96.refs_2_ = f32[1024,512]{1,0:T(8,128)S(1)} custom-call(bf16[1024,1024]{1,0:T(8,128)(2,1)S(1)} %get-tuple-element.37.mine, bf16[1024,1024]{1,0:T(8,128)(2,1)S(1)} %collective-permute-done.18.theirs, bf16[512,512]{1,0:T(8,128)(2,1)S(1)} %pad_maximum_fusion.refs_0_, bf16[512,512]{1,0:T(8,128)(2,1)S(1)} %collective-permute-done.14.refs_1_, ...), custom_call_target="tpu_custom_call" | custom-call | flops 1610612736 | bytes 2097152 | tf_op jit(solution)/shard_map/pallas_call | solution.py:278
  51.2 1.5 %shard_map.97.near = f32[1,384]{1,0:T(1,128)S(1)} custom-call(f32[1,1024]{1,0:T(1,128)S(1)} %get-tuple-element.41.step_d, bf16[16,1024]{1,0:T(8,128)(2,1)S(1)} %get-tuple-element.42.parts, bf16[512,1024]{1,0:T(8,128)(2,1)S(1)} %convert_element_type.3.own, bf16[512,1024]{1,0:T(8,128)(2,1)S(1)} %collective-permute-done.21.other, ...), custom_call_target="tpu_custom_call" | custom-call | flops 805306368 | bytes 1536 | tf_op jit(solution)/shard_map/pallas_call | solution.py:285
  52.7 1.6 %collective-permute-done.22.u0 = bf16[128,1024]{1,0:T(8,128)(2,1)S(1)} collective-permute-done((bf16[128,1024]{1,0:T(8,128)(2,1)S(1)}, bf16[128,1024]{1,0:T(8,128)(2,1)S(1)}, u32[]{:S(2)}, u32[]{:S(2)}) %collective-permute-start.22) | collective-permute-done | bytes 262176 | tf_op jit(solution)/shard_map/ppermute | solution.py:18
  56.8 1.6 %collective-permute-start.26 = (f32[3,512]{1,0:T(4,128)S(1)}, f32[3,512]{1,0:T(4,128)S(1)}, u32[]{:S(2)}, u32[]{:S(2)}) collective-permute-start(f32[3,512]{1,0:T(4,128)S(1)} %get-tuple-element.49), channel_id=1, source_target_pairs={{0,24},{1,25},{2,26},{3,27},{4,28},{5,29},{6,30},{7,31},{8,16},{9,... | collective-permute-start | bytes 18440 | tf_op jit(solution)/shard_map/ppermute | solution.py:18
  58.4 1.7 %collective-permute-start.25 = (f32[3,512]{1,0:T(4,128)S(1)}, f32[3,512]{1,0:T(4,128)S(1)}, u32[]{:S(2)}, u32[]{:S(2)}) collective-permute-start(f32[3,512]{1,0:T(4,128)S(1)} %get-tuple-element.49), channel_id=1, source_target_pairs={{0,16},{1,17},{2,18},{3,19},{4,20},{5,21},{6,22},{7,23},{8,24},{9,... | collective-permute-start | bytes 18440 | tf_op jit(solution)/shard_map/ppermute | solution.py:18
  60.1 1.2 %collective-permute-start.24 = (f32[3,512]{1,0:T(4,128)S(1)}, f32[3,512]{1,0:T(4,128)S(1)}, u32[]{:S(2)}, u32[]{:S(2)}) collective-permute-start(f32[3,512]{1,0:T(4,128)S(1)} %get-tuple-element.49), channel_id=1, source_target_pairs={{0,8},{1,9},{2,10},{3,11},{4,12},{5,13},{6,14},{7,15},{8,0},{9,1},... | collective-permute-start | bytes 18440 | tf_op jit(solution)/shard_map/ppermute | solution.py:18
  64.2 1.3 %collective-permute-start.28 = (f32[3,512]{1,0:T(4,128)S(1)}, f32[3,512]{1,0:T(4,128)S(1)}, u32[]{:S(2)}, u32[]{:S(2)}) collective-permute-start(f32[3,512]{1,0:T(4,128)S(1)} %maximum_maximum_fusion.1), channel_id=1, source_target_pairs={{0,4},{1,5},{2,6},{3,7},{4,0},{5,1},{6,2},{7,3},{8,12},{9,13},{10,... | collective-permute-start | bytes 18440 | tf_op jit(solution)/shard_map/ppermute | solution.py:18
  65.5 1.7 %collective-permute-start.27 = (f32[3,512]{1,0:T(4,128)S(1)}, f32[3,512]{1,0:T(4,128)S(1)}, u32[]{:S(2)}, u32[]{:S(2)}) collective-permute-start(f32[3,512]{1,0:T(4,128)S(1)} %maximum_maximum_fusion.1), channel_id=1, source_target_pairs={{0,2},{1,3},{2,0},{3,1},{4,6},{5,7},{6,4},{7,5},{8,10},{9,11},{10,... | collective-permute-start | bytes 18440 | tf_op jit(solution)/shard_map/ppermute | solution.py:18
  (73 shorter events, 23.7 us)
Async XLA Ops:
  2.0 13.4 %collective-permute-start.5 = (bf16[512,512]{1,0:T(8,128)(2,1)}, bf16[512,512]{1,0:T(8,128)(2,1)S(1)}, u32[]{:S(2)}, u32[]{:S(2)}) collective-permute-start(bf16[512,512]{1,0:T(8,128)(2,1)} %bitcast.5), channel_id=1, source_target_pairs={{0,1},{1,0},{2,3},{3,2},{4,5},{5,4},{6,7},{7,6},{8,9},{9,8},{10,11... | collective-permute-start | bytes 1572872 | tf_op jit(solution)/shard_map/ppermute | solution.py:18
  2.1 8.3 %collective-permute-start.12 = (bf16[32,1024]{1,0:T(8,128)(2,1)}, bf16[32,1024]{1,0:T(8,128)(2,1)S(1)}, u32[]{:S(2)}, u32[]{:S(2)}) collective-permute-start(bf16[32,1024]{1,0:T(8,128)(2,1)} %bitcast.10), channel_id=1, source_target_pairs={{0,2},{1,3},{2,0},{3,1},{4,6},{5,7},{6,4},{7,5},{8,10},{9,11},{10,... | collective-permute-start | bytes 196616 | tf_op jit(solution)/shard_map/ppermute | solution.py:18
  5.0 6.3 %collective-permute-start.1 = (bf16[32,1024]{1,0:T(8,128)(2,1)S(1)}, bf16[32,1024]{1,0:T(8,128)(2,1)S(1)}, u32[]{:S(2)}, u32[]{:S(2)}) collective-permute-start(bf16[32,1024]{1,0:T(8,128)(2,1)S(1)} %pad_maximum_fusion.3), channel_id=1, source_target_pairs={{0,8},{1,9},{2,10},{3,11},{4,12},{5,13},{6,14},{7,15},{8,0},{9,1},... | collective-permute-start | bytes 196616 | tf_op jit(solution)/shard_map/ppermute | solution.py:18
  6.7 7.2 %collective-permute-start.2 = (bf16[32,1024]{1,0:T(8,128)(2,1)S(1)}, bf16[32,1024]{1,0:T(8,128)(2,1)S(1)}, u32[]{:S(2)}, u32[]{:S(2)}) collective-permute-start(bf16[32,1024]{1,0:T(8,128)(2,1)S(1)} %pad_maximum_fusion.3), channel_id=1, source_target_pairs={{0,16},{1,17},{2,18},{3,19},{4,20},{5,21},{6,22},{7,23},{8,24},{9,... | collective-permute-start | bytes 196616 | tf_op jit(solution)/shard_map/ppermute | solution.py:18
  9.3 6.1 %collective-permute-start.3 = (bf16[32,1024]{1,0:T(8,128)(2,1)S(1)}, bf16[32,1024]{1,0:T(8,128)(2,1)S(1)}, u32[]{:S(2)}, u32[]{:S(2)}) collective-permute-start(bf16[32,1024]{1,0:T(8,128)(2,1)S(1)} %pad_maximum_fusion.3), channel_id=1, source_target_pairs={{0,24},{1,25},{2,26},{3,27},{4,28},{5,29},{6,30},{7,31},{8,16},{9,... | collective-permute-start | bytes 196616 | tf_op jit(solution)/shard_map/ppermute | solution.py:18
  10.4 4.9 %collective-permute-start.4 = (bf16[64,512]{1,0:T(8,128)(2,1)S(1)}, bf16[64,512]{1,0:T(8,128)(2,1)S(1)}, u32[]{:S(2)}, u32[]{:S(2)}) collective-permute-start(bf16[64,512]{1,0:T(8,128)(2,1)S(1)} %get-tuple-element.53), channel_id=1, source_target_pairs={{0,1},{1,0},{2,3},{3,2},{4,5},{5,4},{6,7},{7,6},{8,9},{9,8},{10,11... | collective-permute-start | bytes 196616 | tf_op jit(solution)/shard_map/ppermute | solution.py:18
  11.3 9.2 %collective-permute-start.13 = (bf16[64,1024]{1,0:T(8,128)(2,1)S(1)}, bf16[64,1024]{1,0:T(8,128)(2,1)S(1)}, u32[]{:S(2)}, u32[]{:S(2)}) collective-permute-start(bf16[64,1024]{1,0:T(8,128)(2,1)S(1)} %pad_maximum_fusion.2), channel_id=1, source_target_pairs={{0,4},{1,5},{2,6},{3,7},{4,0},{5,1},{6,2},{7,3},{8,12},{9,13},{10,... | collective-permute-start | bytes 393224 | tf_op jit(solution)/shard_map/ppermute | solution.py:18
  15.4 7.5 %collective-permute-start.10 = (bf16[128,512]{1,0:T(8,128)(2,1)S(1)}, bf16[128,512]{1,0:T(8,128)(2,1)S(1)}, u32[]{:S(2)}, u32[]{:S(2)}) collective-permute-start(bf16[128,512]{1,0:T(8,128)(2,1)S(1)} %maximum_select_fusion), channel_id=1, source_target_pairs={{0,16},{1,17},{2,18},{3,19},{4,20},{5,21},{6,22},{7,23},{8,24},{9,... | collective-permute-start | bytes 393224 | tf_op jit(solution)/shard_map/ppermute | solution.py:18
  17.0 11.4 %collective-permute-start.6 = (bf16[128,1024]{1,0:T(8,128)(2,1)S(1)}, bf16[128,1024]{1,0:T(8,128)(2,1)S(1)}, u32[]{:S(2)}, u32[]{:S(2)}) collective-permute-start(bf16[128,1024]{1,0:T(8,128)(2,1)S(1)} %constant_dynamic-update-slice_fusion.w0), channel_id=1, source_target_pairs={{0,2},{1,3},{2,0},{3,1},{4,6},{5,7},{6,4},{7,5},{8,10},{9,11},{10,... | collective-permute-start | bytes 786440 | tf_op jit(solution)/shard_map/ppermute | solution.py:18
  18.0 11.0 %collective-permute-start.7 = (bf16[128,1024]{1,0:T(8,128)(2,1)S(1)}, bf16[128,1024]{1,0:T(8,128)(2,1)S(1)}, u32[]{:S(2)}, u32[]{:S(2)}) collective-permute-start(bf16[128,1024]{1,0:T(8,128)(2,1)S(1)} %constant_dynamic-update-slice_fusion.w0), channel_id=1, source_target_pairs={{0,4},{1,5},{2,6},{3,7},{4,0},{5,1},{6,2},{7,3},{8,12},{9,13},{10,... | collective-permute-start | bytes 786440 | tf_op jit(solution)/shard_map/ppermute | solution.py:18
  19.5 10.6 %collective-permute-start.8 = (bf16[128,1024]{1,0:T(8,128)(2,1)S(1)}, bf16[128,1024]{1,0:T(8,128)(2,1)S(1)}, u32[]{:S(2)}, u32[]{:S(2)}) collective-permute-start(bf16[128,1024]{1,0:T(8,128)(2,1)S(1)} %constant_dynamic-update-slice_fusion.w0), channel_id=1, source_target_pairs={{0,6},{1,7},{2,4},{3,5},{4,2},{5,3},{6,0},{7,1},{8,14},{9,15},{10,... | collective-permute-start | bytes 786440 | tf_op jit(solution)/shard_map/ppermute | solution.py:18
  20.5 6.0 %collective-permute-start.9 = (bf16[128,512]{1,0:T(8,128)(2,1)S(1)}, bf16[128,512]{1,0:T(8,128)(2,1)S(1)}, u32[]{:S(2)}, u32[]{:S(2)}) collective-permute-start(bf16[128,512]{1,0:T(8,128)(2,1)S(1)} %maximum_select_fusion), channel_id=1, source_target_pairs={{0,8},{1,9},{2,10},{3,11},{4,12},{5,13},{6,14},{7,15},{8,0},{9,1},... | collective-permute-start | bytes 393224 | tf_op jit(solution)/shard_map/ppermute | solution.py:18
  22.9 5.5 %collective-permute-start.11 = (bf16[128,512]{1,0:T(8,128)(2,1)S(1)}, bf16[128,512]{1,0:T(8,128)(2,1)S(1)}, u32[]{:S(2)}, u32[]{:S(2)}) collective-permute-start(bf16[128,512]{1,0:T(8,128)(2,1)S(1)} %collective-permute-done.10), channel_id=1, source_target_pairs={{0,8},{1,9},{2,10},{3,11},{4,12},{5,13},{6,14},{7,15},{8,0},{9,1},... | collective-permute-start | bytes 393224 | tf_op jit(solution)/shard_map/ppermute | solution.py:18
  30.2 15.1 %collective-permute-start.14 = (bf16[512,512]{1,0:T(8,128)(2,1)S(1)}, bf16[512,512]{1,0:T(8,128)(2,1)S(1)}, u32[]{:S(2)}, u32[]{:S(2)}) collective-permute-start(bf16[512,512]{1,0:T(8,128)(2,1)S(1)} %pad_maximum_fusion.refs_0_), channel_id=1, source_target_pairs={{0,2},{1,3},{2,0},{3,1},{4,6},{5,7},{6,4},{7,5},{8,10},{9,11},{10,... | collective-permute-start | bytes 1572872 | tf_op jit(solution)/shard_map/ppermute | solution.py:18
  31.2 14.0 %collective-permute-start.15 = (bf16[512,512]{1,0:T(8,128)(2,1)S(1)}, bf16[512,512]{1,0:T(8,128)(2,1)S(1)}, u32[]{:S(2)}, u32[]{:S(2)}) collective-permute-start(bf16[512,512]{1,0:T(8,128)(2,1)S(1)} %pad_maximum_fusion.refs_0_), channel_id=1, source_target_pairs={{0,4},{1,5},{2,6},{3,7},{4,0},{5,1},{6,2},{7,3},{8,12},{9,13},{10,... | collective-permute-start | bytes 1572872 | tf_op jit(solution)/shard_map/ppermute | solution.py:18
  32.5 9.2 %collective-permute-start.16 = (bf16[128,1024]{1,0:T(8,128)(2,1)S(1)}, bf16[128,1024]{1,0:T(8,128)(2,1)S(1)}, u32[]{:S(2)}, u32[]{:S(2)}) collective-permute-start(bf16[128,1024]{1,0:T(8,128)(2,1)S(1)} %pad_maximum_fusion.1.u0), channel_id=1, source_target_pairs={{0,8},{1,9},{2,10},{3,11},{4,12},{5,13},{6,14},{7,15},{8,0},{9,1},... | collective-permute-start | bytes 786440 | tf_op jit(solution)/shard_map/ppermute | solution.py:18
  33.3 11.9 %collective-permute-start.17 = (bf16[128,1024]{1,0:T(8,128)(2,1)S(1)}, bf16[128,1024]{1,0:T(8,128)(2,1)S(1)}, u32[]{:S(2)}, u32[]{:S(2)}) collective-permute-start(bf16[128,1024]{1,0:T(8,128)(2,1)S(1)} %pad_maximum_fusion.1.u0), channel_id=1, source_target_pairs={{0,16},{1,17},{2,18},{3,19},{4,20},{5,21},{6,22},{7,23},{8,24},{9,... | collective-permute-start | bytes 786440 | tf_op jit(solution)/shard_map/ppermute | solution.py:18
  45.5 5.7 %collective-permute-start.21 = (bf16[512,1024]{1,0:T(8,128)(2,1)S(1)}, bf16[512,1024]{1,0:T(8,128)(2,1)S(1)}, u32[]{:S(2)}, u32[]{:S(2)}) collective-permute-start(bf16[512,1024]{1,0:T(8,128)(2,1)S(1)} %convert_element_type.3.own), channel_id=1, source_target_pairs={{0,1},{1,0},{2,3},{3,2},{4,5},{5,4},{6,7},{7,6},{8,9},{9,8},{10,11... | collective-permute-start | bytes 3145736 | tf_op jit(solution)/shard_map/ppermute | solution.py:18
  46.1 8.3 %collective-permute-start.22 = (bf16[128,1024]{1,0:T(8,128)(2,1)S(1)}, bf16[128,1024]{1,0:T(8,128)(2,1)S(1)}, u32[]{:S(2)}, u32[]{:S(2)}) collective-permute-start(bf16[128,1024]{1,0:T(8,128)(2,1)S(1)} %collective-permute-done.17.u2), channel_id=1, source_target_pairs={{0,8},{1,9},{2,10},{3,11},{4,12},{5,13},{6,14},{7,15},{8,0},{9,1},... | collective-permute-start | bytes 786440 | tf_op jit(solution)/shard_map/ppermute | solution.py:18
  46.1 9.0 %collective-permute-start.19 = (bf16[256,512]{1,0:T(8,128)(2,1)S(1)}, bf16[256,512]{1,0:T(8,128)(2,1)S(1)}, u32[]{:S(2)}, u32[]{:S(2)}) collective-permute-start(bf16[256,512]{1,0:T(8,128)(2,1)S(1)} %slice.12), channel_id=1, source_target_pairs={{0,2},{1,3},{2,0},{3,1},{4,6},{5,7},{6,4},{7,5},{8,10},{9,11},{10,... | collective-permute-start | bytes 786440 | tf_op jit(solution)/shard_map/ppermute | solution.py:18
  47.9 8.1 %collective-permute-start.20 = (bf16[256,512]{1,0:T(8,128)(2,1)S(1)}, bf16[256,512]{1,0:T(8,128)(2,1)S(1)}, u32[]{:S(2)}, u32[]{:S(2)}) collective-permute-start(bf16[256,512]{1,0:T(8,128)(2,1)S(1)} %slice.13), channel_id=1, source_target_pairs={{0,4},{1,5},{2,6},{3,7},{4,0},{5,1},{6,2},{7,3},{8,12},{9,13},{10,... | collective-permute-start | bytes 786440 | tf_op jit(solution)/shard_map/ppermute | solution.py:18
  56.8 13.7 %collective-permute-start.23 = (f32[512,512]{1,0:T(8,128)S(1)}, f32[512,512]{1,0:T(8,128)S(1)}, u32[]{:S(2)}, u32[]{:S(2)}) collective-permute-start(f32[512,512]{1,0:T(8,128)S(1)} %get-tuple-element.48), channel_id=1, source_target_pairs={{0,1},{1,0},{2,3},{3,2},{4,5},{5,4},{6,7},{7,6},{8,9},{9,8},{10,11... | collective-permute-start | bytes 3145736 | tf_op jit(solution)/shard_map/ppermute | solution.py:18
  56.8 5.5 %collective-permute-start.26 = (f32[3,512]{1,0:T(4,128)S(1)}, f32[3,512]{1,0:T(4,128)S(1)}, u32[]{:S(2)}, u32[]{:S(2)}) collective-permute-start(f32[3,512]{1,0:T(4,128)S(1)} %get-tuple-element.49), channel_id=1, source_target_pairs={{0,24},{1,25},{2,26},{3,27},{4,28},{5,29},{6,30},{7,31},{8,16},{9,... | collective-permute-start | bytes 18440 | tf_op jit(solution)/shard_map/ppermute | solution.py:18
  58.4 4.6 %collective-permute-start.25 = (f32[3,512]{1,0:T(4,128)S(1)}, f32[3,512]{1,0:T(4,128)S(1)}, u32[]{:S(2)}, u32[]{:S(2)}) collective-permute-start(f32[3,512]{1,0:T(4,128)S(1)} %get-tuple-element.49), channel_id=1, source_target_pairs={{0,16},{1,17},{2,18},{3,19},{4,20},{5,21},{6,22},{7,23},{8,24},{9,... | collective-permute-start | bytes 18440 | tf_op jit(solution)/shard_map/ppermute | solution.py:18
  (12 other events, 178.6 us)
